TPU v7x, 32 devices: a whole 2x2x4 slice. The times are simulated.
32 devices in a mesh: east: 8 (over z, core), north: 4 (over y, x).
Axes of the slice: x: 2, y: 2, z: 4, core: 2. Of those that a mesh axis runs over, the one named last changes fastest.
Arguments:
- increment: float32 [16, 512, 512], P(None, 'east', 'north'), may hold values from -6 to 6
- widths_fine: int32 [512, 512], P('east', 'north'), may hold values from 1 to 8
- widths_half: int32 [256, 256], P('east', 'north'), may hold values from 1 to 8
- widths_quarter: int32 [128, 128], P('east', 'north'), may hold values from 1 to 8
- widths_eighth: int32 [64, 64], P('east', 'north'), may hold values from 1 to 8
- amplitude_fine: float32 [512, 512], P('east', 'north'), may hold values from 0.5 to 2
- amplitude_half: float32 [256, 256], P('east', 'north'), may hold values from 0.5 to 2
- amplitude_quarter: float32 [128, 128], P('east', 'north'), may hold values from 0.5 to 2
- amplitude_eighth: float32 [64, 64], P('east', 'north'), may hold values from 0.5 to 2
- vertical: float32 [4, 16, 16], replicated, may hold values from -1.5 to 1.5
Outputs:
- filtered: float32 [16, 512, 512], P(None, 'east', 'north')
Inputs may be any that keep to these rules, and one draw needn't show every extreme that they name: `widths_fine`: half-widths in cells. `widths_half`: half-widths in cells. `widths_quarter`: half-widths in cells. `widths_eighth`: half-widths in cells.
All inputs are finite; a program needn't handle non-finite values.
Results may differ from a plain program's by a relative error of at most 0.00011.
Values sent between devices are 32-bit elements; how exact they have to be, the bound alone decides.
No kernel may reach another device: no remote copies, remote signals or barrier semaphores. Data moves between devices by JAX's collectives and lax.ppermute only.
A program may use at most 64 MiB of HBM per device.

v0:
```python
import jax
import jax.numpy as jnp
from jax import lax
from jax.sharding import PartitionSpec as P

HMAX = 8


def extended(block, sides, width):
    for axis, dim in sides:
        count = lax.axis_size(axis)
        forward = [(i, i + 1) for i in range(count - 1)]
        backward = [(target, source) for source, target in forward]
        low = lax.ppermute(
            lax.slice_in_dim(block, block.shape[dim] - width, None, axis=dim), axis, forward
        )
        high = lax.ppermute(lax.slice_in_dim(block, 0, width, axis=dim), axis, backward)
        block = jnp.concatenate([low, block, high], axis=dim)
    return block


def swapped(block, axis, bit):
    count = lax.axis_size(axis)
    route = []
    for low in range(count):
        high = low | 1 << bit
        if high != low and high < count:
            route += [(low, high), (high, low)]
    return lax.ppermute(block, axis, route)


def from_behind(shard, axis, by):
    length = lax.axis_size(axis)
    pairs = [(i, i + by) for i in range(length) if 0 <= i + by < length]
    return lax.ppermute(shard, axis, pairs)


def beta_taps(widths):
    grown = widths.astype(jnp.float32) + 1.0
    offsets = jnp.arange(-HMAX, HMAX + 1).astype(jnp.float32)
    ratios = offsets[:, None, None] / grown[None]
    profile = jnp.square(jnp.maximum(1.0 - ratios * ratios, 0.0))
    return profile / jnp.sum(profile, axis=0, keepdims=True)


def east_pass(padded, factors):
    row_count = factors.shape[1]
    running = factors[0][None] * padded[:, 0:row_count, :]
    for offset in range(1, factors.shape[0]):
        running = running + factors[offset][None] * padded[:, offset : offset + row_count, :]
    return running


def north_pass(padded, factors):
    col_count = factors.shape[2]
    running = factors[0][None] * padded[:, :, 0:col_count]
    for offset in range(1, factors.shape[0]):
        running = running + factors[offset][None] * padded[:, :, offset : offset + col_count]
    return running


def restrict(padded):
    row_count = padded.shape[1] - 2
    half_done = 0.375 * (
        padded[:, 1 : row_count + 1 : 2, :] + padded[:, 2 : row_count + 2 : 2, :]
    ) + 0.125 * (padded[:, 0:row_count:2, :] + padded[:, 3 : row_count + 2 : 2, :])
    col_count = padded.shape[2] - 2
    return 0.375 * (
        half_done[:, :, 1 : col_count + 1 : 2] + half_done[:, :, 2 : col_count + 2 : 2]
    ) + 0.125 * (half_done[:, :, 0:col_count:2] + half_done[:, :, 3 : col_count + 2 : 2])


def prolong(padded):
    layers = padded.shape[0]
    coarse_rows = padded.shape[1] - 2
    coarse_cols = padded.shape[2] - 2
    middle = padded[:, 1 : coarse_rows + 1, :]
    even_rows = 0.75 * middle + 0.25 * padded[:, 0:coarse_rows, :]
    odd_rows = 0.75 * middle + 0.25 * padded[:, 2 : coarse_rows + 2, :]
    stacked = jnp.stack([even_rows, odd_rows], axis=2).reshape(
        layers, 2 * coarse_rows, coarse_cols + 2
    )
    fine_index = lax.broadcasted_iota(jnp.int32, (2 * coarse_cols, coarse_cols + 2), 0)
    coarse_index = lax.broadcasted_iota(jnp.int32, (2 * coarse_cols, coarse_cols + 2), 1)
    centre_index = fine_index // 2 + 1
    side_index = fine_index // 2 + 2 * (fine_index % 2)
    weights_table = (
        jnp.where(coarse_index == centre_index, 0.75, 0.0)
        + jnp.where(coarse_index == side_index, 0.25, 0.0)
    ).astype(jnp.float32)
    return jnp.einsum("zxl,yl->zxy", stacked, weights_table, precision=lax.Precision.HIGHEST)


def filter_level(source, widths, amplitude, mixing, generation):
    extent = HMAX
    factors = beta_taps(widths)
    padded = extended(source, (("east", 1),), extent)
    eastward = east_pass(padded, factors)
    widened = extended(eastward, (("north", 2),), extent)
    northward = north_pass(widened, factors)
    mixed = jnp.einsum("ab,bxy->axy", mixing, northward, precision=lax.Precision.HIGHEST)
    return 4.0**generation * amplitude[None] * mixed


def group_level(source, widths, amplitude, mixing, generation):
    layers = source.shape[0]
    row_count = source.shape[1]
    col_count = source.shape[2]
    tap_count = 2 * HMAX + 1
    packed = jnp.concatenate([source, beta_taps(widths), amplitude[None]], axis=0)
    east_parity = lax.axis_index("east") % 2
    north_parity = lax.axis_index("north") % 2
    partner = swapped(packed, "east", 0)
    lower_half = jnp.where(east_parity == 0, packed, partner)
    upper_half = jnp.where(east_parity == 0, partner, packed)
    joined = jnp.concatenate([lower_half, upper_half], axis=1)
    partner_two = swapped(joined, "north", 0)
    south_half = jnp.where(north_parity == 0, joined, partner_two)
    north_half = jnp.where(north_parity == 0, partner_two, joined)
    block = jnp.concatenate([south_half, north_half], axis=2)
    group_source = block[:layers]
    factors = block[layers : layers + tap_count]
    gain_field = block[layers + tap_count]
    west_part = from_behind(group_source[:, -HMAX:, :], "east", 2)
    east_part = from_behind(group_source[:, :HMAX, :], "east", -2)
    eastward = east_pass(jnp.concatenate([west_part, group_source, east_part], axis=1), factors)
    south_part = from_behind(eastward[:, :, -HMAX:], "north", 2)
    north_part = from_behind(eastward[:, :, :HMAX], "north", -2)
    northward = north_pass(jnp.concatenate([south_part, eastward, north_part], axis=2), factors)
    mixed = jnp.einsum("ab,bxy->axy", mixing, northward, precision=lax.Precision.HIGHEST)
    weighted = 4.0**generation * gain_field[None] * mixed
    own_rows = lax.dynamic_slice_in_dim(weighted, east_parity * row_count, row_count, 1)
    return lax.dynamic_slice_in_dim(own_rows, north_parity * col_count, col_count, 2)


def any_level(source, widths, amplitude, mixing, generation):
    if generation >= 2:
        return group_level(source, widths, amplitude, mixing, generation)
    return filter_level(source, widths, amplitude, mixing, generation)


def body(
    increment,
    widths_fine,
    widths_half,
    widths_quarter,
    widths_eighth,
    amplitude_fine,
    amplitude_half,
    amplitude_quarter,
    amplitude_eighth,
    vertical,
):
    sources = [increment]
    for generation in range(3):
        padded = extended(sources[-1], (("east", 1), ("north", 2)), 1)
        sources.append(restrict(padded))
    width_list = [widths_fine, widths_half, widths_quarter, widths_eighth]
    gain_list = [amplitude_fine, amplitude_half, amplitude_quarter, amplitude_eighth]
    result = any_level(sources[3], width_list[3], gain_list[3], vertical[3], 3)
    for generation in (2, 1, 0):
        coarse = extended(result, (("east", 1), ("north", 2)), 1)
        result = any_level(
            sources[generation],
            width_list[generation],
            gain_list[generation],
            vertical[generation],
            generation,
        ) + prolong(coarse)
    return result


def solution(mesh):
    return jax.shard_map(
        body,
        mesh=mesh,
        in_specs=(
            P(None, "east", "north"),
            P("east", "north"),
            P("east", "north"),
            P("east", "north"),
            P("east", "north"),
            P("east", "north"),
            P("east", "north"),
            P("east", "north"),
            P("east", "north"),
            P(),
        ),
        out_specs=P(None, "east", "north"),
        check_vma=False,
    )
```

profile of v0, /device:TPU:0, one launch (start us, length us, event | category | flops | bytes accessed | tf_op | source)
XLA Modules:
  0.0 283.1 jit_solution(7360891979397178399)
XLA Ops:
  0.9 2.4 collective-permute-start.4
  6.2 5.8 %collective-permute-start = (f32[16,8,128]{2,1,0:T(8,128)}, f32[16,8,128]{2,1,0:T(8,128)}, u32[]{:S(2)}, u32[]{:S(2)}) collective-permute-start(f32[16,8,128]{2,1,0:T(8,128)} %get-tuple-element.76), channel_id=1, source_target_pairs={{0,4},{4,8},{8,12},{12,16},{16,20},{20,24},{24,28},{1,5},{5,9},{9,... | collective-permute-start | bytes 196616 | tf_op jit(solution)/shard_map/ppermute | solution.py:14
  22.2 3.4 %collective-permute-start.6 = (f32[16,66,1]{1,0,2:T(8,128)S(1)}, f32[16,66,1]{1,0,2:T(8,128)S(1)}, u32[]{:S(2)}, u32[]{:S(2)}) collective-permute-start(f32[16,66,1]{1,0,2:T(8,128)S(1)} %copy.59), channel_id=1, source_target_pairs={{0,1},{1,2},{2,3},{4,5},{5,6},{6,7},{8,9},{9,10},{10,11},{12,13},{... | collective-permute-start | bytes 12680 | tf_op jit(solution)/shard_map/ppermute | solution.py:14
  28.0 3.4 %collective-permute-done.7 = f32[16,66,1]{1,0,2:T(8,128)S(1)} collective-permute-done((f32[16,66,1]{1,0,2:T(8,128)S(1)}, f32[16,66,1]{1,0,2:T(8,128)S(1)}, u32[]{:S(2)}, u32[]{:S(2)}) %collective-permute-start.7) | collective-permute-done | bytes 4256 | tf_op jit(solution)/shard_map/ppermute | solution.py:17
  33.4 1.5 slice.1129
  36.1 6.1 %slice.1130 = f32[16,32,64]{2,1,0:T(8,128)S(1)} slice(f32[16,32,130]{2,1,0:T(8,128)S(1)} %multiply_add_fusion), slice={[0:16:1], [0:32:1], [1:129:2]} | slice | bytes 262144 | tf_op jit(solution)/shard_map/slice | solution.py:69
  42.3 6.1 %slice.1131 = f32[16,32,64]{2,1,0:T(8,128)S(1)} slice(f32[16,32,130]{2,1,0:T(8,128)S(1)} %multiply_add_fusion), slice={[0:16:1], [0:32:1], [2:130:2]} | slice | bytes 262144 | tf_op jit(solution)/shard_map/slice | solution.py:69
  48.5 6.1 %slice.1132 = f32[16,32,64]{2,1,0:T(8,128)S(1)} slice(f32[16,32,130]{2,1,0:T(8,128)S(1)} %multiply_add_fusion), slice={[0:16:1], [0:32:1], [0:128:2]} | slice | bytes 262144 | tf_op jit(solution)/shard_map/slice | solution.py:70
  54.5 6.1 %slice.1133 = f32[16,32,64]{2,1,0:T(8,128)S(1)} slice(f32[16,32,130]{2,1,0:T(8,128)S(1)} %multiply_add_fusion), slice={[0:16:1], [0:32:1], [3:130:2]} | slice | bytes 262144 | tf_op jit(solution)/shard_map/slice | solution.py:70
  60.8 2.2 collective-permute-start.12
  64.9 3.8 %collective-permute-done.13 = f32[16,1,64]{2,1,0:T(1,128)S(1)} collective-permute-done((f32[16,1,64]{2,1,0:T(1,128)S(1)}, f32[16,1,64]{2,1,0:T(1,128)S(1)}, u32[]{:S(2)}, u32[]{:S(2)}) %collective-permute-start.13) | collective-permute-done | bytes 4128 | tf_op jit(solution)/shard_map/ppermute | solution.py:17
  69.0 4.3 %collective-permute-start.14 = (f32[16,34,1]{2,1,0:T(8,128)S(1)}, f32[16,34,1]{2,1,0:T(8,128)S(1)}, u32[]{:S(2)}, u32[]{:S(2)}) collective-permute-start(f32[16,34,1]{2,1,0:T(8,128)S(1)} %get-tuple-element.78), channel_id=1, source_target_pairs={{0,1},{1,2},{2,3},{4,5},{5,6},{6,7},{8,9},{9,10},{10,11},{12,13},{... | collective-permute-start | bytes 6536 | tf_op jit(solution)/shard_map/ppermute | solution.py:14
  75.4 4.6 %collective-permute-done.14 = f32[16,34,1]{2,1,0:T(8,128)S(1)} collective-permute-done((f32[16,34,1]{2,1,0:T(8,128)S(1)}, f32[16,34,1]{2,1,0:T(8,128)S(1)}, u32[]{:S(2)}, u32[]{:S(2)}) %collective-permute-start.14) | collective-permute-done | bytes 2208 | tf_op jit(solution)/shard_map/ppermute | solution.py:14
  80.0 8.1 %collective-permute-done.15 = f32[16,34,1]{2,1,0:T(8,128)S(1)} collective-permute-done((f32[16,34,1]{2,1,0:T(8,128)S(1)}, f32[16,34,1]{2,1,0:T(8,128)S(1)}, u32[]{:S(2)}, u32[]{:S(2)}) %collective-permute-start.15) | collective-permute-done | bytes 2208 | tf_op jit(solution)/shard_map/ppermute | solution.py:17
  94.0 3.2 %collective-permute-start.22 = (f32[16,1,32]{2,1,0:T(1,128)S(1)}, f32[16,1,32]{2,1,0:T(1,128)S(1)}, u32[]{:S(2)}, u32[]{:S(2)}) collective-permute-start(f32[16,1,32]{2,1,0:T(1,128)S(1)} %get-tuple-element.123), channel_id=1, source_target_pairs={{0,4},{4,8},{8,12},{12,16},{16,20},{20,24},{24,28},{1,5},{5,9},{9,... | collective-permute-start | bytes 6152 | tf_op jit(solution)/shard_map/ppermute | solution.py:14
  98.6 3.0 %collective-permute-done.23 = f32[16,1,32]{2,1,0:T(1,128)S(1)} collective-permute-done((f32[16,1,32]{2,1,0:T(1,128)S(1)}, f32[16,1,32]{2,1,0:T(1,128)S(1)}, u32[]{:S(2)}, u32[]{:S(2)}) %collective-permute-start.23) | collective-permute-done | bytes 2080 | tf_op jit(solution)/shard_map/ppermute | solution.py:17
  101.8 1.6 collective-permute-start.24
  104.8 4.0 %collective-permute-start.8 = (f32[16,8,64]{2,1,0:T(8,128)S(1)}, f32[16,8,64]{2,1,0:T(8,128)S(1)}, u32[]{:S(2)}, u32[]{:S(2)}) collective-permute-start(f32[16,8,64]{2,1,0:T(8,128)S(1)} %get-tuple-element.109), channel_id=1, source_target_pairs={{0,4},{4,8},{8,12},{12,16},{16,20},{20,24},{24,28},{1,5},{5,9},{9,... | collective-permute-start | bytes 98312 | tf_op jit(solution)/shard_map/ppermute | solution.py:14
  110.1 2.4 collective-permute-done.25
  117.8 2.5 collective-permute-start.10
  121.9 4.3 %collective-permute-done.10 = f32[16,32,8]{2,1,0:T(8,128)S(1)} collective-permute-done((f32[16,32,8]{2,1,0:T(8,128)S(1)}, f32[16,32,8]{2,1,0:T(8,128)S(1)}, u32[]{:S(2)}, u32[]{:S(2)}) %collective-permute-start.10) | collective-permute-done | bytes 16416 | tf_op jit(solution)/shard_map/ppermute | solution.py:14
  126.3 2.5 collective-permute-start.27
  128.7 5.4 %collective-permute-done.11 = f32[16,32,8]{2,1,0:T(8,128)S(1)} collective-permute-done((f32[16,32,8]{2,1,0:T(8,128)S(1)}, f32[16,32,8]{2,1,0:T(8,128)S(1)}, u32[]{:S(2)}, u32[]{:S(2)}) %collective-permute-start.11) | collective-permute-done | bytes 16416 | tf_op jit(solution)/shard_map/ppermute | solution.py:17
  134.2 2.2 fusion.206
  139.8 3.7 %collective-permute-start.28 = (f32[16,8,32]{2,1,0:T(8,128)S(1)}, f32[16,8,32]{2,1,0:T(8,128)S(1)}, u32[]{:S(2)}, u32[]{:S(2)}) collective-permute-start(f32[16,8,32]{2,1,0:T(8,128)S(1)} %get-tuple-element.49), channel_id=1, source_target_pairs={{0,8},{4,12},{8,16},{12,20},{16,24},{20,28},{1,9},{5,13},{9,17},{1... | collective-permute-start | bytes 49160 | tf_op jit(solution)/shard_map/ppermute | solution.py:35
  145.3 4.3 %collective-permute-done.29 = f32[16,8,32]{2,1,0:T(8,128)S(1)} collective-permute-done((f32[16,8,32]{2,1,0:T(8,128)S(1)}, f32[16,8,32]{2,1,0:T(8,128)S(1)}, u32[]{:S(2)}, u32[]{:S(2)}) %collective-permute-start.29) | collective-permute-done | bytes 16416 | tf_op jit(solution)/shard_map/ppermute | solution.py:35
  153.9 4.4 %collective-permute-done.31 = f32[16,16,8]{2,1,0:T(8,128)S(1)} collective-permute-done((f32[16,16,8]{2,1,0:T(8,128)S(1)}, f32[16,16,8]{2,1,0:T(8,128)S(1)}, u32[]{:S(2)}, u32[]{:S(2)}) %collective-permute-start.31) | collective-permute-done | bytes 8224 | tf_op jit(solution)/shard_map/ppermute | solution.py:35
  163.5 3.8 %collective-permute-done.33 = f32[16,1,16]{0,2,1:T(8,128)S(1)} collective-permute-done((f32[16,1,16]{0,2,1:T(8,128)S(1)}, f32[16,1,16]{0,2,1:T(8,128)S(1)}, u32[]{:S(2)}, u32[]{:S(2)}) %collective-permute-start.33) | collective-permute-done | bytes 1056 | tf_op jit(solution)/shard_map/ppermute | solution.py:17
  167.3 3.4 %collective-permute-start.34 = (f32[16,10,1]{0,2,1:T(1,128)S(1)}, f32[16,10,1]{0,2,1:T(1,128)S(1)}, u32[]{:S(2)}, u32[]{:S(2)}) collective-permute-start(f32[16,10,1]{0,2,1:T(1,128)S(1)} %get-tuple-element.127), channel_id=1, source_target_pairs={{0,1},{1,2},{2,3},{4,5},{5,6},{6,7},{8,9},{9,10},{10,11},{12,13},{... | collective-permute-start | bytes 1928 | tf_op jit(solution)/shard_map/ppermute | solution.py:14
  173.4 2.6 collective-permute-start.17
  176.2 11.8 %collective-permute-done.17 = f32[34,32,32]{0,2,1:T(8,128)} collective-permute-done((f32[34,32,32]{0,2,1:T(8,128)}, f32[34,32,32]{0,2,1:T(8,128)}, u32[]{:S(2)}, u32[]{:S(2)}) %collective-permute-start.17) | collective-permute-done | bytes 139296 | tf_op jit(solution)/shard_map/ppermute | solution.py:29
  188.0 1.6 copy.65
  190.9 5.0 %collective-permute-start.18 = (f32[16,8,64]{2,1,0:T(8,128)S(1)}, f32[16,8,64]{2,1,0:T(8,128)S(1)}, u32[]{:S(2)}, u32[]{:S(2)}) collective-permute-start(f32[16,8,64]{2,1,0:T(8,128)S(1)} %get-tuple-element.23), channel_id=1, source_target_pairs={{0,8},{4,12},{8,16},{12,20},{16,24},{20,28},{1,9},{5,13},{9,17},{1... | collective-permute-start | bytes 98312 | tf_op jit(solution)/shard_map/ppermute | solution.py:35
  197.8 4.3 %collective-permute-done.19 = f32[16,8,64]{2,1,0:T(8,128)S(1)} collective-permute-done((f32[16,8,64]{2,1,0:T(8,128)S(1)}, f32[16,8,64]{2,1,0:T(8,128)S(1)}, u32[]{:S(2)}, u32[]{:S(2)}) %collective-permute-start.19) | collective-permute-done | bytes 32800 | tf_op jit(solution)/shard_map/ppermute | solution.py:35
  203.6 3.4 %collective-permute-start.20 = (f32[16,32,8]{2,1,0:T(8,128)}, f32[16,32,8]{2,1,0:T(8,128)S(1)}, u32[]{:S(2)}, u32[]{:S(2)}) collective-permute-start(f32[16,32,8]{2,1,0:T(8,128)} %get-tuple-element.103), channel_id=1, source_target_pairs={{0,2},{1,3},{4,6},{5,7},{8,10},{9,11},{12,14},{13,15},{16,18},{17,... | collective-permute-start | bytes 49160 | tf_op jit(solution)/shard_map/ppermute | solution.py:35
  209.6 2.2 collective-permute-done.20
  211.8 4.1 %collective-permute-done.21 = f32[16,32,8]{2,1,0:T(8,128)} collective-permute-done((f32[16,32,8]{2,1,0:T(8,128)}, f32[16,32,8]{2,1,0:T(8,128)}, u32[]{:S(2)}, u32[]{:S(2)}) %collective-permute-start.21) | collective-permute-done | bytes 16416 | tf_op jit(solution)/shard_map/ppermute | solution.py:35
  215.9 4.3 %fusion.166 = f32[16,32,64]{2,1,0:T(8,128)S(1)} fusion(f32[16,32,8]{2,1,0:T(8,128)} %collective-permute-done.21, f32[16,32,64]{2,1,0:T(8,128)S(1)} %fusion.76, f32[16,32,8]{2,1,0:T(8,128)S(1)} %collective-permute-done.20, f32[32,64]{1,0:T(8,128)S(1)} %get-tuple-element.19, f32[32,64]{1,0:T(8,128)} %copy-done.17, f32[32,64]{1,0:T(8,128)S(1)} %get-tuple-element.21, ...), kind=kLoop, calls=%fused_computation.319 | loop fusion | flops 1605632 | bytes 434176 | tf_op jit(solution)/shard_map/add | solution.py:58
  226.8 2.3 collective-permute-start.38
  230.7 4.6 %collective-permute-start.2 = (f32[16,64,8]{2,1,0:T(8,128)S(1)}, f32[16,64,8]{2,1,0:T(8,128)S(1)}, u32[]{:S(2)}, u32[]{:S(2)}) collective-permute-start(f32[16,64,8]{2,1,0:T(8,128)S(1)} %get-tuple-element.72), channel_id=1, source_target_pairs={{0,1},{1,2},{2,3},{4,5},{5,6},{6,7},{8,9},{9,10},{10,11},{12,13},{... | collective-permute-start | bytes 98312 | tf_op jit(solution)/shard_map/ppermute | solution.py:14
  237.3 3.5 %collective-permute-start.40 = (f32[16,1,64]{2,0,1:T(8,128)S(1)}, f32[16,1,64]{2,0,1:T(8,128)S(1)}, u32[]{:S(2)}, u32[]{:S(2)}) collective-permute-start(f32[16,1,64]{2,0,1:T(8,128)S(1)} %get-tuple-element.101), channel_id=1, source_target_pairs={{0,4},{4,8},{8,12},{12,16},{16,20},{20,24},{24,28},{1,5},{5,9},{9,... | collective-permute-start | bytes 12296 | tf_op jit(solution)/shard_map/ppermute | solution.py:14
  242.1 4.6 %collective-permute-done.2 = f32[16,64,8]{2,1,0:T(8,128)S(1)} collective-permute-done((f32[16,64,8]{2,1,0:T(8,128)S(1)}, f32[16,64,8]{2,1,0:T(8,128)S(1)}, u32[]{:S(2)}, u32[]{:S(2)}) %collective-permute-start.2) | collective-permute-done | bytes 32800 | tf_op jit(solution)/shard_map/ppermute | solution.py:14
  246.7 13.2 %collective-permute-done.3 = f32[16,64,8]{2,1,0:T(8,128)S(1)} collective-permute-done((f32[16,64,8]{2,1,0:T(8,128)S(1)}, f32[16,64,8]{2,1,0:T(8,128)S(1)}, u32[]{:S(2)}, u32[]{:S(2)}) %collective-permute-start.3) | collective-permute-done | bytes 32800 | tf_op jit(solution)/shard_map/ppermute | solution.py:17
  259.8 4.3 %fusion.8 = f32[16,64,128]{2,1,0:T(8,128)S(1)} fusion(f32[16,64,128]{2,1,0:T(8,128)S(1)} %fusion.51, f32[16,64,8]{2,1,0:T(8,128)S(1)} %collective-permute-done.3, f32[16,64,8]{2,1,0:T(8,128)S(1)} %collective-permute-done.2, f32[64,128]{1,0:T(8,128)S(1)} %copy-done.1, f32[64,128]{1,0:T(8,128)S(1)} %copy-done.2, f32[64,128]{1,0:T(8,128)S(1)} %copy-done.3, ...), kind=kLoop, calls=%fused_computation.73 | loop fusion | flops 6422528 | bytes 1671168 | tf_op jit(solution)/shard_map/add | solution.py:58
  264.4 2.8 collective-permute-start.42
  268.5 1.6 fusion
  270.1 3.9 %collective-permute-done.42 = f32[16,34,1]{2,0,1:T(8,128)S(1)} collective-permute-done((f32[16,34,1]{2,0,1:T(8,128)S(1)}, f32[16,34,1]{2,0,1:T(8,128)S(1)}, u32[]{:S(2)}, u32[]{:S(2)}) %collective-permute-start.42) | collective-permute-done | bytes 2208 | tf_op jit(solution)/shard_map/ppermute | solution.py:14
  274.0 6.5 %collective-permute-done.43 = f32[16,34,1]{2,0,1:T(8,128)S(1)} collective-permute-done((f32[16,34,1]{2,0,1:T(8,128)S(1)}, f32[16,34,1]{2,0,1:T(8,128)S(1)}, u32[]{:S(2)}, u32[]{:S(2)}) %collective-permute-start.43) | collective-permute-done | bytes 2208 | tf_op jit(solution)/shard_map/ppermute | solution.py:17
  (319 shorter events, 79.6 us)
Async XLA Ops:
  0.0 18.2 %copy-start.47 = (s32[32,64]{1,0:T(8,128)S(1)}, s32[32,64]{1,0:T(8,128)}, u32[]{:S(2)}) copy-start(s32[32,64]{1,0:T(8,128)} %param.12) | copy-start | bytes 24580
  0.0 19.2 %copy-start.48 = (f32[32,64]{1,0:T(8,128)S(1)}, f32[32,64]{1,0:T(8,128)}, u32[]{:S(2)}) copy-start(f32[32,64]{1,0:T(8,128)} %param.16) | copy-start | bytes 24580
  0.0 19.8 %copy-start.46 = (s32[64,128]{1,0:T(8,128)S(1)}, s32[64,128]{1,0:T(8,128)}, u32[]{:S(2)}) copy-start(s32[64,128]{1,0:T(8,128)} %param.11) | copy-start | bytes 98308
  0.9 20.7 %collective-permute-start.4 = (f32[16,1,128]{2,1,0:T(1,128)S(1)}, f32[16,1,128]{2,1,0:T(1,128)S(1)}, u32[]{:S(2)}, u32[]{:S(2)}) collective-permute-start(f32[16,1,128]{2,1,0:T(1,128)S(1)} %get-tuple-element.70), channel_id=1, source_target_pairs={{0,4},{4,8},{8,12},{12,16},{16,20},{20,24},{24,28},{1,5},{5,9},{9,... | collective-permute-start | bytes 24584 | tf_op jit(solution)/shard_map/ppermute | solution.py:14
  3.3 18.3 %collective-permute-start.5 = (f32[16,1,128]{2,1,0:T(1,128)S(1)}, f32[16,1,128]{2,1,0:T(1,128)S(1)}, u32[]{:S(2)}, u32[]{:S(2)}) collective-permute-start(f32[16,1,128]{2,1,0:T(1,128)S(1)} %get-tuple-element.71), channel_id=1, source_target_pairs={{4,0},{8,4},{12,8},{16,12},{20,16},{24,20},{28,24},{5,1},{9,5},{13... | collective-permute-start | bytes 24584 | tf_op jit(solution)/shard_map/ppermute | solution.py:17
  6.2 131.4 %collective-permute-start = (f32[16,8,128]{2,1,0:T(8,128)}, f32[16,8,128]{2,1,0:T(8,128)}, u32[]{:S(2)}, u32[]{:S(2)}) collective-permute-start(f32[16,8,128]{2,1,0:T(8,128)} %get-tuple-element.76), channel_id=1, source_target_pairs={{0,4},{4,8},{8,12},{12,16},{16,20},{20,24},{24,28},{1,5},{5,9},{9,... | collective-permute-start | bytes 196616 | tf_op jit(solution)/shard_map/ppermute | solution.py:14
  12.0 140.7 %collective-permute-start.1 = (f32[16,8,128]{2,1,0:T(8,128)}, f32[16,8,128]{2,1,0:T(8,128)}, u32[]{:S(2)}, u32[]{:S(2)}) collective-permute-start(f32[16,8,128]{2,1,0:T(8,128)} %get-tuple-element.77), channel_id=1, source_target_pairs={{4,0},{8,4},{12,8},{16,12},{20,16},{24,20},{28,24},{5,1},{9,5},{13... | collective-permute-start | bytes 196616 | tf_op jit(solution)/shard_map/ppermute | solution.py:17
  22.2 5.5 %collective-permute-start.6 = (f32[16,66,1]{1,0,2:T(8,128)S(1)}, f32[16,66,1]{1,0,2:T(8,128)S(1)}, u32[]{:S(2)}, u32[]{:S(2)}) collective-permute-start(f32[16,66,1]{1,0,2:T(8,128)S(1)} %copy.59), channel_id=1, source_target_pairs={{0,1},{1,2},{2,3},{4,5},{5,6},{6,7},{8,9},{9,10},{10,11},{12,13},{... | collective-permute-start | bytes 12680 | tf_op jit(solution)/shard_map/ppermute | solution.py:14
  25.8 5.6 %collective-permute-start.7 = (f32[16,66,1]{1,0,2:T(8,128)S(1)}, f32[16,66,1]{1,0,2:T(8,128)S(1)}, u32[]{:S(2)}, u32[]{:S(2)}) collective-permute-start(f32[16,66,1]{1,0,2:T(8,128)S(1)} %copy.60), channel_id=1, source_target_pairs={{1,0},{2,1},{3,2},{5,4},{6,5},{7,6},{9,8},{10,9},{11,10},{13,12},{... | collective-permute-start | bytes 12680 | tf_op jit(solution)/shard_map/ppermute | solution.py:17
  60.8 4.1 %collective-permute-start.12 = (f32[16,1,64]{2,1,0:T(1,128)S(1)}, f32[16,1,64]{2,1,0:T(1,128)S(1)}, u32[]{:S(2)}, u32[]{:S(2)}) collective-permute-start(f32[16,1,64]{2,1,0:T(1,128)S(1)} %get-tuple-element.105), channel_id=1, source_target_pairs={{0,4},{4,8},{8,12},{12,16},{16,20},{20,24},{24,28},{1,5},{5,9},{9,... | collective-permute-start | bytes 12296 | tf_op jit(solution)/shard_map/ppermute | solution.py:14
  63.1 5.7 %collective-permute-start.13 = (f32[16,1,64]{2,1,0:T(1,128)S(1)}, f32[16,1,64]{2,1,0:T(1,128)S(1)}, u32[]{:S(2)}, u32[]{:S(2)}) collective-permute-start(f32[16,1,64]{2,1,0:T(1,128)S(1)} %get-tuple-element.106), channel_id=1, source_target_pairs={{4,0},{8,4},{12,8},{16,12},{20,16},{24,20},{28,24},{5,1},{9,5},{13... | collective-permute-start | bytes 12296 | tf_op jit(solution)/shard_map/ppermute | solution.py:17
  69.0 11.0 %collective-permute-start.14 = (f32[16,34,1]{2,1,0:T(8,128)S(1)}, f32[16,34,1]{2,1,0:T(8,128)S(1)}, u32[]{:S(2)}, u32[]{:S(2)}) collective-permute-start(f32[16,34,1]{2,1,0:T(8,128)S(1)} %get-tuple-element.78), channel_id=1, source_target_pairs={{0,1},{1,2},{2,3},{4,5},{5,6},{6,7},{8,9},{9,10},{10,11},{12,13},{... | collective-permute-start | bytes 6536 | tf_op jit(solution)/shard_map/ppermute | solution.py:14
  73.3 14.7 %collective-permute-start.15 = (f32[16,34,1]{2,1,0:T(8,128)S(1)}, f32[16,34,1]{2,1,0:T(8,128)S(1)}, u32[]{:S(2)}, u32[]{:S(2)}) collective-permute-start(f32[16,34,1]{2,1,0:T(8,128)S(1)} %get-tuple-element.79), channel_id=1, source_target_pairs={{1,0},{2,1},{3,2},{5,4},{6,5},{7,6},{9,8},{10,9},{11,10},{13,12},{... | collective-permute-start | bytes 6536 | tf_op jit(solution)/shard_map/ppermute | solution.py:17
  94.0 4.7 %collective-permute-start.22 = (f32[16,1,32]{2,1,0:T(1,128)S(1)}, f32[16,1,32]{2,1,0:T(1,128)S(1)}, u32[]{:S(2)}, u32[]{:S(2)}) collective-permute-start(f32[16,1,32]{2,1,0:T(1,128)S(1)} %get-tuple-element.123), channel_id=1, source_target_pairs={{0,4},{4,8},{8,12},{12,16},{16,20},{20,24},{24,28},{1,5},{5,9},{9,... | collective-permute-start | bytes 6152 | tf_op jit(solution)/shard_map/ppermute | solution.py:14
  97.1 4.5 %collective-permute-start.23 = (f32[16,1,32]{2,1,0:T(1,128)S(1)}, f32[16,1,32]{2,1,0:T(1,128)S(1)}, u32[]{:S(2)}, u32[]{:S(2)}) collective-permute-start(f32[16,1,32]{2,1,0:T(1,128)S(1)} %get-tuple-element.124), channel_id=1, source_target_pairs={{4,0},{8,4},{12,8},{16,12},{20,16},{24,20},{28,24},{5,1},{9,5},{13... | collective-permute-start | bytes 6152 | tf_op jit(solution)/shard_map/ppermute | solution.py:17
  101.8 7.0 %collective-permute-start.24 = (f32[16,18,1]{2,1,0:T(8,128)S(1)}, f32[16,18,1]{2,1,0:T(8,128)S(1)}, u32[]{:S(2)}, u32[]{:S(2)}) collective-permute-start(f32[16,18,1]{2,1,0:T(8,128)S(1)} %get-tuple-element.111), channel_id=1, source_target_pairs={{0,1},{1,2},{2,3},{4,5},{5,6},{6,7},{8,9},{9,10},{10,11},{12,13},{... | collective-permute-start | bytes 3464 | tf_op jit(solution)/shard_map/ppermute | solution.py:14
  103.5 9.1 %collective-permute-start.25 = (f32[16,18,1]{2,1,0:T(8,128)S(1)}, f32[16,18,1]{2,1,0:T(8,128)S(1)}, u32[]{:S(2)}, u32[]{:S(2)}) collective-permute-start(f32[16,18,1]{2,1,0:T(8,128)S(1)} %get-tuple-element.112), channel_id=1, source_target_pairs={{1,0},{2,1},{3,2},{5,4},{6,5},{7,6},{9,8},{10,9},{11,10},{13,12},{... | collective-permute-start | bytes 3464 | tf_op jit(solution)/shard_map/ppermute | solution.py:17
  104.8 12.0 %collective-permute-start.8 = (f32[16,8,64]{2,1,0:T(8,128)S(1)}, f32[16,8,64]{2,1,0:T(8,128)S(1)}, u32[]{:S(2)}, u32[]{:S(2)}) collective-permute-start(f32[16,8,64]{2,1,0:T(8,128)S(1)} %get-tuple-element.109), channel_id=1, source_target_pairs={{0,4},{4,8},{8,12},{12,16},{16,20},{20,24},{24,28},{1,5},{5,9},{9,... | collective-permute-start | bytes 98312 | tf_op jit(solution)/shard_map/ppermute | solution.py:14
  108.8 8.0 %collective-permute-start.9 = (f32[16,8,64]{2,1,0:T(8,128)S(1)}, f32[16,8,64]{2,1,0:T(8,128)S(1)}, u32[]{:S(2)}, u32[]{:S(2)}) collective-permute-start(f32[16,8,64]{2,1,0:T(8,128)S(1)} %get-tuple-element.110), channel_id=1, source_target_pairs={{4,0},{8,4},{12,8},{16,12},{20,16},{24,20},{28,24},{5,1},{9,5},{13... | collective-permute-start | bytes 98312 | tf_op jit(solution)/shard_map/ppermute | solution.py:17
  114.6 1.7 collective-permute-start.26
  116.3 47.1 %collective-permute-start.16 = (f32[34,16,32]{2,1,0:T(8,128)S(1)}, f32[34,16,32]{2,1,0:T(8,128)S(1)}, u32[]{:S(2)}, u32[]{:S(2)}) collective-permute-start(f32[34,16,32]{2,1,0:T(8,128)S(1)} %pad_maximum_fusion.8), channel_id=1, source_target_pairs={{0,4},{4,0},{8,12},{12,8},{16,20},{20,16},{24,28},{28,24},{1,5},{5... | collective-permute-start | bytes 208904 | tf_op jit(solution)/shard_map/ppermute | solution.py:29
  116.9 17.2 %copy-start.23 = (f32[32,64]{1,0:T(8,128)S(1)}, f32[32,64]{1,0:T(8,128)}, u32[]{:S(2)}) copy-start(f32[32,64]{1,0:T(8,128)} %get-tuple-element.90) | copy-start | bytes 24580
  117.8 8.4 %collective-permute-start.10 = (f32[16,32,8]{2,1,0:T(8,128)S(1)}, f32[16,32,8]{2,1,0:T(8,128)S(1)}, u32[]{:S(2)}, u32[]{:S(2)}) collective-permute-start(f32[16,32,8]{2,1,0:T(8,128)S(1)} %get-tuple-element.107), channel_id=1, source_target_pairs={{0,1},{1,2},{2,3},{4,5},{5,6},{6,7},{8,9},{9,10},{10,11},{12,13},{... | collective-permute-start | bytes 49160 | tf_op jit(solution)/shard_map/ppermute | solution.py:14
  120.4 13.7 %collective-permute-start.11 = (f32[16,32,8]{2,1,0:T(8,128)S(1)}, f32[16,32,8]{2,1,0:T(8,128)S(1)}, u32[]{:S(2)}, u32[]{:S(2)}) collective-permute-start(f32[16,32,8]{2,1,0:T(8,128)S(1)} %get-tuple-element.108), channel_id=1, source_target_pairs={{1,0},{2,1},{3,2},{5,4},{6,5},{7,6},{9,8},{10,9},{11,10},{13,12},{... | collective-permute-start | bytes 49160 | tf_op jit(solution)/shard_map/ppermute | solution.py:17
  126.3 13.0 %collective-permute-start.27 = (f32[34,16,16]{2,1,0:T(8,128)S(1)}, f32[34,16,16]{2,1,0:T(8,128)S(1)}, u32[]{:S(2)}, u32[]{:S(2)}) collective-permute-start(f32[34,16,16]{2,1,0:T(8,128)S(1)} %copy.71), channel_id=1, source_target_pairs={{0,1},{1,0},{2,3},{3,2},{4,5},{5,4},{6,7},{7,6},{8,9},{9,8},{10,11... | collective-permute-start | bytes 104456 | tf_op jit(solution)/shard_map/ppermute | solution.py:29
  139.8 5.6 %collective-permute-start.28 = (f32[16,8,32]{2,1,0:T(8,128)S(1)}, f32[16,8,32]{2,1,0:T(8,128)S(1)}, u32[]{:S(2)}, u32[]{:S(2)}) collective-permute-start(f32[16,8,32]{2,1,0:T(8,128)S(1)} %get-tuple-element.49), channel_id=1, source_target_pairs={{0,8},{4,12},{8,16},{12,20},{16,24},{20,28},{1,9},{5,13},{9,17},{1... | collective-permute-start | bytes 49160 | tf_op jit(solution)/shard_map/ppermute | solution.py:35
  143.5 6.2 %collective-permute-start.29 = (f32[16,8,32]{2,1,0:T(8,128)S(1)}, f32[16,8,32]{2,1,0:T(8,128)S(1)}, u32[]{:S(2)}, u32[]{:S(2)}) collective-permute-start(f32[16,8,32]{2,1,0:T(8,128)S(1)} %get-tuple-element.50), channel_id=1, source_target_pairs={{8,0},{12,4},{16,8},{20,12},{24,16},{28,20},{9,1},{13,5},{17,9},{2... | collective-permute-start | bytes 49160 | tf_op jit(solution)/shard_map/ppermute | solution.py:35
  150.1 3.8 %collective-permute-start.30 = (f32[16,16,8]{2,1,0:T(8,128)S(1)}, f32[16,16,8]{2,1,0:T(8,128)S(1)}, u32[]{:S(2)}, u32[]{:S(2)}) collective-permute-start(f32[16,16,8]{2,1,0:T(8,128)S(1)} %get-tuple-element.119), channel_id=1, source_target_pairs={{0,2},{1,3},{4,6},{5,7},{8,10},{9,11},{12,14},{13,15},{16,18},{17,... | collective-permute-start | bytes 24584 | tf_op jit(solution)/shard_map/ppermute | solution.py:35
  151.4 6.9 %collective-permute-start.31 = (f32[16,16,8]{2,1,0:T(8,128)S(1)}, f32[16,16,8]{2,1,0:T(8,128)S(1)}, u32[]{:S(2)}, u32[]{:S(2)}) collective-permute-start(f32[16,16,8]{2,1,0:T(8,128)S(1)} %get-tuple-element.120), channel_id=1, source_target_pairs={{2,0},{3,1},{6,4},{7,5},{10,8},{11,9},{14,12},{15,13},{18,16},{19,... | collective-permute-start | bytes 24584 | tf_op jit(solution)/shard_map/ppermute | solution.py:35
  160.8 2.7 collective-permute-start.32
  162.1 5.1 %collective-permute-start.33 = (f32[16,1,16]{0,2,1:T(8,128)S(1)}, f32[16,1,16]{0,2,1:T(8,128)S(1)}, u32[]{:S(2)}, u32[]{:S(2)}) collective-permute-start(f32[16,1,16]{0,2,1:T(8,128)S(1)} %get-tuple-element.130), channel_id=1, source_target_pairs={{4,0},{8,4},{12,8},{16,12},{20,16},{24,20},{28,24},{5,1},{9,5},{13... | collective-permute-start | bytes 3080 | tf_op jit(solution)/shard_map/ppermute | solution.py:17
  167.3 8.8 %collective-permute-start.34 = (f32[16,10,1]{0,2,1:T(1,128)S(1)}, f32[16,10,1]{0,2,1:T(1,128)S(1)}, u32[]{:S(2)}, u32[]{:S(2)}) collective-permute-start(f32[16,10,1]{0,2,1:T(1,128)S(1)} %get-tuple-element.127), channel_id=1, source_target_pairs={{0,1},{1,2},{2,3},{4,5},{5,6},{6,7},{8,9},{9,10},{10,11},{12,13},{... | collective-permute-start | bytes 1928 | tf_op jit(solution)/shard_map/ppermute | solution.py:14
  170.6 5.5 %collective-permute-start.35 = (f32[16,10,1]{0,2,1:T(1,128)S(1)}, f32[16,10,1]{0,2,1:T(1,128)S(1)}, u32[]{:S(2)}, u32[]{:S(2)}) collective-permute-start(f32[16,10,1]{0,2,1:T(1,128)S(1)} %get-tuple-element.128), channel_id=1, source_target_pairs={{1,0},{2,1},{3,2},{5,4},{6,5},{7,6},{9,8},{10,9},{11,10},{13,12},{... | collective-permute-start | bytes 1928 | tf_op jit(solution)/shard_map/ppermute | solution.py:17
  173.4 14.6 %collective-permute-start.17 = (f32[34,32,32]{0,2,1:T(8,128)}, f32[34,32,32]{0,2,1:T(8,128)}, u32[]{:S(2)}, u32[]{:S(2)}) collective-permute-start(f32[34,32,32]{0,2,1:T(8,128)} %copy.64), channel_id=1, source_target_pairs={{0,1},{1,0},{2,3},{3,2},{4,5},{5,4},{6,7},{7,6},{8,9},{9,8},{10,11... | collective-permute-start | bytes 417800 | tf_op jit(solution)/shard_map/ppermute | solution.py:29
  190.9 6.9 %collective-permute-start.18 = (f32[16,8,64]{2,1,0:T(8,128)S(1)}, f32[16,8,64]{2,1,0:T(8,128)S(1)}, u32[]{:S(2)}, u32[]{:S(2)}) collective-permute-start(f32[16,8,64]{2,1,0:T(8,128)S(1)} %get-tuple-element.23), channel_id=1, source_target_pairs={{0,8},{4,12},{8,16},{12,20},{16,24},{20,28},{1,9},{5,13},{9,17},{1... | collective-permute-start | bytes 98312 | tf_op jit(solution)/shard_map/ppermute | solution.py:35
  195.9 6.2 %collective-permute-start.19 = (f32[16,8,64]{2,1,0:T(8,128)S(1)}, f32[16,8,64]{2,1,0:T(8,128)S(1)}, u32[]{:S(2)}, u32[]{:S(2)}) collective-permute-start(f32[16,8,64]{2,1,0:T(8,128)S(1)} %get-tuple-element.24), channel_id=1, source_target_pairs={{8,0},{12,4},{16,8},{20,12},{24,16},{28,20},{9,1},{13,5},{17,9},{2... | collective-permute-start | bytes 98312 | tf_op jit(solution)/shard_map/ppermute | solution.py:35
  203.6 8.1 %collective-permute-start.20 = (f32[16,32,8]{2,1,0:T(8,128)}, f32[16,32,8]{2,1,0:T(8,128)S(1)}, u32[]{:S(2)}, u32[]{:S(2)}) collective-permute-start(f32[16,32,8]{2,1,0:T(8,128)} %get-tuple-element.103), channel_id=1, source_target_pairs={{0,2},{1,3},{4,6},{5,7},{8,10},{9,11},{12,14},{13,15},{16,18},{17,... | collective-permute-start | bytes 49160 | tf_op jit(solution)/shard_map/ppermute | solution.py:35
  207.0 8.9 %collective-permute-start.21 = (f32[16,32,8]{2,1,0:T(8,128)}, f32[16,32,8]{2,1,0:T(8,128)}, u32[]{:S(2)}, u32[]{:S(2)}) collective-permute-start(f32[16,32,8]{2,1,0:T(8,128)} %get-tuple-element.104), channel_id=1, source_target_pairs={{2,0},{3,1},{6,4},{7,5},{10,8},{11,9},{14,12},{15,13},{18,16},{19,... | collective-permute-start | bytes 49160 | tf_op jit(solution)/shard_map/ppermute | solution.py:35
  221.8 3.8 %collective-permute-start.36 = (f32[16,1,32]{2,0,1:T(8,128)S(1)}, f32[16,1,32]{2,0,1:T(8,128)S(1)}, u32[]{:S(2)}, u32[]{:S(2)}) collective-permute-start(f32[16,1,32]{2,0,1:T(8,128)S(1)} %get-tuple-element.117), channel_id=1, source_target_pairs={{0,4},{4,8},{8,12},{12,16},{16,20},{20,24},{24,28},{1,5},{5,9},{9,... | collective-permute-start | bytes 6152 | tf_op jit(solution)/shard_map/ppermute | solution.py:14
  223.1 3.6 %collective-permute-start.37 = (f32[16,1,32]{2,0,1:T(8,128)S(1)}, f32[16,1,32]{2,0,1:T(8,128)S(1)}, u32[]{:S(2)}, u32[]{:S(2)}) collective-permute-start(f32[16,1,32]{2,0,1:T(8,128)S(1)} %get-tuple-element.118), channel_id=1, source_target_pairs={{4,0},{8,4},{12,8},{16,12},{20,16},{24,20},{28,24},{5,1},{9,5},{13... | collective-permute-start | bytes 6152 | tf_op jit(solution)/shard_map/ppermute | solution.py:17
  226.8 9.8 %collective-permute-start.38 = (f32[16,18,1]{2,0,1:T(8,128)S(1)}, f32[16,18,1]{2,0,1:T(8,128)S(1)}, u32[]{:S(2)}, u32[]{:S(2)}) collective-permute-start(f32[16,18,1]{2,0,1:T(8,128)S(1)} %get-tuple-element.115), channel_id=1, source_target_pairs={{0,1},{1,2},{2,3},{4,5},{5,6},{6,7},{8,9},{9,10},{10,11},{12,13},{... | collective-permute-start | bytes 3464 | tf_op jit(solution)/shard_map/ppermute | solution.py:14
  229.1 7.5 %collective-permute-start.39 = (f32[16,18,1]{2,0,1:T(8,128)S(1)}, f32[16,18,1]{2,0,1:T(8,128)S(1)}, u32[]{:S(2)}, u32[]{:S(2)}) collective-permute-start(f32[16,18,1]{2,0,1:T(8,128)S(1)} %get-tuple-element.116), channel_id=1, source_target_pairs={{1,0},{2,1},{3,2},{5,4},{6,5},{7,6},{9,8},{10,9},{11,10},{13,12},{... | collective-permute-start | bytes 3464 | tf_op jit(solution)/shard_map/ppermute | solution.py:17
  230.7 16.0 %collective-permute-start.2 = (f32[16,64,8]{2,1,0:T(8,128)S(1)}, f32[16,64,8]{2,1,0:T(8,128)S(1)}, u32[]{:S(2)}, u32[]{:S(2)}) collective-permute-start(f32[16,64,8]{2,1,0:T(8,128)S(1)} %get-tuple-element.72), channel_id=1, source_target_pairs={{0,1},{1,2},{2,3},{4,5},{5,6},{6,7},{8,9},{9,10},{10,11},{12,13},{... | collective-permute-start | bytes 98312 | tf_op jit(solution)/shard_map/ppermute | solution.py:14
  235.3 24.6 %collective-permute-start.3 = (f32[16,64,8]{2,1,0:T(8,128)S(1)}, f32[16,64,8]{2,1,0:T(8,128)S(1)}, u32[]{:S(2)}, u32[]{:S(2)}) collective-permute-start(f32[16,64,8]{2,1,0:T(8,128)S(1)} %get-tuple-element.73), channel_id=1, source_target_pairs={{1,0},{2,1},{3,2},{5,4},{6,5},{7,6},{9,8},{10,9},{11,10},{13,12},{... | collective-permute-start | bytes 98312 | tf_op jit(solution)/shard_map/ppermute | solution.py:17
  237.3 26.9 %collective-permute-start.40 = (f32[16,1,64]{2,0,1:T(8,128)S(1)}, f32[16,1,64]{2,0,1:T(8,128)S(1)}, u32[]{:S(2)}, u32[]{:S(2)}) collective-permute-start(f32[16,1,64]{2,0,1:T(8,128)S(1)} %get-tuple-element.101), channel_id=1, source_target_pairs={{0,4},{4,8},{8,12},{12,16},{16,20},{20,24},{24,28},{1,5},{5,9},{9,... | collective-permute-start | bytes 12296 | tf_op jit(solution)/shard_map/ppermute | solution.py:14
  240.8 23.5 %collective-permute-start.41 = (f32[16,1,64]{2,0,1:T(8,128)S(1)}, f32[16,1,64]{2,0,1:T(8,128)S(1)}, u32[]{:S(2)}, u32[]{:S(2)}) collective-permute-start(f32[16,1,64]{2,0,1:T(8,128)S(1)} %get-tuple-element.102), channel_id=1, source_target_pairs={{4,0},{8,4},{12,8},{16,12},{20,16},{24,20},{28,24},{5,1},{9,5},{13... | collective-permute-start | bytes 12296 | tf_op jit(solution)/shard_map/ppermute | solution.py:17
  264.4 9.6 %collective-permute-start.42 = (f32[16,34,1]{2,0,1:T(8,128)S(1)}, f32[16,34,1]{2,0,1:T(8,128)S(1)}, u32[]{:S(2)}, u32[]{:S(2)}) collective-permute-start(f32[16,34,1]{2,0,1:T(8,128)S(1)} %get-tuple-element.82), channel_id=1, source_target_pairs={{0,1},{1,2},{2,3},{4,5},{5,6},{6,7},{8,9},{9,10},{10,11},{12,13},{... | collective-permute-start | bytes 6536 | tf_op jit(solution)/shard_map/ppermute | solution.py:14
  267.2 13.3 %collective-permute-start.43 = (f32[16,34,1]{2,0,1:T(8,128)S(1)}, f32[16,34,1]{2,0,1:T(8,128)S(1)}, u32[]{:S(2)}, u32[]{:S(2)}) collective-permute-start(f32[16,34,1]{2,0,1:T(8,128)S(1)} %get-tuple-element.83), channel_id=1, source_target_pairs={{1,0},{2,1},{3,2},{5,4},{6,5},{7,6},{9,8},{10,9},{11,10},{13,12},{... | collective-permute-start | bytes 6536 | tf_op jit(solution)/shard_map/ppermute | solution.py:17
  (64 other events, 628.6 us)
where the time goes:
time: 285 us; the launch traced here: 283 us
  waiting for transfers between devices  102 us (36%)
  starting transfers between devices  94.6 us (33%)
  local copies, waits for them, and re-layouts  49.1 us (17%)
  other arithmetic  28.7 us (10%)
  matrix products  6.54 us (2%)
    ppermute x16, waiting for transfers between devices, extended(): lax.ppermute(lax.slice_in_dim(block, 0, width, axis=dim), axis, backward)  50.7 us
    ppermute x16, starting transfers between devices, extended(): lax.ppermute(lax.slice_in_dim(block, block.shape[dim] - width, None, axis...  48.7 us
    ppermute x16, starting transfers between devices, extended(): lax.ppermute(lax.slice_in_dim(block, 0, width, axis=dim), axis, backward)  21.1 us
    ppermute x8, waiting for transfers between devices, from_behind(): return lax.ppermute(shard, axis, pairs)  20.5 us
    ppermute x8, starting transfers between devices, from_behind(): return lax.ppermute(shard, axis, pairs)  18.6 us
    ppermute x16, waiting for transfers between devices, extended(): lax.ppermute(lax.slice_in_dim(block, block.shape[dim] - width, None, axis...  17.5 us
    ppermute x4, waiting for transfers between devices, swapped(): return lax.ppermute(block, axis, route)  13.4 us
    add x4, other arithmetic, north_pass(): running + factors[offset][None] * padded[:, :, offset:offset + col_count]  11.9 us
  transfers between devices with their start and end apart: 44, of which 26 were waited for; matrix products, arithmetic and copies ran while one was open for 25% of the time, Pallas kernels for 0%

commit v1 on v0

v1 whole, which is shorter than its diff:
```python
import functools

import jax
import jax.numpy as jnp
import numpy as np
from jax import lax
from jax.experimental import pallas as pl
from jax.experimental.pallas import tpu as pltpu
from jax.sharding import PartitionSpec as P

H = 8
LANES = 128
LEVELS = 3
F32 = jnp.float32
BF16 = jnp.bfloat16
SLOT = H + 2
PER_TILE = LANES // SLOT


def tables(rows, cols):
    bases, at = [], H
    for l in range(1, LEVELS + 1):
        bases.append(at)
        at += (cols >> l) + 2
    assert at <= LANES and cols == LANES
    down = np.zeros((4, cols, LANES), np.float32)
    for variant in range(4):
        current = np.eye(cols)
        low = 0
        for l in range(1, LEVELS + 1):
            m = cols >> l
            step = np.zeros((current.shape[1], m + 2))
            for j in range(-1, m + 1):
                for f, w in ((2 * j, 0.375), (2 * j + 1, 0.375), (2 * j - 1, 0.125), (2 * j + 2, 0.125)):
                    if 0 <= f - low < current.shape[1]:
                        step[f - low, j + 1] += w
            current = current @ step
            if variant & 1:
                current[:, 0] = 0
            if variant & 2:
                current[:, -1] = 0
            low = -1
            down[variant, :, bases[l - 1] : bases[l - 1] + m + 2] = current
    up = np.zeros((LEVELS + 1, LANES, LANES), np.float32)
    for l in range(LEVELS):
        m = cols >> l
        for f in range(-1, m + 1) if l else range(m):
            j = f // 2
            out = f + H + 1 if l else f
            up[l, j + H + 1, out] += 0.75
            up[l, j + (1 if f % 2 else -1) + H + 1, out] += 0.25
    for z in range(16):
        for i in range(8):
            j = i // 2 + 1
            up[LEVELS, z * 8 + i, j * 16 + z] += 0.75
            up[LEVELS, z * 8 + i, (j + (1 if i % 2 else -1)) * 16 + z] += 0.25
    for t in (down, up):
        assert (t == t.astype(jnp.bfloat16).astype(np.float32)).all()
    return bases, down.astype(jnp.bfloat16), up.astype(jnp.bfloat16)


def split(x):
    high = x.astype(BF16)
    return high, (x - high.astype(F32)).astype(BF16)


def mm(a, b):
    return jnp.dot(a, b, preferred_element_type=F32)


def dot_exact(x, weights):
    high, low = split(x)
    return mm(high, weights) + mm(low, weights)


def lanes_of(rows):
    return lax.broadcasted_iota(jnp.int32, (rows, LANES), 1)


def roll(x, shift):
    shift %= LANES
    return pltpu.roll(x, shift, 1) if shift else x


def taps(widths):
    grown = widths + 1.0
    inverse = 1.0 / (grown * grown)
    profile = [jnp.square(jnp.maximum(1.0 - float(k * k) * inverse, 0.0)) for k in range(1, H + 1)]
    total = profile[0]
    for p in profile[1:]:
        total = total + p
    scale = 1.0 / (1.0 + 2.0 * total)
    return [scale] + [p * scale for p in profile]


def prepare(geo, inc, *refs):
    widths, gains = refs[:LEVELS], refs[LEVELS : 2 * LEVELS]
    table, field, *rest = refs[2 * LEVELS :]
    coarse, (send_a, send_b, send_c, send_d, half) = rest[:LEVELS], rest[LEVELS:]
    Z, R, M, bases = geo["Z"], geo["R"], geo["M"], geo["bases"]
    e, n = lax.axis_index("east"), lax.axis_index("north")
    has_low, has_high = e > 0, e < geo["E"] - 1
    even = e % 2 == 0
    flat = field.reshape(R * Z, M)
    for z in range(Z):
        flat[pl.ds(z, R, stride=Z), :] = inc[z]
    variant = (n == 0).astype(jnp.int32) + 2 * (n == geo["N"] - 1).astype(jnp.int32)
    weights = table[variant]
    half_flat = half.reshape(R * Z, M)
    chunk = R * Z // 4
    for c in range(4):
        half_flat[pl.ds(c * chunk, chunk), :] = dot_exact(flat[pl.ds(c * chunk, chunk), :], weights)
    source, low, top = half, 0, R
    for l in range(1, LEVELS + 1):
        r, out = R >> l, coarse[l - 1]

        def get(i, source=source, low=low, top=top):
            return source[i - low] if low <= i < top else None

        for j in range(-1, r + 1):
            total = None
            for pair, w in (((2 * j, 2 * j + 1), 0.375), ((2 * j - 1, 2 * j + 2), 0.125)):
                terms = [t for t in (get(i) for i in pair) if t is not None]
                if terms:
                    part = w * functools.reduce(jnp.add, terms)
                    total = part if total is None else total + part
            if j == -1:
                total = jnp.where(has_low, total, 0.0)
            if j == r:
                total = jnp.where(has_high, total, 0.0)
            out[j + 1] = total
        source, low, top = out, -1, r + 1
    start = R - H
    send_a[0:H] = field[pl.ds(jnp.where(even, start, 0), H)]
    send_b[0:H] = field[pl.ds(jnp.where(even, 0, start), H)]
    lane = lanes_of(Z)
    for i in range(SLOT):
        def merged(picks):
            out = coarse[LEVELS - 1][picks[LEVELS - 1]]
            for l in range(LEVELS - 1, 0, -1):
                out = jnp.where(lane < bases[l], coarse[l - 1][picks[l - 1]], out)
            return out

        lower = merged([i] * LEVELS)
        upper = merged([(R >> l) - H + i for l in range(1, LEVELS + 1)])
        send_a[H + i] = jnp.where(even, upper, lower)
        send_b[H + i] = jnp.where(even, lower, upper)
    last = H + SLOT
    send_a[last] = jnp.zeros((Z, LANES), F32)
    send_b[last] = jnp.zeros((Z, LANES), F32)
    for j, ref in enumerate((*widths, *gains)):
        r, m = ref.shape
        lower = ref[pl.ds(0, 1), :].astype(F32)
        upper = ref[pl.ds(r - 1, 1), :].astype(F32)
        send_a[last, pl.ds(j, 1), pl.ds(0, m)] = jnp.where(even, upper, lower)
        send_b[last, pl.ds(j, 1), pl.ds(0, m)] = jnp.where(even, lower, upper)
    r = R >> LEVELS
    forward = (e // 2) % 2 == 0
    for i in range(2):
        lower, upper = coarse[LEVELS - 1][i], coarse[LEVELS - 1][r + i]
        send_c[i] = jnp.where(forward, upper, lower)
        send_d[i] = jnp.where(forward, lower, upper)


def east_rows(source, factors, out, count, block, factor_at=0):
    def step(b, carry):
        x0 = b * block
        rows = [source[x0 + i] for i in range(block + 2 * H)]
        for i in range(block):
            def factor(k):
                return factors[k, pl.ds(x0 + i + factor_at, 1), :]

            total = factor(0) * rows[i + H]
            for k in range(1, H + 1):
                total = total + factor(k) * (rows[i + H + k] + rows[i + H - k])
            out[x0 + i] = total
        return carry

    lax.fori_loop(0, count // block, step, 0)


def middle(geo, *refs):
    Z, R, M, bases = geo["Z"], geo["R"], geo["M"], geo["bases"]
    it = iter(refs)
    take = lambda count: [next(it) for _ in range(count)]
    (field,) = take(1)
    coarse = take(LEVELS)
    got_a, got_b, got_c, got_d, widths0 = take(5)
    widths, gains = take(LEVELS), take(LEVELS)
    eastward, factors = take(2)
    joined = take(LEVELS)
    send_x, send_y = take(2)
    wide, gain = take(LEVELS), take(LEVELS)
    (full,) = take(1)
    e, n = lax.axis_index("east"), lax.axis_index("north")
    even = e % 2 == 0
    forward = (e // 2) % 2 == 0
    for k, a in enumerate(taps(widths0[...].astype(F32))):
        factors[k] = a
    full[pl.ds(H, R)] = field[...]
    full[0:H] = jnp.where(even, got_b[0:H], got_a[0:H])
    full[H + R : R + 2 * H] = jnp.where(even, got_a[0:H], got_b[0:H])
    east_rows(full, factors, eastward, R, 2)
    for l in range(1, LEVELS + 1):
        r, out, own = R >> l, joined[l - 1], coarse[l - 1]
        out[H : H + r + 2] = own[...]
        out[0:H] = jnp.zeros((H, Z, LANES), F32)
        out[H + r + 2 : 2 * H + r + 2] = jnp.zeros((H, Z, LANES), F32)
    for i in range(SLOT):
        a, b = got_a[H + i], got_b[H + i]
        lower, upper = jnp.where(even, b, a), jnp.where(even, a, b)
        for l in range(1, LEVELS + 1):
            r, out = R >> l, joined[l - 1]
            out[i] = out[i] + lower
            out[r + H + i] = out[r + H + i] + upper
    r, out = R >> LEVELS, joined[LEVELS - 1]
    for i in range(2):
        c, d = got_c[i], got_d[i]
        out[i] = out[i] + jnp.where(forward, d, c)
        out[r + 2 * H + i] = out[r + 2 * H + i] + jnp.where(forward, c, d)
    last = H + SLOT
    rows_a, rows_b = got_a[last], got_b[last]
    lower, upper = jnp.where(even, rows_b, rows_a), jnp.where(even, rows_a, rows_b)
    for j, (own, out) in enumerate(zip((*widths, *gains), (*wide, *gain))):
        r, m = own.shape
        out[...] = jnp.zeros(out.shape, F32)
        out[pl.ds(H, r), pl.ds(H + 1, m)] = own[...].astype(F32)
        out[pl.ds(H - 1, 1), pl.ds(H + 1, m)] = lower[j : j + 1, 0:m]
        out[pl.ds(H + r, 1), pl.ds(H + 1, m)] = upper[j : j + 1, 0:m]
    north_even = n % 2 == 0
    lane = lanes_of(Z)

    def send(t, low_side, high_side):
        send_x[t] = jnp.where(north_even, high_side, low_side)
        send_y[t] = jnp.where(north_even, low_side, high_side)

    zero = jnp.zeros((Z, LANES), F32)
    todo = [(l, i) for l in range(LEVELS) for i in range(joined[l].shape[0])]
    for t in range(geo["coarse_tiles"]):
        low_side, high_side = zero, zero
        for s, (l, i) in enumerate(todo[t * PER_TILE : (t + 1) * PER_TILE]):
            row, m = joined[l][i], M >> (l + 1)
            here = (lane >= SLOT * s) & (lane < SLOT * (s + 1))
            low_side = jnp.where(here, roll(row, SLOT * s - bases[l]), low_side)
            high_side = jnp.where(here, roll(row, SLOT * s - bases[l] - m + H), high_side)
        send(t, low_side, high_side)
    per = LANES // H
    for t in range(R // per):
        low_side, high_side = zero, zero
        for s in range(per):
            row = eastward[t * per + s]
            here = (lane >= H * s) & (lane < H * (s + 1))
            low_side = jnp.where(here, roll(row, H * s), low_side)
            high_side = jnp.where(here, roll(row, H * s - M + H), high_side)
        send(geo["coarse_tiles"] + t, low_side, high_side)
    base = geo["coarse_tiles"] + R // per
    for t in range(wide[0].shape[0] // Z):
        low_side, high_side = zero, zero
        for j, ref in enumerate((*wide, *gain)):
            rows, m = ref.shape[0], M >> (j % LEVELS + 1)
            have = min(max(rows - t * Z, 0), Z)
            if not have:
                continue
            part = ref[pl.ds(t * Z, have), :]
            if have < Z:
                part = jnp.concatenate([part, jnp.zeros((Z - have, LANES), F32)], axis=0)
            here = (lane >= 16 * j) & (lane < 16 * j + H + 1)
            low_side = jnp.where(here, roll(part, 16 * j - H - 1), low_side)
            high_side = jnp.where(here, roll(part, 16 * j - m), high_side)
        send(base + t, low_side, high_side)


def kron(vertical, transposed):
    Z = 16
    i = lax.broadcasted_iota(jnp.int32, (LANES, Z), 0)
    a = lax.broadcasted_iota(jnp.int32, (LANES, Z), 1)
    left = ((i // 8 if transposed else i % Z) == a).astype(F32).astype(BF16)
    b = lax.broadcasted_iota(jnp.int32, (Z, LANES), 0)
    o = lax.broadcasted_iota(jnp.int32, (Z, LANES), 1)
    right = (o % Z == b).astype(F32).astype(BF16)
    p = lax.broadcasted_iota(jnp.int32, (LANES, LANES), 0)
    q = lax.broadcasted_iota(jnp.int32, (LANES, LANES), 1)
    mask = (p % 8 if transposed else p // Z) == q // Z
    return [jnp.where(mask, mm(mm(left, part).astype(BF16), right), 0.0).astype(BF16) for part in split(vertical)]


def mix(matrix, data):
    high, low = split(data)
    return mm(matrix[0], high) + mm(matrix[0], low) + mm(matrix[1], high)


def finish(geo, *refs):
    Z, R, M, bases = geo["Z"], geo["R"], geo["M"], geo["bases"]
    it = iter(refs)
    take = lambda count: [next(it) for _ in range(count)]
    eastward, factors = take(2)
    joined = take(LEVELS)
    wide, gain = take(LEVELS), take(LEVELS)
    got_x, got_y, gain0, vertical, table = take(5)
    (out,) = take(1)
    got_low, got_high, ext, coarse_factors, passed, north, result, spread, wf, gf = take(10)
    e, n = lax.axis_index("east"), lax.axis_index("north")
    has_low, has_high = e > 0, e < geo["E"] - 1
    north_even = n % 2 == 0
    got_low[...] = jnp.where(north_even, got_y[...], got_x[...])
    got_high[...] = jnp.where(north_even, got_x[...], got_y[...])
    lane = lanes_of(Z)
    per = LANES // H
    base = geo["coarse_tiles"] + R // per
    first = 0
    starts = []
    for l in range(LEVELS):
        starts.append(first)
        first += joined[l].shape[0]
    previous = None
    for l in range(LEVELS - 1, -1, -1):
        r, m = R >> (l + 1), M >> (l + 1)
        rows = r + 2 * H + 2
        count = wide[l].shape[0]
        for source, target, j in ((wide[l], wf, l), (gain[l], gf, LEVELS + l)):
            for c in range(0, count, 8):
                t, at = base + c // Z, c % Z
                lane8 = lanes_of(8)
                low_side = roll(got_low[t, at : at + 8, :], -16 * j)
                high_side = roll(got_high[t, at : at + 8, :], m + H + 1 - 16 * j)
                own = source[pl.ds(c, 8), :]
                target[pl.ds(c, 8), :] = jnp.where(
                    lane8 < H + 1, low_side, jnp.where(lane8 < m + H + 1, own, jnp.where(lane8 < m + 2 * H + 2, high_side, 0.0))
                )
        for k, a in enumerate(taps(wf[pl.ds(0, count), :])):
            coarse_factors[k, pl.ds(0, count), :] = a
        for i in range(rows):
            t, s = divmod(starts[l] + i, PER_TILE)
            own = roll(joined[l][i], H - bases[l])
            low_side = roll(got_low[t], -SLOT * s)
            high_side = roll(got_high[t], m + H - SLOT * s)
            ext[i] = (
                jnp.where((lane >= H) & (lane < m + H + 2), own, 0.0)
                + jnp.where(lane < SLOT, low_side, 0.0)
                + jnp.where((lane >= m + H) & (lane < m + H + SLOT), high_side, 0.0)
            )
        east_rows(ext, coarse_factors, passed, r + 2, 2, H - 1)

        def step(b, carry):
            for i in range(2):
                x = 2 * b + i
                value = passed[x]
                total = coarse_factors[0, pl.ds(x + H - 1, 1), :] * value
                for k in range(1, H + 1):
                    total = total + coarse_factors[k, pl.ds(x + H - 1, 1), :] * (roll(value, -k) + roll(value, k))
                north[x] = total
            return carry

        lax.fori_loop(0, (r + 2) // 2, step, 0)
        groups = (r + 2 + 7) // 8
        north[r + 2 : groups * 8] = jnp.zeros((groups * 8 - r - 2, Z, LANES), F32)
        matrix = kron(vertical[l + 1] * 4.0 ** (l + 1), False)
        for g in range(groups):
            mixed = mix(matrix, north[8 * g : 8 * g + 8].reshape(8 * Z, LANES))
            for i in range(8):
                row = 8 * g + i
                if row < r + 2:
                    result[row] = gf[pl.ds(row + H - 1, 1), :] * mixed[i * Z : (i + 1) * Z]
        if previous is not None:
            inside = ((lane > H) | (n > 0)) & ((lane < m + H + 1) | (n < geo["N"] - 1))
            for row in range(-1, r + 1):
                j = row // 2
                other = j + (1 if row % 2 else -1)
                total = result[row + 1] + 0.75 * spread[j + 1] + 0.25 * spread[other + 1]
                keep = inside
                if row == -1:
                    keep = keep & has_low
                if row == r:
                    keep = keep & has_high
                result[row + 1] = jnp.where(keep, total, 0.0)
        flat = result.reshape(result.shape[0] * Z, LANES)
        spread_flat = spread.reshape(spread.shape[0] * Z, LANES)
        weights = table[l]
        spread_flat[pl.ds(0, (r + 2) * Z), :] = dot_exact(flat[pl.ds(0, (r + 2) * Z), :], weights)
        previous = True
    matrix = kron(vertical[0], True)
    widen = table[LEVELS][:, 0 : 6 * Z]

    def block(b, carry):
        t = geo["coarse_tiles"] + b // 2
        for i in range(8):
            x = 8 * b + i
            value = eastward[x]
            s = (b % 2) * 8 + i
            low_side = pltpu.roll(got_low[t], (2 * LANES - H - H * s) % LANES, 1)
            high_side = pltpu.roll(got_high[t], (2 * LANES - H * s) % LANES, 1)
            halo = jnp.where(lane < LANES // 2, high_side, low_side)
            total = factors[0, pl.ds(x, 1), :] * value
            for k in range(1, H + 1):
                ahead = roll(jnp.where(lane < k, halo, value), -k)
                behind = roll(jnp.where(lane >= LANES - k, halo, value), k)
                total = total + factors[k, pl.ds(x, 1), :] * (ahead + behind)
            north[i] = total
        mixed = mix(matrix, north[0:8].reshape(8 * Z, LANES))
        coarse = spread[pl.ds(4 * b, 6)].reshape(6 * Z, LANES)
        high, low = split(coarse)
        added = mm(widen, high) + mm(widen, low)
        weight = gain0[pl.ds(pl.multiple_of(8 * b, 8), 8), :]
        for z in range(Z):
            out[z, pl.ds(pl.multiple_of(8 * b, 8), 8), :] = weight * mixed[z * 8 : z * 8 + 8] + added[z * 8 : z * 8 + 8]
        return carry

    lax.fori_loop(0, R // 8, block, 0)


def swap(x, axis, first, by=1):
    count = lax.axis_size(axis)
    route = []
    for i in range(count - by):
        if (i // by) % 2 == first:
            route += [(i, i + by), (i + by, i)]
    return lax.ppermute(x, axis, route)


def body(inc, w0, w1, w2, w3, g0, g1, g2, g3, vertical):
    Z, R, M = inc.shape
    bases, down, up = tables(R, M)
    total_rows = sum((R >> l) + 2 * H + 2 for l in range(1, LEVELS + 1))
    geo = dict(
        Z=Z, R=R, M=M, bases=bases, E=lax.axis_size("east"), N=lax.axis_size("north"),
        coarse_tiles=-(-total_rows // PER_TILE),
    )
    shape = lambda *dims: jax.ShapeDtypeStruct(dims, F32)
    levels = range(1, LEVELS + 1)
    params = pltpu.CompilerParams(vmem_limit_bytes=48 * 1024 * 1024)
    east_tiles = H + SLOT + 1
    outs = pl.pallas_call(
        functools.partial(prepare, geo),
        out_shape=[shape(R, Z, M)] + [shape((R >> l) + 2, Z, M) for l in levels]
        + [shape(east_tiles, Z, M)] * 2 + [shape(2, Z, M)] * 2,
        scratch_shapes=[pltpu.VMEM((R, Z, M), F32)],
        compiler_params=params,
    )(inc, w1, w2, w3, g1, g2, g3, jnp.asarray(down))
    field, coarse, sends = outs[0], outs[1 : 1 + LEVELS], outs[1 + LEVELS :]
    got_b = swap(sends[1], "east", 1)
    got_a = swap(sends[0], "east", 0)
    got_c = swap(sends[2], "east", 0, 2)
    got_d = swap(sends[3], "east", 1, 2)
    wide_shapes = [shape((R >> l) + 2 * H, M) for l in levels]
    north_tiles = geo["coarse_tiles"] + R * H // LANES + wide_shapes[0].shape[0] // Z
    outs = pl.pallas_call(
        functools.partial(middle, geo),
        out_shape=[shape(R, Z, M), shape(H + 1, R, M)]
        + [shape((R >> l) + 2 * H + 2, Z, M) for l in levels]
        + [shape(north_tiles, Z, M)] * 2 + wide_shapes * 2,
        scratch_shapes=[pltpu.VMEM((R + 2 * H, Z, M), F32)],
        compiler_params=params,
    )(field, *coarse, got_a, got_b, got_c, got_d, w0, w1, w2, w3, g1, g2, g3)
    eastward, factors = outs[0], outs[1]
    joined, (send_x, send_y) = outs[2 : 2 + LEVELS], outs[2 + LEVELS : 4 + LEVELS]
    wide, gain = outs[4 + LEVELS : 4 + 2 * LEVELS], outs[4 + 2 * LEVELS :]
    got_x = swap(send_x, "north", 0)
    got_y = swap(send_y, "north", 1)
    rows1 = (R >> 1) + 2
    padded = -(-rows1 // 8) * 8
    return pl.pallas_call(
        functools.partial(finish, geo),
        out_shape=shape(Z, R, M),
        scratch_shapes=[
            pltpu.VMEM((north_tiles, Z, M), F32),
            pltpu.VMEM((north_tiles, Z, M), F32),
            pltpu.VMEM((rows1 + 2 * H, Z, M), F32),
            pltpu.VMEM((H + 1, wide_shapes[0].shape[0], M), F32),
            pltpu.VMEM((rows1, Z, M), F32),
            pltpu.VMEM((padded, Z, M), F32),
            pltpu.VMEM((rows1, Z, M), F32),
            pltpu.VMEM((rows1, Z, M), F32),
            pltpu.VMEM(wide_shapes[0].shape, F32),
            pltpu.VMEM(wide_shapes[0].shape, F32),
        ],
        compiler_params=params,
    )(eastward, factors, *joined, *wide, *gain, got_x, got_y, g0, vertical, jnp.asarray(up))


def solution(mesh):
    tile = P("east", "north")
    return jax.shard_map(
        body,
        mesh=mesh,
        in_specs=(P(None, "east", "north"), *([tile] * 8), P()),
        out_specs=P(None, "east", "north"),
        check_vma=False,
    )
```

time: 285 us -> 41.3 us (0.14)
  the two profiles are of different devices: /device:TPU:0 before, /device:TPU:20 now
where the time goes in v1:
time: 41.3 us; the launch traced here: 40.7 us
  Pallas kernels  15.1 us (37%)
  starting transfers between devices  10.1 us (24%)
  waiting for transfers between devices  9.16 us (22%)
  local copies, waits for them, and re-layouts  6.17 us (15%)
    pallas_call x1, Pallas kernels, body(): pl.pallas_call(functools.partial(finish, geo), out_shape=shape(Z, R, M),...  13 us
    ppermute x6, starting transfers between devices, swap(): return lax.ppermute(x, axis, route)  10.1 us
    ppermute x6, waiting for transfers between devices, swap(): return lax.ppermute(x, axis, route)  9.16 us
    unnamed x26, local copies, waits for them, and re-layouts  6.17 us
    pallas_call x1, Pallas kernels, body(): pl.pallas_call(functools.partial(middle, geo), out_shape=[shape(R, Z, M),...  1.71 us
  transfers between devices with their start and end apart: 6, of which 4 were waited for; matrix products, arithmetic and copies ran while one was open for 0% of the time, Pallas kernels for 0%

profile of v1, /device:TPU:20, one launch (start us, length us, event | category | flops | bytes accessed | tf_op | source)
XLA Modules:
  0.0 40.7 jit_solution(5243623650650606521)
XLA Ops:
  0.0 0.0 copy-start
  0.0 1.0 %copy-done = f32[16,64,128]{2,1,0:T(8,128)S(1)} copy-done((f32[16,64,128]{2,1,0:T(8,128)S(1)}, f32[16,64,128]{2,1,0:T(8,128)}, u32[]{:S(2)}) %copy-start) | copy-done | bytes 524312
  1.0 0.0 copy-start.2
  1.0 0.9 %copy-done.2 = bf16[4,128,128]{2,1,0:T(8,128)(2,1)S(1)} copy-done((bf16[4,128,128]{2,1,0:T(8,128)(2,1)S(1)}, bf16[4,128,128]{2,1,0:T(8,128)(2,1)}, u32[]{:S(2)}) %copy-start.2) | copy-done | bytes 131096
  1.9 0.0 copy-start.3
  1.9 0.7 %copy-done.3 = s32[32,64]{1,0:T(8,128)S(1)} copy-done((s32[32,64]{1,0:T(8,128)S(1)}, s32[32,64]{1,0:T(8,128)}, u32[]{:S(2)}) %copy-start.3) | copy-done | bytes 8216
  2.7 0.0 copy-start.4
  2.7 0.7 %copy-done.4 = f32[32,64]{1,0:T(8,128)S(1)} copy-done((f32[32,64]{1,0:T(8,128)S(1)}, f32[32,64]{1,0:T(8,128)}, u32[]{:S(2)}) %copy-start.4) | copy-done | bytes 8216
  3.4 0.0 copy-start.7
  3.4 0.7 %copy-done.7 = s32[16,32]{1,0:T(8,128)S(1)} copy-done((s32[16,32]{1,0:T(8,128)S(1)}, s32[16,32]{1,0:T(8,128)}, u32[]{:S(2)}) %copy-start.7) | copy-done | bytes 2072
  4.1 0.0 copy-start.8
  4.1 0.7 %copy-done.8 = f32[16,32]{1,0:T(8,128)S(1)} copy-done((f32[16,32]{1,0:T(8,128)S(1)}, f32[16,32]{1,0:T(8,128)}, u32[]{:S(2)}) %copy-start.8) | copy-done | bytes 2072
  4.8 0.0 copy-start.10
  4.8 0.7 %copy-done.10 = s32[8,16]{1,0:T(8,128)S(1)} copy-done((s32[8,16]{1,0:T(8,128)S(1)}, s32[8,16]{1,0:T(8,128)}, u32[]{:S(2)}) %copy-start.10) | copy-done | bytes 536
  5.5 0.0 copy-start.11
  5.5 0.7 %copy-done.11 = f32[8,16]{1,0:T(8,128)S(1)} copy-done((f32[8,16]{1,0:T(8,128)S(1)}, f32[8,16]{1,0:T(8,128)}, u32[]{:S(2)}) %copy-start.11) | copy-done | bytes 536
  6.2 0.0 copy-start.9
  6.2 0.4 %shard_map.118 = (f32[64,16,128]{2,1,0:T(8,128)S(1)}, f32[34,16,128]{2,1,0:T(8,128)S(1)}, f32[18,16,128]{2,1,0:T(8,128)S(1)}, f32[10,16,128]{2,1,0:T(8,128)S(1)}...) custom-call(f32[16,64,128]{2,1,0:T(8,128)S(1)} %copy-done, ...), custom_call_target="tpu_custom_call" | custom-call | tf_op jit(solution)/shard_map/pallas_call | solution.py:432
  6.6 0.1 collective-permute-start
  6.7 2.4 %collective-permute-start.1 = (f32[19,16,128]{2,1,0:T(8,128)S(1)}, f32[19,16,128]{2,1,0:T(8,128)S(1)}, u32[]{:S(2)}, u32[]{:S(2)}) collective-permute-start(f32[19,16,128]{2,1,0:T(8,128)S(1)} %get-tuple-element.31), channel_id=1, source_target_pairs={{4,8},{8,4},{12,16},{16,12},{20,24},{24,20},{5,9},{9,5},{13,17},{1... | collective-permute-start | bytes 466952 | tf_op jit(solution)/shard_map/ppermute | solution.py:417
  9.1 1.6 %collective-permute-start.2 = (f32[2,16,128]{2,1,0:T(8,128)S(1)}, f32[2,16,128]{2,1,0:T(8,128)S(1)}, u32[]{:S(2)}, u32[]{:S(2)}) collective-permute-start(f32[2,16,128]{2,1,0:T(8,128)S(1)} %get-tuple-element.32), channel_id=1, source_target_pairs={{0,8},{8,0},{4,12},{12,4},{16,24},{24,16},{20,28},{28,20},{1,9},{9... | collective-permute-start | bytes 49160 | tf_op jit(solution)/shard_map/ppermute | solution.py:417
  10.8 0.0 copy-start.12
  10.8 2.0 %collective-permute-start.3 = (f32[2,16,128]{2,1,0:T(8,128)S(1)}, f32[2,16,128]{2,1,0:T(8,128)S(1)}, u32[]{:S(2)}, u32[]{:S(2)}) collective-permute-start(f32[2,16,128]{2,1,0:T(8,128)S(1)} %get-tuple-element.33), channel_id=1, source_target_pairs={{8,16},{16,8},{12,20},{20,12},{9,17},{17,9},{13,21},{21,13},{10,18... | collective-permute-start | bytes 49160 | tf_op jit(solution)/shard_map/ppermute | solution.py:417
  12.8 1.4 %collective-permute-done.2.refs_6_ = f32[2,16,128]{2,1,0:T(8,128)S(1)} collective-permute-done((f32[2,16,128]{2,1,0:T(8,128)S(1)}, f32[2,16,128]{2,1,0:T(8,128)S(1)}, u32[]{:S(2)}, u32[]{:S(2)}) %collective-permute-start.2) | collective-permute-done | bytes 16416 | tf_op jit(solution)/shard_map/ppermute | solution.py:417
  14.2 2.3 %collective-permute-done.3.refs_7_ = f32[2,16,128]{2,1,0:T(8,128)S(1)} collective-permute-done((f32[2,16,128]{2,1,0:T(8,128)S(1)}, f32[2,16,128]{2,1,0:T(8,128)S(1)}, u32[]{:S(2)}, u32[]{:S(2)}) %collective-permute-start.3) | collective-permute-done | bytes 16416 | tf_op jit(solution)/shard_map/ppermute | solution.py:417
  16.5 0.0 collective-permute-done.refs_4_
  16.5 0.0 collective-permute-done.1.refs_5_
  16.5 0.0 copy-done.9
  16.5 0.0 copy-done.12
  16.5 0.0 copy-start.1
  16.6 0.0 copy-start.5
  16.6 0.0 copy-start.6
  16.6 1.7 %shard_map.119 = (f32[64,16,128]{2,1,0:T(8,128)S(1)}, f32[9,64,128]{2,1,0:T(8,128)S(1)}, f32[50,16,128]{2,1,0:T(8,128)S(1)}, f32[34,16,128]{2,1,0:T(8,128)S(1)},...) custom-call(f32[64,16,128]{2,1,0:T(8,128)S(1)} %get-tuple-element.26, ...), custom_call_target="tpu_custom_call" | custom-call | tf_op jit(solution)/shard_map/pallas_call | solution.py:446
  18.3 1.6 %collective-permute-start.4 = (f32[17,16,128]{2,1,0:T(8,128)S(1)}, f32[17,16,128]{2,1,0:T(8,128)S(1)}, u32[]{:S(2)}, u32[]{:S(2)}) collective-permute-start(f32[17,16,128]{2,1,0:T(8,128)S(1)} %get-tuple-element.45), channel_id=1, source_target_pairs={{0,1},{1,0},{2,3},{3,2},{4,5},{5,4},{6,7},{7,6},{8,9},{9,8},{10,11... | collective-permute-start | bytes 417800 | tf_op jit(solution)/shard_map/ppermute | solution.py:417
  19.9 2.4 %collective-permute-start.5 = (f32[17,16,128]{2,1,0:T(8,128)S(1)}, f32[17,16,128]{2,1,0:T(8,128)S(1)}, u32[]{:S(2)}, u32[]{:S(2)}) collective-permute-start(f32[17,16,128]{2,1,0:T(8,128)S(1)} %get-tuple-element.46), channel_id=1, source_target_pairs={{1,2},{2,1},{5,6},{6,5},{9,10},{10,9},{13,14},{14,13},{17,18},{18,... | collective-permute-start | bytes 417800 | tf_op jit(solution)/shard_map/ppermute | solution.py:417
  22.2 1.2 %collective-permute-done.4.refs_11_ = f32[17,16,128]{2,1,0:T(8,128)S(1)} collective-permute-done((f32[17,16,128]{2,1,0:T(8,128)S(1)}, f32[17,16,128]{2,1,0:T(8,128)S(1)}, u32[]{:S(2)}, u32[]{:S(2)}) %collective-permute-start.4) | collective-permute-done | bytes 139296 | tf_op jit(solution)/shard_map/ppermute | solution.py:417
  23.4 4.3 %collective-permute-done.5.refs_12_ = f32[17,16,128]{2,1,0:T(8,128)S(1)} collective-permute-done((f32[17,16,128]{2,1,0:T(8,128)S(1)}, f32[17,16,128]{2,1,0:T(8,128)S(1)}, u32[]{:S(2)}, u32[]{:S(2)}) %collective-permute-start.5) | collective-permute-done | bytes 139296 | tf_op jit(solution)/shard_map/ppermute | solution.py:417
  27.7 0.0 copy-done.1
  27.7 0.0 copy-done.5
  27.7 0.0 copy-done.6
  27.7 13.0 %shard_map.120 = f32[16,64,128]{2,1,0:T(8,128)} custom-call(f32[64,16,128]{2,1,0:T(8,128)S(1)} %get-tuple-element.34.refs_0_, f32[9,64,128]{2,1,0:T(8,128)S(1)} %get-tuple-element.35.refs_1_, f32[50,16,128]{2,1,0:T(8,128)S(1)} %get-tuple-element.36.refs_2_, f32[34,16,128]{2,1,0:T(8,128)S(1)} %get-tuple-element.37.refs_3_, ...), custom_call_target="tpu_custom_call" | custom-call | tf_op jit(solution)/shard_map/pallas_call | solution.py:461
Async XLA Ops:
  0.0 1.0 %copy-start = (f32[16,64,128]{2,1,0:T(8,128)S(1)}, f32[16,64,128]{2,1,0:T(8,128)}, u32[]{:S(2)}) copy-start(f32[16,64,128]{2,1,0:T(8,128)} %inc.1) | copy-start | bytes 1572868
  1.0 0.9 %copy-start.2 = (bf16[4,128,128]{2,1,0:T(8,128)(2,1)S(1)}, bf16[4,128,128]{2,1,0:T(8,128)(2,1)}, u32[]{:S(2)}) copy-start(bf16[4,128,128]{2,1,0:T(8,128)(2,1)} %constant.4.clone.refs_6_) | copy-start | bytes 393220
  1.9 0.7 %copy-start.3 = (s32[32,64]{1,0:T(8,128)S(1)}, s32[32,64]{1,0:T(8,128)}, u32[]{:S(2)}) copy-start(s32[32,64]{1,0:T(8,128)} %refs_9_.1) | copy-start | bytes 24580
  2.7 0.7 %copy-start.4 = (f32[32,64]{1,0:T(8,128)S(1)}, f32[32,64]{1,0:T(8,128)}, u32[]{:S(2)}) copy-start(f32[32,64]{1,0:T(8,128)} %refs_12_.1) | copy-start | bytes 24580
  3.4 0.7 %copy-start.7 = (s32[16,32]{1,0:T(8,128)S(1)}, s32[16,32]{1,0:T(8,128)}, u32[]{:S(2)}) copy-start(s32[16,32]{1,0:T(8,128)} %refs_10_.1) | copy-start | bytes 6148
  4.1 0.7 %copy-start.8 = (f32[16,32]{1,0:T(8,128)S(1)}, f32[16,32]{1,0:T(8,128)}, u32[]{:S(2)}) copy-start(f32[16,32]{1,0:T(8,128)} %refs_13_.2) | copy-start | bytes 6148
  4.8 0.7 %copy-start.10 = (s32[8,16]{1,0:T(8,128)S(1)}, s32[8,16]{1,0:T(8,128)}, u32[]{:S(2)}) copy-start(s32[8,16]{1,0:T(8,128)} %refs_11_.1) | copy-start | bytes 1540
  5.5 0.7 %copy-start.11 = (f32[8,16]{1,0:T(8,128)S(1)}, f32[8,16]{1,0:T(8,128)}, u32[]{:S(2)}) copy-start(f32[8,16]{1,0:T(8,128)} %refs_14_.2) | copy-start | bytes 1540
  6.2 10.4 %copy-start.9 = (s32[64,128]{1,0:T(8,128)S(1)}, s32[64,128]{1,0:T(8,128)}, u32[]{:S(2)}) copy-start(s32[64,128]{1,0:T(8,128)} %refs_8_.1) | copy-start | bytes 98308
  6.6 9.9 %collective-permute-start = (f32[19,16,128]{2,1,0:T(8,128)S(1)}, f32[19,16,128]{2,1,0:T(8,128)S(1)}, u32[]{:S(2)}, u32[]{:S(2)}) collective-permute-start(f32[19,16,128]{2,1,0:T(8,128)S(1)} %get-tuple-element.30), channel_id=1, source_target_pairs={{0,4},{4,0},{8,12},{12,8},{16,20},{20,16},{24,28},{28,24},{1,5},{5... | collective-permute-start | bytes 466952 | tf_op jit(solution)/shard_map/ppermute | solution.py:417
  6.7 9.9 %collective-permute-start.1 = (f32[19,16,128]{2,1,0:T(8,128)S(1)}, f32[19,16,128]{2,1,0:T(8,128)S(1)}, u32[]{:S(2)}, u32[]{:S(2)}) collective-permute-start(f32[19,16,128]{2,1,0:T(8,128)S(1)} %get-tuple-element.31), channel_id=1, source_target_pairs={{4,8},{8,4},{12,16},{16,12},{20,24},{24,20},{5,9},{9,5},{13,17},{1... | collective-permute-start | bytes 466952 | tf_op jit(solution)/shard_map/ppermute | solution.py:417
  9.1 5.1 %collective-permute-start.2 = (f32[2,16,128]{2,1,0:T(8,128)S(1)}, f32[2,16,128]{2,1,0:T(8,128)S(1)}, u32[]{:S(2)}, u32[]{:S(2)}) collective-permute-start(f32[2,16,128]{2,1,0:T(8,128)S(1)} %get-tuple-element.32), channel_id=1, source_target_pairs={{0,8},{8,0},{4,12},{12,4},{16,24},{24,16},{20,28},{28,20},{1,9},{9... | collective-permute-start | bytes 49160 | tf_op jit(solution)/shard_map/ppermute | solution.py:417
  10.8 5.8 %copy-start.12 = (f32[8,16]{1,0:T(8,128)S(1)}, f32[8,16]{1,0:T(8,128)}, u32[]{:S(2)}) copy-start(f32[8,16]{1,0:T(8,128)} %refs_14_.2) | copy-start | bytes 1540
  10.8 5.8 %collective-permute-start.3 = (f32[2,16,128]{2,1,0:T(8,128)S(1)}, f32[2,16,128]{2,1,0:T(8,128)S(1)}, u32[]{:S(2)}, u32[]{:S(2)}) collective-permute-start(f32[2,16,128]{2,1,0:T(8,128)S(1)} %get-tuple-element.33), channel_id=1, source_target_pairs={{8,16},{16,8},{12,20},{20,12},{9,17},{17,9},{13,21},{21,13},{10,18... | collective-permute-start | bytes 49160 | tf_op jit(solution)/shard_map/ppermute | solution.py:417
  16.5 11.2 %copy-start.1 = (bf16[4,128,128]{2,1,0:T(8,128)(2,1)S(1)}, bf16[4,128,128]{2,1,0:T(8,128)(2,1)}, u32[]{:S(2)}) copy-start(bf16[4,128,128]{2,1,0:T(8,128)(2,1)} %constant.5.clone.refs_15_) | copy-start | bytes 393220
  16.6 11.1 %copy-start.5 = (f32[64,128]{1,0:T(8,128)S(1)}, f32[64,128]{1,0:T(8,128)}, u32[]{:S(2)}) copy-start(f32[64,128]{1,0:T(8,128)} %refs_13_.3) | copy-start | bytes 98308
  16.6 11.1 %copy-start.6 = (f32[4,16,16]{2,1,0:T(8,128)S(1)}, f32[4,16,16]{2,1,0:T(8,128)}, u32[]{:S(2)}) copy-start(f32[4,16,16]{2,1,0:T(8,128)} %refs_14_.3) | copy-start | bytes 12292
  18.3 5.1 %collective-permute-start.4 = (f32[17,16,128]{2,1,0:T(8,128)S(1)}, f32[17,16,128]{2,1,0:T(8,128)S(1)}, u32[]{:S(2)}, u32[]{:S(2)}) collective-permute-start(f32[17,16,128]{2,1,0:T(8,128)S(1)} %get-tuple-element.45), channel_id=1, source_target_pairs={{0,1},{1,0},{2,3},{3,2},{4,5},{5,4},{6,7},{7,6},{8,9},{9,8},{10,11... | collective-permute-start | bytes 417800 | tf_op jit(solution)/shard_map/ppermute | solution.py:417
  19.9 7.8 %collective-permute-start.5 = (f32[17,16,128]{2,1,0:T(8,128)S(1)}, f32[17,16,128]{2,1,0:T(8,128)S(1)}, u32[]{:S(2)}, u32[]{:S(2)}) collective-permute-start(f32[17,16,128]{2,1,0:T(8,128)S(1)} %get-tuple-element.46), channel_id=1, source_target_pairs={{1,2},{2,1},{5,6},{6,5},{9,10},{10,9},{13,14},{14,13},{17,18},{18,... | collective-permute-start | bytes 417800 | tf_op jit(solution)/shard_map/ppermute | solution.py:417

commit v2 on v1

--- a/solution.py
+++ b/solution.py
@@ -41,14 +41,18 @@
                 current[:, -1] = 0
             low = -1
             down[variant, :, bases[l - 1] : bases[l - 1] + m + 2] = current
+    frames = [0]
+    for l in range(1, LEVELS + 1):
+        own = bases[l - 1] + 1
+        frames.append(own if own + (cols >> l) + H < LANES else H + 1)
     up = np.zeros((LEVELS + 1, LANES, LANES), np.float32)
     for l in range(LEVELS):
         m = cols >> l
         for f in range(-1, m + 1) if l else range(m):
             j = f // 2
-            out = f + H + 1 if l else f
-            up[l, j + H + 1, out] += 0.75
-            up[l, j + (1 if f % 2 else -1) + H + 1, out] += 0.25
+            out, at = f + frames[l], frames[l + 1]
+            up[l, j + at, out] += 0.75
+            up[l, j + (1 if f % 2 else -1) + at, out] += 0.25
     for z in range(16):
         for i in range(8):
             j = i // 2 + 1
@@ -56,7 +60,9 @@
             up[LEVELS, z * 8 + i, (j + (1 if i % 2 else -1)) * 16 + z] += 0.25
     for t in (down, up):
         assert (t == t.astype(jnp.bfloat16).astype(np.float32)).all()
-    return bases, down.astype(jnp.bfloat16), up.astype(jnp.bfloat16)
+    shifts = np.concatenate([np.eye(LANES, k=k) + np.eye(LANES, k=-k) for k in range(1, H + 1)], axis=1)
+    shifts = np.concatenate([shifts, shifts], axis=0)
+    return bases, frames, down.astype(jnp.bfloat16), up.astype(jnp.bfloat16), shifts.astype(jnp.bfloat16)
 
 
 def split(x):
@@ -93,15 +99,23 @@
     return [scale] + [p * scale for p in profile]
 
 
-def prepare(geo, inc, *refs):
-    widths, gains = refs[:LEVELS], refs[LEVELS : 2 * LEVELS]
-    table, field, *rest = refs[2 * LEVELS :]
-    coarse, (send_a, send_b, send_c, send_d, half) = rest[:LEVELS], rest[LEVELS:]
+def prepare(geo, *refs):
+    count = 2 * LEVELS + 2
+    outside, (field, *rest) = refs[:count], refs[count:]
+    coarse, (send_a, send_b, send_c, send_d, half, *inside) = rest[:LEVELS], rest[LEVELS:]
+    sems = inside.pop()
+    copies = [pltpu.make_async_copy(a, b, sems.at[i]) for i, (a, b) in enumerate(zip(outside, inside))]
+    for copy in copies:
+        copy.start()
+    inc, table, *small = inside
+    widths, gains = small[:LEVELS], small[LEVELS:]
     Z, R, M, bases = geo["Z"], geo["R"], geo["M"], geo["bases"]
     e, n = lax.axis_index("east"), lax.axis_index("north")
     has_low, has_high = e > 0, e < geo["E"] - 1
     even = e % 2 == 0
     flat = field.reshape(R * Z, M)
+    for copy in copies:
+        copy.wait()
     for z in range(Z):
         flat[pl.ds(z, R, stride=Z), :] = inc[z]
     variant = (n == 0).astype(jnp.int32) + 2 * (n == geo["N"] - 1).astype(jnp.int32)
@@ -162,10 +176,10 @@
         send_d[i] = jnp.where(forward, lower, upper)
 
 
-def east_rows(source, factors, out, count, block, factor_at=0):
+def east_rows(source, factors, out, count, block, factor_at=0, source_at=0, out_at=0):
     def step(b, carry):
         x0 = b * block
-        rows = [source[x0 + i] for i in range(block + 2 * H)]
+        rows = [source[x0 + i + source_at] for i in range(block + 2 * H)]
         for i in range(block):
             def factor(k):
                 return factors[k, pl.ds(x0 + i + factor_at, 1), :]
@@ -173,7 +187,7 @@
             total = factor(0) * rows[i + H]
             for k in range(1, H + 1):
                 total = total + factor(k) * (rows[i + H + k] + rows[i + H - k])
-            out[x0 + i] = total
+            out[x0 + i + out_at] = total
         return carry
 
     lax.fori_loop(0, count // block, step, 0)
@@ -200,7 +214,7 @@
     full[pl.ds(H, R)] = field[...]
     full[0:H] = jnp.where(even, got_b[0:H], got_a[0:H])
     full[H + R : R + 2 * H] = jnp.where(even, got_a[0:H], got_b[0:H])
-    east_rows(full, factors, eastward, R, 2)
+    east_rows(full, factors, eastward, R, 4)
     for l in range(1, LEVELS + 1):
         r, out, own = R >> l, joined[l - 1], coarse[l - 1]
         out[H : H + r + 2] = own[...]
@@ -224,9 +238,10 @@
     for j, (own, out) in enumerate(zip((*widths, *gains), (*wide, *gain))):
         r, m = own.shape
         out[...] = jnp.zeros(out.shape, F32)
-        out[pl.ds(H, r), pl.ds(H + 1, m)] = own[...].astype(F32)
-        out[pl.ds(H - 1, 1), pl.ds(H + 1, m)] = lower[j : j + 1, 0:m]
-        out[pl.ds(H + r, 1), pl.ds(H + 1, m)] = upper[j : j + 1, 0:m]
+        at = geo["frames"][j % LEVELS + 1]
+        out[pl.ds(H, r), pl.ds(at, m)] = own[...].astype(F32)
+        out[pl.ds(H - 1, 1), pl.ds(at, m)] = lower[j : j + 1, 0:m]
+        out[pl.ds(H + r, 1), pl.ds(at, m)] = upper[j : j + 1, 0:m]
     north_even = n % 2 == 0
     lane = lanes_of(Z)
 
@@ -248,10 +263,10 @@
     for t in range(R // per):
         low_side, high_side = zero, zero
         for s in range(per):
-            row = eastward[t * per + s]
-            here = (lane >= H * s) & (lane < H * (s + 1))
-            low_side = jnp.where(here, roll(row, H * s), low_side)
-            high_side = jnp.where(here, roll(row, H * s - M + H), high_side)
+            row, at = eastward[t * per + s], 2 * H * (s % H) + H * (s // H)
+            here = (lane >= at) & (lane < at + H)
+            low_side = jnp.where(here, roll(row, at), low_side)
+            high_side = jnp.where(here, roll(row, at - M + H), high_side)
         send(geo["coarse_tiles"] + t, low_side, high_side)
     base = geo["coarse_tiles"] + R // per
     for t in range(wide[0].shape[0] // Z):
@@ -265,8 +280,9 @@
             if have < Z:
                 part = jnp.concatenate([part, jnp.zeros((Z - have, LANES), F32)], axis=0)
             here = (lane >= 16 * j) & (lane < 16 * j + H + 1)
-            low_side = jnp.where(here, roll(part, 16 * j - H - 1), low_side)
-            high_side = jnp.where(here, roll(part, 16 * j - m), high_side)
+            at = geo["frames"][j % LEVELS + 1]
+            low_side = jnp.where(here, roll(part, 16 * j - at), low_side)
+            high_side = jnp.where(here, roll(part, 16 * j - at - m + H + 1), high_side)
         send(base + t, low_side, high_side)
 
 
@@ -290,122 +306,137 @@
 
 
 def finish(geo, *refs):
-    Z, R, M, bases = geo["Z"], geo["R"], geo["M"], geo["bases"]
+    Z, R, M, bases, frames = geo["Z"], geo["R"], geo["M"], geo["bases"], geo["frames"]
     it = iter(refs)
     take = lambda count: [next(it) for _ in range(count)]
     eastward, factors = take(2)
     joined = take(LEVELS)
     wide, gain = take(LEVELS), take(LEVELS)
-    got_x, got_y, gain0, vertical, table = take(5)
+    got_x, got_y, gain0, widths0, vertical, table, shifts = take(7)
     (out,) = take(1)
-    got_low, got_high, ext, coarse_factors, passed, north, result, spread, wf, gf = take(10)
+    got_low, got_high, ext, passed, north, result, spread, wf, gf, cf, north0, edge = take(12)
     e, n = lax.axis_index("east"), lax.axis_index("north")
     has_low, has_high = e > 0, e < geo["E"] - 1
     north_even = n % 2 == 0
     got_low[...] = jnp.where(north_even, got_y[...], got_x[...])
     got_high[...] = jnp.where(north_even, got_x[...], got_y[...])
     lane = lanes_of(Z)
+    lane8 = lanes_of(8)
     per = LANES // H
     base = geo["coarse_tiles"] + R // per
-    first = 0
-    starts = []
+    levels = range(1, LEVELS + 1)
+    rows_of = [R >> l for l in levels]
+    starts = lambda more: [sum(rows_of[:l]) + l * more for l in range(LEVELS + 1)]
+    ext_at = starts(2 * H + 2)
+    out_at = starts(2)
+    width_at = starts(2 * H)
     for l in range(LEVELS):
-        starts.append(first)
-        first += joined[l].shape[0]
-    previous = None
+        r, m, at = R >> (l + 1), M >> (l + 1), frames[l + 1]
+        for source, target, j in ((wide[l], wf, l), (gain[l], gf, LEVELS + l)):
+            for c in range(0, r + 2 * H, 8):
+                t, row = base + c // Z, c % Z
+                low_side = roll(got_low[t, row : row + 8, :], at - H - 1 - 16 * j)
+                high_side = roll(got_high[t, row : row + 8, :], at + m - 16 * j)
+                joint = jnp.where(lane8 < at, low_side, jnp.where(lane8 < at + m, source[pl.ds(c, 8), :], high_side))
+                target[pl.ds(width_at[l] + c, 8), :] = jnp.where((lane8 >= at - H - 1) & (lane8 < at + m + H + 1), joint, 0.0)
+        for i in range(r + 2 * H + 2):
+            t, s = divmod(ext_at[l] + i, PER_TILE)
+            own = roll(joined[l][i], at - 1 - bases[l])
+            low_side = roll(got_low[t], at - H - 1 - SLOT * s)
+            high_side = roll(got_high[t], at + m - 1 - SLOT * s)
+            ext[ext_at[l] + i] = (
+                jnp.where((lane >= at - 1) & (lane < at + m + 1), own, 0.0)
+                + jnp.where((lane >= at - H - 1) & (lane < at + 1), low_side, 0.0)
+                + jnp.where((lane >= at + m - 1) & (lane < at + m + H + 1), high_side, 0.0)
+            )
+    for k, a in enumerate(taps(wf[...])):
+        cf[k] = a
+    for l in range(LEVELS):
+        r = R >> (l + 1)
+        east_rows(ext, cf, passed, r + 2, 2, width_at[l] + H - 1, ext_at[l], out_at[l])
+
+    def north_rows(source, target, rows, factor):
+        data = source[pl.ds(rows[0], len(rows))].reshape(len(rows) * Z, LANES)
+        pair = jnp.concatenate(split(data), axis=1)
+        for k in range(1, H + 1, 2):
+            moved = mm(pair, shifts[:, (k - 1) * LANES : (k + 1) * LANES])
+            for i, x in enumerate(rows):
+                here = moved[i * Z : (i + 1) * Z]
+                before = factor(0, x) * source[x] if k == 1 else target[x]
+                target[x] = before + factor(k, x) * here[:, :LANES] + factor(k + 1, x) * here[:, LANES:]
+
+    total = out_at[-1]
+
+    def coarse_factor(k, x):
+        l = max(i for i in range(LEVELS) if out_at[i] <= x)
+        return cf[k, pl.ds(width_at[l] + H - 1 + x - out_at[l], 1), :]
+
+    half = -(-total // 2)
+    north_rows(passed, north, range(0, half), coarse_factor)
+    north_rows(passed, north, range(half, total), coarse_factor)
     for l in range(LEVELS - 1, -1, -1):
-        r, m = R >> (l + 1), M >> (l + 1)
-        rows = r + 2 * H + 2
-        count = wide[l].shape[0]
-        for source, target, j in ((wide[l], wf, l), (gain[l], gf, LEVELS + l)):
-            for c in range(0, count, 8):
-                t, at = base + c // Z, c % Z
-                lane8 = lanes_of(8)
-                low_side = roll(got_low[t, at : at + 8, :], -16 * j)
-                high_side = roll(got_high[t, at : at + 8, :], m + H + 1 - 16 * j)
-                own = source[pl.ds(c, 8), :]
-                target[pl.ds(c, 8), :] = jnp.where(
-                    lane8 < H + 1, low_side, jnp.where(lane8 < m + H + 1, own, jnp.where(lane8 < m + 2 * H + 2, high_side, 0.0))
-                )
-        for k, a in enumerate(taps(wf[pl.ds(0, count), :])):
-            coarse_factors[k, pl.ds(0, count), :] = a
-        for i in range(rows):
-            t, s = divmod(starts[l] + i, PER_TILE)
-            own = roll(joined[l][i], H - bases[l])
-            low_side = roll(got_low[t], -SLOT * s)
-            high_side = roll(got_high[t], m + H - SLOT * s)
-            ext[i] = (
-                jnp.where((lane >= H) & (lane < m + H + 2), own, 0.0)
-                + jnp.where(lane < SLOT, low_side, 0.0)
-                + jnp.where((lane >= m + H) & (lane < m + H + SLOT), high_side, 0.0)
-            )
-        east_rows(ext, coarse_factors, passed, r + 2, 2, H - 1)
-
-        def step(b, carry):
-            for i in range(2):
-                x = 2 * b + i
-                value = passed[x]
-                total = coarse_factors[0, pl.ds(x + H - 1, 1), :] * value
-                for k in range(1, H + 1):
-                    total = total + coarse_factors[k, pl.ds(x + H - 1, 1), :] * (roll(value, -k) + roll(value, k))
-                north[x] = total
-            return carry
-
-        lax.fori_loop(0, (r + 2) // 2, step, 0)
+        r, m, at = R >> (l + 1), M >> (l + 1), frames[l + 1]
         groups = (r + 2 + 7) // 8
-        north[r + 2 : groups * 8] = jnp.zeros((groups * 8 - r - 2, Z, LANES), F32)
         matrix = kron(vertical[l + 1] * 4.0 ** (l + 1), False)
         for g in range(groups):
-            mixed = mix(matrix, north[8 * g : 8 * g + 8].reshape(8 * Z, LANES))
-            for i in range(8):
+            have = min(8, r + 2 - 8 * g)
+            data = north[out_at[l] + 8 * g : out_at[l] + 8 * g + have].reshape(have * Z, LANES)
+            if have < 8:
+                data = jnp.concatenate([data, jnp.zeros(((8 - have) * Z, LANES), F32)], axis=0)
+            mixed = mix(matrix, data)
+            for i in range(have):
                 row = 8 * g + i
-                if row < r + 2:
-                    result[row] = gf[pl.ds(row + H - 1, 1), :] * mixed[i * Z : (i + 1) * Z]
-        if previous is not None:
-            inside = ((lane > H) | (n > 0)) & ((lane < m + H + 1) | (n < geo["N"] - 1))
+                result[row] = gf[pl.ds(width_at[l] + row + H - 1, 1), :] * mixed[i * Z : (i + 1) * Z]
+        if l < LEVELS - 1:
+            inside = ((lane >= at) | (n > 0)) & ((lane < at + m) | (n < geo["N"] - 1))
             for row in range(-1, r + 1):
                 j = row // 2
                 other = j + (1 if row % 2 else -1)
-                total = result[row + 1] + 0.75 * spread[j + 1] + 0.25 * spread[other + 1]
+                summed = result[row + 1] + 0.75 * spread[j + 1] + 0.25 * spread[other + 1]
                 keep = inside
                 if row == -1:
                     keep = keep & has_low
                 if row == r:
                     keep = keep & has_high
-                result[row + 1] = jnp.where(keep, total, 0.0)
+                result[row + 1] = jnp.where(keep, summed, 0.0)
         flat = result.reshape(result.shape[0] * Z, LANES)
         spread_flat = spread.reshape(spread.shape[0] * Z, LANES)
-        weights = table[l]
-        spread_flat[pl.ds(0, (r + 2) * Z), :] = dot_exact(flat[pl.ds(0, (r + 2) * Z), :], weights)
-        previous = True
+        spread_flat[pl.ds(0, (r + 2) * Z), :] = dot_exact(flat[pl.ds(0, (r + 2) * Z), :], table[l])
+    slot = lane8 % (2 * H)
+    width = jnp.zeros((H, LANES), F32)
+    for s in range(H):
+        rows = widths0[pl.ds(s, R // H, stride=H), :].astype(F32)
+        width = jnp.where(lane8 // (2 * H) == s, roll(rows, 2 * H * s + H), width)
+    edge_taps = [jnp.where((slot >= H - k) & (slot < H + k), a, 0.0) for k, a in enumerate(taps(width))]
+    low_half = lane % (2 * H) < H
+    for t in range(R // H):
+        tile = geo["coarse_tiles"] + t // 2
+        low_side, high_side = got_low[tile], got_high[tile]
+        if t % 2:
+            low_side = roll(low_side, -H)
+        else:
+            high_side = roll(high_side, H)
+        halo = jnp.where(low_half, low_side, high_side)
+        summed = jnp.zeros((Z, LANES), F32)
+        for k in range(1, H + 1):
+            summed = summed + edge_taps[k][t : t + 1] * jnp.where(low_half, roll(halo, -k), roll(halo, k))
+        edge[t] = summed
     matrix = kron(vertical[0], True)
     widen = table[LEVELS][:, 0 : 6 * Z]
-
-    def block(b, carry):
-        t = geo["coarse_tiles"] + b // 2
+    factor0 = lambda k, x: factors[k, pl.ds(x, 1), :]
+    for x0 in range(0, R, R // 2):
+        north_rows(eastward, north0, range(x0, x0 + R // 2), factor0)
+    at_edge = (lane < H) | (lane >= M - H)
+    for b in range(R // 8):
         for i in range(8):
             x = 8 * b + i
-            value = eastward[x]
-            s = (b % 2) * 8 + i
-            low_side = pltpu.roll(got_low[t], (2 * LANES - H - H * s) % LANES, 1)
-            high_side = pltpu.roll(got_high[t], (2 * LANES - H * s) % LANES, 1)
-            halo = jnp.where(lane < LANES // 2, high_side, low_side)
-            total = factors[0, pl.ds(x, 1), :] * value
-            for k in range(1, H + 1):
-                ahead = roll(jnp.where(lane < k, halo, value), -k)
-                behind = roll(jnp.where(lane >= LANES - k, halo, value), k)
-                total = total + factors[k, pl.ds(x, 1), :] * (ahead + behind)
-            north[i] = total
-        mixed = mix(matrix, north[0:8].reshape(8 * Z, LANES))
-        coarse = spread[pl.ds(4 * b, 6)].reshape(6 * Z, LANES)
-        high, low = split(coarse)
+            north0[x] = north0[x] + jnp.where(at_edge, roll(edge[b], M - H - 2 * H * i), 0.0)
+        mixed = mix(matrix, north0[8 * b : 8 * b + 8].reshape(8 * Z, LANES))
+        high, low = split(spread[4 * b : 4 * b + 6].reshape(6 * Z, LANES))
         added = mm(widen, high) + mm(widen, low)
-        weight = gain0[pl.ds(pl.multiple_of(8 * b, 8), 8), :]
+        weight = gain0[pl.ds(8 * b, 8), :]
         for z in range(Z):
-            out[z, pl.ds(pl.multiple_of(8 * b, 8), 8), :] = weight * mixed[z * 8 : z * 8 + 8] + added[z * 8 : z * 8 + 8]
-        return carry
-
-    lax.fori_loop(0, R // 8, block, 0)
+            out[z, pl.ds(8 * b, 8), :] = weight * mixed[z * 8 : z * 8 + 8] + added[z * 8 : z * 8 + 8]
 
 
 def swap(x, axis, first, by=1):
@@ -419,23 +450,26 @@
 
 def body(inc, w0, w1, w2, w3, g0, g1, g2, g3, vertical):
     Z, R, M = inc.shape
-    bases, down, up = tables(R, M)
+    bases, frames, down, up, shifts = tables(R, M)
     total_rows = sum((R >> l) + 2 * H + 2 for l in range(1, LEVELS + 1))
     geo = dict(
-        Z=Z, R=R, M=M, bases=bases, E=lax.axis_size("east"), N=lax.axis_size("north"),
+        Z=Z, R=R, M=M, bases=bases, frames=frames, E=lax.axis_size("east"), N=lax.axis_size("north"),
         coarse_tiles=-(-total_rows // PER_TILE),
     )
     shape = lambda *dims: jax.ShapeDtypeStruct(dims, F32)
     levels = range(1, LEVELS + 1)
     params = pltpu.CompilerParams(vmem_limit_bytes=48 * 1024 * 1024)
     east_tiles = H + SLOT + 1
+    given = (inc, jnp.asarray(down), w1, w2, w3, g1, g2, g3)
     outs = pl.pallas_call(
         functools.partial(prepare, geo),
         out_shape=[shape(R, Z, M)] + [shape((R >> l) + 2, Z, M) for l in levels]
         + [shape(east_tiles, Z, M)] * 2 + [shape(2, Z, M)] * 2,
-        scratch_shapes=[pltpu.VMEM((R, Z, M), F32)],
+        in_specs=[pl.BlockSpec(memory_space=pl.ANY)] * len(given),
+        scratch_shapes=[pltpu.VMEM((R, Z, M), F32)] + [pltpu.VMEM(x.shape, x.dtype) for x in given]
+        + [pltpu.SemaphoreType.DMA((len(given),))],
         compiler_params=params,
-    )(inc, w1, w2, w3, g1, g2, g3, jnp.asarray(down))
+    )(*given)
     field, coarse, sends = outs[0], outs[1 : 1 + LEVELS], outs[1 + LEVELS :]
     got_b = swap(sends[1], "east", 1)
     got_a = swap(sends[0], "east", 0)
@@ -457,24 +491,21 @@
     got_x = swap(send_x, "north", 0)
     got_y = swap(send_y, "north", 1)
     rows1 = (R >> 1) + 2
-    padded = -(-rows1 // 8) * 8
+    out_rows = sum((R >> l) + 2 for l in levels)
+    width_rows = out_rows + LEVELS * (2 * H - 2)
     return pl.pallas_call(
         functools.partial(finish, geo),
         out_shape=shape(Z, R, M),
         scratch_shapes=[
-            pltpu.VMEM((north_tiles, Z, M), F32),
-            pltpu.VMEM((north_tiles, Z, M), F32),
-            pltpu.VMEM((rows1 + 2 * H, Z, M), F32),
-            pltpu.VMEM((H + 1, wide_shapes[0].shape[0], M), F32),
-            pltpu.VMEM((rows1, Z, M), F32),
-            pltpu.VMEM((padded, Z, M), F32),
-            pltpu.VMEM((rows1, Z, M), F32),
-            pltpu.VMEM((rows1, Z, M), F32),
-            pltpu.VMEM(wide_shapes[0].shape, F32),
-            pltpu.VMEM(wide_shapes[0].shape, F32),
+            pltpu.VMEM(dims, F32)
+            for dims in (
+                (north_tiles, Z, M), (north_tiles, Z, M), (total_rows, Z, M), (out_rows, Z, M), (out_rows, Z, M),
+                (rows1, Z, M), (rows1, Z, M), (width_rows, M), (width_rows, M), (H + 1, width_rows, M),
+                (R, Z, M), (R // H, Z, M),
+            )
         ],
         compiler_params=params,
-    )(eastward, factors, *joined, *wide, *gain, got_x, got_y, g0, vertical, jnp.asarray(up))
+    )(eastward, factors, *joined, *wide, *gain, got_x, got_y, g0, w0, vertical, jnp.asarray(up), jnp.asarray(shifts))
 
 
 def solution(mesh):

time: 41.3 us -> 34 us (0.82)
  Pallas kernels: 15.1 us -> 7.85 us
    pallas_call x1, Pallas kernels: 13 us -> 5.46 us  [body(): pl.pallas_call(functools.partial(finish, geo), out_shape=shape(Z, R, M),...]
    unnamed x26 -> x28, local copies, waits for them, and re-layouts: 6.17 us -> 6.18 us
where the time goes in v2:
time: 34 us; the launch traced here: 33.4 us
  starting transfers between devices  10.1 us (30%)
  waiting for transfers between devices  9.17 us (27%)
  Pallas kernels  7.85 us (23%)
  local copies, waits for them, and re-layouts  6.18 us (18%)
    ppermute x6, starting transfers between devices, swap(): return lax.ppermute(x, axis, route)  10.1 us
    ppermute x6, waiting for transfers between devices, swap(): return lax.ppermute(x, axis, route)  9.17 us
    unnamed x28, local copies, waits for them, and re-layouts  6.18 us
    pallas_call x1, Pallas kernels, body(): pl.pallas_call(functools.partial(finish, geo), out_shape=shape(Z, R, M),...  5.46 us
    pallas_call x1, Pallas kernels, body(): pl.pallas_call(functools.partial(middle, geo), out_shape=[shape(R, Z, M),...  1.59 us
    pallas_call x1, Pallas kernels, body(): pl.pallas_call(functools.partial(prepare, geo), out_shape=[shape(R, Z, M)...  0.8 us
  transfers between devices with their start and end apart: 6, of which 4 were waited for; matrix products, arithmetic and copies ran while one was open for 0% of the time, Pallas kernels for 0%

profile of v2, /device:TPU:20, one launch (start us, length us, event | category | flops | bytes accessed | tf_op | source)
XLA Modules:
  0.0 33.4 jit_solution(12884312044352584051)
XLA Ops:
  0.0 0.0 copy-start.1
  0.0 1.0 %copy-done.1 = f32[16,64,128]{2,1,0:T(8,128)S(1)} copy-done((f32[16,64,128]{2,1,0:T(8,128)S(1)}, f32[16,64,128]{2,1,0:T(8,128)}, u32[]{:S(2)}) %copy-start.1) | copy-done | bytes 524312
  1.0 0.0 copy-start.4
  1.0 0.9 %copy-done.4 = bf16[4,128,128]{2,1,0:T(8,128)(2,1)S(1)} copy-done((bf16[4,128,128]{2,1,0:T(8,128)(2,1)S(1)}, bf16[4,128,128]{2,1,0:T(8,128)(2,1)}, u32[]{:S(2)}) %copy-start.4) | copy-done | bytes 131096
  1.9 0.0 copy-start.5
  1.9 0.7 %copy-done.5 = s32[32,64]{1,0:T(8,128)S(1)} copy-done((s32[32,64]{1,0:T(8,128)S(1)}, s32[32,64]{1,0:T(8,128)}, u32[]{:S(2)}) %copy-start.5) | copy-done | bytes 8216
  2.7 0.0 copy-start.6
  2.7 0.7 %copy-done.6 = f32[32,64]{1,0:T(8,128)S(1)} copy-done((f32[32,64]{1,0:T(8,128)S(1)}, f32[32,64]{1,0:T(8,128)}, u32[]{:S(2)}) %copy-start.6) | copy-done | bytes 8216
  3.4 0.0 copy-start.9
  3.4 0.7 %copy-done.9 = s32[16,32]{1,0:T(8,128)S(1)} copy-done((s32[16,32]{1,0:T(8,128)S(1)}, s32[16,32]{1,0:T(8,128)}, u32[]{:S(2)}) %copy-start.9) | copy-done | bytes 2072
  4.1 0.0 copy-start.10
  4.1 0.7 %copy-done.10 = f32[16,32]{1,0:T(8,128)S(1)} copy-done((f32[16,32]{1,0:T(8,128)S(1)}, f32[16,32]{1,0:T(8,128)}, u32[]{:S(2)}) %copy-start.10) | copy-done | bytes 2072
  4.8 0.0 copy-start.11
  4.8 0.7 %copy-done.11 = s32[8,16]{1,0:T(8,128)S(1)} copy-done((s32[8,16]{1,0:T(8,128)S(1)}, s32[8,16]{1,0:T(8,128)}, u32[]{:S(2)}) %copy-start.11) | copy-done | bytes 536
  5.5 0.0 copy-start.12
  5.5 0.7 %copy-done.12 = f32[8,16]{1,0:T(8,128)S(1)} copy-done((f32[8,16]{1,0:T(8,128)S(1)}, f32[8,16]{1,0:T(8,128)}, u32[]{:S(2)}) %copy-start.12) | copy-done | bytes 536
  6.2 0.0 copy-start.2
  6.2 0.8 %shard_map.127 = (f32[64,16,128]{2,1,0:T(8,128)S(1)}, f32[34,16,128]{2,1,0:T(8,128)S(1)}, f32[18,16,128]{2,1,0:T(8,128)S(1)}, f32[10,16,128]{2,1,0:T(8,128)S(1)}...) custom-call(f32[16,64,128]{2,1,0:T(8,128)S(1)} %copy-done.1, ...), custom_call_target="tpu_custom_call" | custom-call | tf_op jit(solution)/shard_map/pallas_call | solution.py:464
  7.0 0.1 collective-permute-start
  7.0 2.5 %collective-permute-start.1 = (f32[19,16,128]{2,1,0:T(8,128)S(1)}, f32[19,16,128]{2,1,0:T(8,128)S(1)}, u32[]{:S(2)}, u32[]{:S(2)}) collective-permute-start(f32[19,16,128]{2,1,0:T(8,128)S(1)} %get-tuple-element.31), channel_id=1, source_target_pairs={{4,8},{8,4},{12,16},{16,12},{20,24},{24,20},{5,9},{9,5},{13,17},{1... | collective-permute-start | bytes 466952 | tf_op jit(solution)/shard_map/ppermute | solution.py:448
  9.5 1.6 %collective-permute-start.2 = (f32[2,16,128]{2,1,0:T(8,128)S(1)}, f32[2,16,128]{2,1,0:T(8,128)S(1)}, u32[]{:S(2)}, u32[]{:S(2)}) collective-permute-start(f32[2,16,128]{2,1,0:T(8,128)S(1)} %get-tuple-element.32), channel_id=1, source_target_pairs={{0,8},{8,0},{4,12},{12,4},{16,24},{24,16},{20,28},{28,20},{1,9},{9... | collective-permute-start | bytes 49160 | tf_op jit(solution)/shard_map/ppermute | solution.py:448
  11.1 0.0 copy-start.13
  11.1 2.0 %collective-permute-start.3 = (f32[2,16,128]{2,1,0:T(8,128)S(1)}, f32[2,16,128]{2,1,0:T(8,128)S(1)}, u32[]{:S(2)}, u32[]{:S(2)}) collective-permute-start(f32[2,16,128]{2,1,0:T(8,128)S(1)} %get-tuple-element.33), channel_id=1, source_target_pairs={{8,16},{16,8},{12,20},{20,12},{9,17},{17,9},{13,21},{21,13},{10,18... | collective-permute-start | bytes 49160 | tf_op jit(solution)/shard_map/ppermute | solution.py:448
  13.2 1.4 %collective-permute-done.2.refs_6_ = f32[2,16,128]{2,1,0:T(8,128)S(1)} collective-permute-done((f32[2,16,128]{2,1,0:T(8,128)S(1)}, f32[2,16,128]{2,1,0:T(8,128)S(1)}, u32[]{:S(2)}, u32[]{:S(2)}) %collective-permute-start.2) | collective-permute-done | bytes 16416 | tf_op jit(solution)/shard_map/ppermute | solution.py:448
  14.6 2.3 %collective-permute-done.3.refs_7_ = f32[2,16,128]{2,1,0:T(8,128)S(1)} collective-permute-done((f32[2,16,128]{2,1,0:T(8,128)S(1)}, f32[2,16,128]{2,1,0:T(8,128)S(1)}, u32[]{:S(2)}, u32[]{:S(2)}) %collective-permute-start.3) | collective-permute-done | bytes 16416 | tf_op jit(solution)/shard_map/ppermute | solution.py:448
  16.9 0.0 collective-permute-done.refs_4_
  16.9 0.0 collective-permute-done.1.refs_5_
  16.9 0.0 copy-done.2
  16.9 0.0 copy-done.13
  16.9 0.0 copy-start
  16.9 0.0 copy-start.3
  16.9 0.0 copy-start.7
  17.0 0.0 copy-start.8
  17.0 1.6 %shard_map.128 = (f32[64,16,128]{2,1,0:T(8,128)S(1)}, f32[9,64,128]{2,1,0:T(8,128)S(1)}, f32[50,16,128]{2,1,0:T(8,128)S(1)}, f32[34,16,128]{2,1,0:T(8,128)S(1)},...) custom-call(f32[64,16,128]{2,1,0:T(8,128)S(1)} %get-tuple-element.26, ...), custom_call_target="tpu_custom_call" | custom-call | tf_op jit(solution)/shard_map/pallas_call | solution.py:480
  18.6 1.6 %collective-permute-start.4 = (f32[17,16,128]{2,1,0:T(8,128)S(1)}, f32[17,16,128]{2,1,0:T(8,128)S(1)}, u32[]{:S(2)}, u32[]{:S(2)}) collective-permute-start(f32[17,16,128]{2,1,0:T(8,128)S(1)} %get-tuple-element.45), channel_id=1, source_target_pairs={{0,1},{1,0},{2,3},{3,2},{4,5},{5,4},{6,7},{7,6},{8,9},{9,8},{10,11... | collective-permute-start | bytes 417800 | tf_op jit(solution)/shard_map/ppermute | solution.py:448
  20.1 2.4 %collective-permute-start.5 = (f32[17,16,128]{2,1,0:T(8,128)S(1)}, f32[17,16,128]{2,1,0:T(8,128)S(1)}, u32[]{:S(2)}, u32[]{:S(2)}) collective-permute-start(f32[17,16,128]{2,1,0:T(8,128)S(1)} %get-tuple-element.46), channel_id=1, source_target_pairs={{1,2},{2,1},{5,6},{6,5},{9,10},{10,9},{13,14},{14,13},{17,18},{18,... | collective-permute-start | bytes 417800 | tf_op jit(solution)/shard_map/ppermute | solution.py:448
  22.5 1.2 %collective-permute-done.4.refs_11_ = f32[17,16,128]{2,1,0:T(8,128)S(1)} collective-permute-done((f32[17,16,128]{2,1,0:T(8,128)S(1)}, f32[17,16,128]{2,1,0:T(8,128)S(1)}, u32[]{:S(2)}, u32[]{:S(2)}) %collective-permute-start.4) | collective-permute-done | bytes 139296 | tf_op jit(solution)/shard_map/ppermute | solution.py:448
  23.7 4.3 %collective-permute-done.5.refs_12_ = f32[17,16,128]{2,1,0:T(8,128)S(1)} collective-permute-done((f32[17,16,128]{2,1,0:T(8,128)S(1)}, f32[17,16,128]{2,1,0:T(8,128)S(1)}, u32[]{:S(2)}, u32[]{:S(2)}) %collective-permute-start.5) | collective-permute-done | bytes 139296 | tf_op jit(solution)/shard_map/ppermute | solution.py:448
  28.0 0.0 copy-done
  28.0 0.0 copy-done.3
  28.0 0.0 copy-done.7
  28.0 0.0 copy-done.8
  28.0 5.5 %shard_map.129 = f32[16,64,128]{2,1,0:T(8,128)} custom-call(f32[64,16,128]{2,1,0:T(8,128)S(1)} %get-tuple-element.34.refs_0_, f32[9,64,128]{2,1,0:T(8,128)S(1)} %get-tuple-element.35.refs_1_, f32[50,16,128]{2,1,0:T(8,128)S(1)} %get-tuple-element.36.refs_2_, f32[34,16,128]{2,1,0:T(8,128)S(1)} %get-tuple-element.37.refs_3_, ...), custom_call_target="tpu_custom_call" | custom-call | tf_op jit(solution)/shard_map/pallas_call | solution.py:496
Async XLA Ops:
  0.0 1.0 %copy-start.1 = (f32[16,64,128]{2,1,0:T(8,128)S(1)}, f32[16,64,128]{2,1,0:T(8,128)}, u32[]{:S(2)}) copy-start(f32[16,64,128]{2,1,0:T(8,128)} %refs_0_.1) | copy-start | bytes 1572868
  1.0 0.9 %copy-start.4 = (bf16[4,128,128]{2,1,0:T(8,128)(2,1)S(1)}, bf16[4,128,128]{2,1,0:T(8,128)(2,1)}, u32[]{:S(2)}) copy-start(bf16[4,128,128]{2,1,0:T(8,128)(2,1)} %constant.6.clone.refs_1_) | copy-start | bytes 393220
  1.9 0.7 %copy-start.5 = (s32[32,64]{1,0:T(8,128)S(1)}, s32[32,64]{1,0:T(8,128)}, u32[]{:S(2)}) copy-start(s32[32,64]{1,0:T(8,128)} %refs_9_.1) | copy-start | bytes 24580
  2.7 0.7 %copy-start.6 = (f32[32,64]{1,0:T(8,128)S(1)}, f32[32,64]{1,0:T(8,128)}, u32[]{:S(2)}) copy-start(f32[32,64]{1,0:T(8,128)} %refs_12_.1) | copy-start | bytes 24580
  3.4 0.7 %copy-start.9 = (s32[16,32]{1,0:T(8,128)S(1)}, s32[16,32]{1,0:T(8,128)}, u32[]{:S(2)}) copy-start(s32[16,32]{1,0:T(8,128)} %refs_10_.1) | copy-start | bytes 6148
  4.1 0.7 %copy-start.10 = (f32[16,32]{1,0:T(8,128)S(1)}, f32[16,32]{1,0:T(8,128)}, u32[]{:S(2)}) copy-start(f32[16,32]{1,0:T(8,128)} %refs_13_.2) | copy-start | bytes 6148
  4.8 0.7 %copy-start.11 = (s32[8,16]{1,0:T(8,128)S(1)}, s32[8,16]{1,0:T(8,128)}, u32[]{:S(2)}) copy-start(s32[8,16]{1,0:T(8,128)} %refs_11_.1) | copy-start | bytes 1540
  5.5 0.7 %copy-start.12 = (f32[8,16]{1,0:T(8,128)S(1)}, f32[8,16]{1,0:T(8,128)}, u32[]{:S(2)}) copy-start(f32[8,16]{1,0:T(8,128)} %refs_14_.2) | copy-start | bytes 1540
  6.2 10.8 %copy-start.2 = (s32[64,128]{1,0:T(8,128)S(1)}, s32[64,128]{1,0:T(8,128)}, u32[]{:S(2)}) copy-start(s32[64,128]{1,0:T(8,128)} %refs_14_.3) | copy-start | bytes 98308
  7.0 9.9 %collective-permute-start = (f32[19,16,128]{2,1,0:T(8,128)S(1)}, f32[19,16,128]{2,1,0:T(8,128)S(1)}, u32[]{:S(2)}, u32[]{:S(2)}) collective-permute-start(f32[19,16,128]{2,1,0:T(8,128)S(1)} %get-tuple-element.30), channel_id=1, source_target_pairs={{0,4},{4,0},{8,12},{12,8},{16,20},{20,16},{24,28},{28,24},{1,5},{5... | collective-permute-start | bytes 466952 | tf_op jit(solution)/shard_map/ppermute | solution.py:448
  7.0 9.9 %collective-permute-start.1 = (f32[19,16,128]{2,1,0:T(8,128)S(1)}, f32[19,16,128]{2,1,0:T(8,128)S(1)}, u32[]{:S(2)}, u32[]{:S(2)}) collective-permute-start(f32[19,16,128]{2,1,0:T(8,128)S(1)} %get-tuple-element.31), channel_id=1, source_target_pairs={{4,8},{8,4},{12,16},{16,12},{20,24},{24,20},{5,9},{9,5},{13,17},{1... | collective-permute-start | bytes 466952 | tf_op jit(solution)/shard_map/ppermute | solution.py:448
  9.5 5.1 %collective-permute-start.2 = (f32[2,16,128]{2,1,0:T(8,128)S(1)}, f32[2,16,128]{2,1,0:T(8,128)S(1)}, u32[]{:S(2)}, u32[]{:S(2)}) collective-permute-start(f32[2,16,128]{2,1,0:T(8,128)S(1)} %get-tuple-element.32), channel_id=1, source_target_pairs={{0,8},{8,0},{4,12},{12,4},{16,24},{24,16},{20,28},{28,20},{1,9},{9... | collective-permute-start | bytes 49160 | tf_op jit(solution)/shard_map/ppermute | solution.py:448
  11.1 5.8 %copy-start.13 = (f32[8,16]{1,0:T(8,128)S(1)}, f32[8,16]{1,0:T(8,128)}, u32[]{:S(2)}) copy-start(f32[8,16]{1,0:T(8,128)} %refs_14_.2) | copy-start | bytes 1540
  11.1 5.8 %collective-permute-start.3 = (f32[2,16,128]{2,1,0:T(8,128)S(1)}, f32[2,16,128]{2,1,0:T(8,128)S(1)}, u32[]{:S(2)}, u32[]{:S(2)}) collective-permute-start(f32[2,16,128]{2,1,0:T(8,128)S(1)} %get-tuple-element.33), channel_id=1, source_target_pairs={{8,16},{16,8},{12,20},{20,12},{9,17},{17,9},{13,21},{21,13},{10,18... | collective-permute-start | bytes 49160 | tf_op jit(solution)/shard_map/ppermute | solution.py:448
  16.9 11.0 %copy-start = (bf16[256,1024]{1,0:T(8,128)(2,1)S(1)}, bf16[256,1024]{1,0:T(8,128)(2,1)}, u32[]{:S(2)}) copy-start(bf16[256,1024]{1,0:T(8,128)(2,1)} %constant.8.clone.refs_17_) | copy-start | bytes 1572868
  16.9 11.0 %copy-start.3 = (bf16[4,128,128]{2,1,0:T(8,128)(2,1)S(1)}, bf16[4,128,128]{2,1,0:T(8,128)(2,1)}, u32[]{:S(2)}) copy-start(bf16[4,128,128]{2,1,0:T(8,128)(2,1)} %constant.7.clone.refs_16_) | copy-start | bytes 393220
  16.9 11.0 %copy-start.7 = (f32[64,128]{1,0:T(8,128)S(1)}, f32[64,128]{1,0:T(8,128)}, u32[]{:S(2)}) copy-start(f32[64,128]{1,0:T(8,128)} %refs_13_.3) | copy-start | bytes 98308
  17.0 11.0 %copy-start.8 = (f32[4,16,16]{2,1,0:T(8,128)S(1)}, f32[4,16,16]{2,1,0:T(8,128)}, u32[]{:S(2)}) copy-start(f32[4,16,16]{2,1,0:T(8,128)} %refs_15_.1) | copy-start | bytes 12292
  18.6 5.1 %collective-permute-start.4 = (f32[17,16,128]{2,1,0:T(8,128)S(1)}, f32[17,16,128]{2,1,0:T(8,128)S(1)}, u32[]{:S(2)}, u32[]{:S(2)}) collective-permute-start(f32[17,16,128]{2,1,0:T(8,128)S(1)} %get-tuple-element.45), channel_id=1, source_target_pairs={{0,1},{1,0},{2,3},{3,2},{4,5},{5,4},{6,7},{7,6},{8,9},{9,8},{10,11... | collective-permute-start | bytes 417800 | tf_op jit(solution)/shard_map/ppermute | solution.py:448
  20.1 7.8 %collective-permute-start.5 = (f32[17,16,128]{2,1,0:T(8,128)S(1)}, f32[17,16,128]{2,1,0:T(8,128)S(1)}, u32[]{:S(2)}, u32[]{:S(2)}) collective-permute-start(f32[17,16,128]{2,1,0:T(8,128)S(1)} %get-tuple-element.46), channel_id=1, source_target_pairs={{1,2},{2,1},{5,6},{6,5},{9,10},{10,9},{13,14},{14,13},{17,18},{18,... | collective-permute-start | bytes 417800 | tf_op jit(solution)/shard_map/ppermute | solution.py:448

commit v3 on v2

--- a/solution.py
+++ b/solution.py
@@ -465,11 +465,11 @@
         functools.partial(prepare, geo),
         out_shape=[shape(R, Z, M)] + [shape((R >> l) + 2, Z, M) for l in levels]
         + [shape(east_tiles, Z, M)] * 2 + [shape(2, Z, M)] * 2,
-        in_specs=[pl.BlockSpec(memory_space=pl.ANY)] * len(given),
+        in_specs=[pl.BlockSpec(memory_space=pltpu.HBM)] * len(given),
         scratch_shapes=[pltpu.VMEM((R, Z, M), F32)] + [pltpu.VMEM(x.shape, x.dtype) for x in given]
         + [pltpu.SemaphoreType.DMA((len(given),))],
         compiler_params=params,
-    )(*given)
+    )(*[pltpu.with_memory_space_constraint(x, pltpu.HBM) for x in given])
     field, coarse, sends = outs[0], outs[1 : 1 + LEVELS], outs[1 + LEVELS :]
     got_b = swap(sends[1], "east", 1)
     got_a = swap(sends[0], "east", 0)

time: 34 us -> 28.4 us (0.84); the launches traced: 33.4 us -> 28.2 us
  local copies, waits for them, and re-layouts: 6.18 us -> 0.06 us
  Pallas kernels: 7.85 us -> 8.68 us
    unnamed x28 -> x22, local copies, waits for them, and re-layouts: 6.18 us -> 0.06 us
    pallas_call x1, Pallas kernels: 0.8 us -> 1.64 us  [body(): pl.pallas_call(functools.partial(prepare, geo), out_shape=[shape(R, Z, M)...]
where the time goes in v3:
time: 28.4 us; the launch traced here: 28.2 us
  starting transfers between devices  10.1 us (36%)
  waiting for transfers between devices  9.16 us (32%)
  Pallas kernels  8.68 us (31%)
    ppermute x6, starting transfers between devices, swap(): return lax.ppermute(x, axis, route)  10.1 us
    ppermute x6, waiting for transfers between devices, swap(): return lax.ppermute(x, axis, route)  9.16 us
    pallas_call x1, Pallas kernels, body(): pl.pallas_call(functools.partial(finish, geo), out_shape=shape(Z, R, M),...  5.46 us
    pallas_call x1, Pallas kernels, body(): pl.pallas_call(functools.partial(prepare, geo), out_shape=[shape(R, Z, M)...  1.64 us
    pallas_call x1, Pallas kernels, body(): pl.pallas_call(functools.partial(middle, geo), out_shape=[shape(R, Z, M),...  1.59 us
  transfers between devices with their start and end apart: 6, of which 4 were waited for; matrix products, arithmetic and copies ran while one was open for 0% of the time, Pallas kernels for 0%

profile of v3, /device:TPU:20, one launch (start us, length us, event | category | flops | bytes accessed | tf_op | source)
XLA Modules:
  0.0 28.2 jit_solution(13044009065928056810)
XLA Ops:
  0.0 0.0 copy-start.1
  0.0 0.0 copy-start.3
  0.0 0.0 copy-start.4
  0.0 0.0 copy-start.8
  0.0 0.0 copy-start.10
  0.0 1.6 %shard_map.127 = (f32[64,16,128]{2,1,0:T(8,128)S(1)}, f32[34,16,128]{2,1,0:T(8,128)S(1)}, f32[18,16,128]{2,1,0:T(8,128)S(1)}, f32[10,16,128]{2,1,0:T(8,128)S(1)}...) custom-call(f32[16,64,128]{2,1,0:T(8,128)} %refs_0_.1, ...), custom_call_target="tpu_custom_call" | custom-call | tf_op jit(solution)/shard_map/pallas_call | solution.py:464
  1.7 0.0 copy-start.7
  1.7 0.1 collective-permute-start
  1.8 2.4 %collective-permute-start.1 = (f32[19,16,128]{2,1,0:T(8,128)S(1)}, f32[19,16,128]{2,1,0:T(8,128)S(1)}, u32[]{:S(2)}, u32[]{:S(2)}) collective-permute-start(f32[19,16,128]{2,1,0:T(8,128)S(1)} %get-tuple-element.31), channel_id=1, source_target_pairs={{4,8},{8,4},{12,16},{16,12},{20,24},{24,20},{5,9},{9,5},{13,17},{1... | collective-permute-start | bytes 466952 | tf_op jit(solution)/shard_map/ppermute | solution.py:448
  4.2 1.6 %collective-permute-start.2 = (f32[2,16,128]{2,1,0:T(8,128)S(1)}, f32[2,16,128]{2,1,0:T(8,128)S(1)}, u32[]{:S(2)}, u32[]{:S(2)}) collective-permute-start(f32[2,16,128]{2,1,0:T(8,128)S(1)} %get-tuple-element.32), channel_id=1, source_target_pairs={{0,8},{8,0},{4,12},{12,4},{16,24},{24,16},{20,28},{28,20},{1,9},{9... | collective-permute-start | bytes 49160 | tf_op jit(solution)/shard_map/ppermute | solution.py:448
  5.9 0.0 copy-start.9
  5.9 2.0 %collective-permute-start.3 = (f32[2,16,128]{2,1,0:T(8,128)S(1)}, f32[2,16,128]{2,1,0:T(8,128)S(1)}, u32[]{:S(2)}, u32[]{:S(2)}) collective-permute-start(f32[2,16,128]{2,1,0:T(8,128)S(1)} %get-tuple-element.33), channel_id=1, source_target_pairs={{8,16},{16,8},{12,20},{20,12},{9,17},{17,9},{13,21},{21,13},{10,18... | collective-permute-start | bytes 49160 | tf_op jit(solution)/shard_map/ppermute | solution.py:448
  7.9 1.4 %collective-permute-done.2.refs_6_ = f32[2,16,128]{2,1,0:T(8,128)S(1)} collective-permute-done((f32[2,16,128]{2,1,0:T(8,128)S(1)}, f32[2,16,128]{2,1,0:T(8,128)S(1)}, u32[]{:S(2)}, u32[]{:S(2)}) %collective-permute-start.2) | collective-permute-done | bytes 16416 | tf_op jit(solution)/shard_map/ppermute | solution.py:448
  9.3 2.3 %collective-permute-done.3.refs_7_ = f32[2,16,128]{2,1,0:T(8,128)S(1)} collective-permute-done((f32[2,16,128]{2,1,0:T(8,128)S(1)}, f32[2,16,128]{2,1,0:T(8,128)S(1)}, u32[]{:S(2)}, u32[]{:S(2)}) %collective-permute-start.3) | collective-permute-done | bytes 16416 | tf_op jit(solution)/shard_map/ppermute | solution.py:448
  11.6 0.0 collective-permute-done.refs_4_
  11.6 0.0 collective-permute-done.1.refs_5_
  11.6 0.0 copy-done.1
  11.6 0.0 copy-done.3
  11.6 0.0 copy-done.4
  11.7 0.0 copy-done.8
  11.7 0.0 copy-done.10
  11.7 0.0 copy-done.7
  11.7 0.0 copy-done.9
  11.7 0.0 copy-start
  11.7 0.0 copy-start.2
  11.7 0.0 copy-start.5
  11.7 0.0 copy-start.6
  11.7 1.6 %shard_map.128 = (f32[64,16,128]{2,1,0:T(8,128)S(1)}, f32[9,64,128]{2,1,0:T(8,128)S(1)}, f32[50,16,128]{2,1,0:T(8,128)S(1)}, f32[34,16,128]{2,1,0:T(8,128)S(1)},...) custom-call(f32[64,16,128]{2,1,0:T(8,128)S(1)} %get-tuple-element.26, ...), custom_call_target="tpu_custom_call" | custom-call | tf_op jit(solution)/shard_map/pallas_call | solution.py:480
  13.3 1.6 %collective-permute-start.4 = (f32[17,16,128]{2,1,0:T(8,128)S(1)}, f32[17,16,128]{2,1,0:T(8,128)S(1)}, u32[]{:S(2)}, u32[]{:S(2)}) collective-permute-start(f32[17,16,128]{2,1,0:T(8,128)S(1)} %get-tuple-element.45), channel_id=1, source_target_pairs={{0,1},{1,0},{2,3},{3,2},{4,5},{5,4},{6,7},{7,6},{8,9},{9,8},{10,11... | collective-permute-start | bytes 417800 | tf_op jit(solution)/shard_map/ppermute | solution.py:448
  14.9 2.4 %collective-permute-start.5 = (f32[17,16,128]{2,1,0:T(8,128)S(1)}, f32[17,16,128]{2,1,0:T(8,128)S(1)}, u32[]{:S(2)}, u32[]{:S(2)}) collective-permute-start(f32[17,16,128]{2,1,0:T(8,128)S(1)} %get-tuple-element.46), channel_id=1, source_target_pairs={{1,2},{2,1},{5,6},{6,5},{9,10},{10,9},{13,14},{14,13},{17,18},{18,... | collective-permute-start | bytes 417800 | tf_op jit(solution)/shard_map/ppermute | solution.py:448
  17.3 1.2 %collective-permute-done.4.refs_11_ = f32[17,16,128]{2,1,0:T(8,128)S(1)} collective-permute-done((f32[17,16,128]{2,1,0:T(8,128)S(1)}, f32[17,16,128]{2,1,0:T(8,128)S(1)}, u32[]{:S(2)}, u32[]{:S(2)}) %collective-permute-start.4) | collective-permute-done | bytes 139296 | tf_op jit(solution)/shard_map/ppermute | solution.py:448
  18.5 4.3 %collective-permute-done.5.refs_12_ = f32[17,16,128]{2,1,0:T(8,128)S(1)} collective-permute-done((f32[17,16,128]{2,1,0:T(8,128)S(1)}, f32[17,16,128]{2,1,0:T(8,128)S(1)}, u32[]{:S(2)}, u32[]{:S(2)}) %collective-permute-start.5) | collective-permute-done | bytes 139296 | tf_op jit(solution)/shard_map/ppermute | solution.py:448
  22.7 0.0 copy-done
  22.7 0.0 copy-done.2
  22.7 0.0 copy-done.5
  22.7 0.0 copy-done.6
  22.8 5.5 %shard_map.129 = f32[16,64,128]{2,1,0:T(8,128)} custom-call(f32[64,16,128]{2,1,0:T(8,128)S(1)} %get-tuple-element.34.refs_0_, f32[9,64,128]{2,1,0:T(8,128)S(1)} %get-tuple-element.35.refs_1_, f32[50,16,128]{2,1,0:T(8,128)S(1)} %get-tuple-element.36.refs_2_, f32[34,16,128]{2,1,0:T(8,128)S(1)} %get-tuple-element.37.refs_3_, ...), custom_call_target="tpu_custom_call" | custom-call | tf_op jit(solution)/shard_map/pallas_call | solution.py:496
Async XLA Ops:
  0.0 11.6 %copy-start.1 = (s32[64,128]{1,0:T(8,128)S(1)}, s32[64,128]{1,0:T(8,128)}, u32[]{:S(2)}) copy-start(s32[64,128]{1,0:T(8,128)} %refs_14_.3) | copy-start | bytes 98308
  0.0 11.6 %copy-start.3 = (s32[32,64]{1,0:T(8,128)S(1)}, s32[32,64]{1,0:T(8,128)}, u32[]{:S(2)}) copy-start(s32[32,64]{1,0:T(8,128)} %refs_9_.1) | copy-start | bytes 24580
  0.0 11.6 %copy-start.4 = (f32[32,64]{1,0:T(8,128)S(1)}, f32[32,64]{1,0:T(8,128)}, u32[]{:S(2)}) copy-start(f32[32,64]{1,0:T(8,128)} %refs_12_.1) | copy-start | bytes 24580
  0.0 11.6 %copy-start.8 = (f32[16,32]{1,0:T(8,128)S(1)}, f32[16,32]{1,0:T(8,128)}, u32[]{:S(2)}) copy-start(f32[16,32]{1,0:T(8,128)} %refs_13_.2) | copy-start | bytes 6148
  0.0 11.6 %copy-start.10 = (f32[8,16]{1,0:T(8,128)S(1)}, f32[8,16]{1,0:T(8,128)}, u32[]{:S(2)}) copy-start(f32[8,16]{1,0:T(8,128)} %refs_14_.2) | copy-start | bytes 1540
  1.7 10.0 %copy-start.7 = (s32[16,32]{1,0:T(8,128)S(1)}, s32[16,32]{1,0:T(8,128)}, u32[]{:S(2)}) copy-start(s32[16,32]{1,0:T(8,128)} %refs_10_.1) | copy-start | bytes 6148
  1.7 9.9 %collective-permute-start = (f32[19,16,128]{2,1,0:T(8,128)S(1)}, f32[19,16,128]{2,1,0:T(8,128)S(1)}, u32[]{:S(2)}, u32[]{:S(2)}) collective-permute-start(f32[19,16,128]{2,1,0:T(8,128)S(1)} %get-tuple-element.30), channel_id=1, source_target_pairs={{0,4},{4,0},{8,12},{12,8},{16,20},{20,16},{24,28},{28,24},{1,5},{5... | collective-permute-start | bytes 466952 | tf_op jit(solution)/shard_map/ppermute | solution.py:448
  1.8 9.9 %collective-permute-start.1 = (f32[19,16,128]{2,1,0:T(8,128)S(1)}, f32[19,16,128]{2,1,0:T(8,128)S(1)}, u32[]{:S(2)}, u32[]{:S(2)}) collective-permute-start(f32[19,16,128]{2,1,0:T(8,128)S(1)} %get-tuple-element.31), channel_id=1, source_target_pairs={{4,8},{8,4},{12,16},{16,12},{20,24},{24,20},{5,9},{9,5},{13,17},{1... | collective-permute-start | bytes 466952 | tf_op jit(solution)/shard_map/ppermute | solution.py:448
  4.2 5.1 %collective-permute-start.2 = (f32[2,16,128]{2,1,0:T(8,128)S(1)}, f32[2,16,128]{2,1,0:T(8,128)S(1)}, u32[]{:S(2)}, u32[]{:S(2)}) collective-permute-start(f32[2,16,128]{2,1,0:T(8,128)S(1)} %get-tuple-element.32), channel_id=1, source_target_pairs={{0,8},{8,0},{4,12},{12,4},{16,24},{24,16},{20,28},{28,20},{1,9},{9... | collective-permute-start | bytes 49160 | tf_op jit(solution)/shard_map/ppermute | solution.py:448
  5.9 5.8 %copy-start.9 = (s32[8,16]{1,0:T(8,128)S(1)}, s32[8,16]{1,0:T(8,128)}, u32[]{:S(2)}) copy-start(s32[8,16]{1,0:T(8,128)} %refs_11_.1) | copy-start | bytes 1540
  5.9 5.8 %collective-permute-start.3 = (f32[2,16,128]{2,1,0:T(8,128)S(1)}, f32[2,16,128]{2,1,0:T(8,128)S(1)}, u32[]{:S(2)}, u32[]{:S(2)}) collective-permute-start(f32[2,16,128]{2,1,0:T(8,128)S(1)} %get-tuple-element.33), channel_id=1, source_target_pairs={{8,16},{16,8},{12,20},{20,12},{9,17},{17,9},{13,21},{21,13},{10,18... | collective-permute-start | bytes 49160 | tf_op jit(solution)/shard_map/ppermute | solution.py:448
  11.7 11.0 %copy-start = (bf16[256,1024]{1,0:T(8,128)(2,1)S(1)}, bf16[256,1024]{1,0:T(8,128)(2,1)}, u32[]{:S(2)}) copy-start(bf16[256,1024]{1,0:T(8,128)(2,1)} %constant.8.clone.refs_17_) | copy-start | bytes 1572868
  11.7 11.0 %copy-start.2 = (bf16[4,128,128]{2,1,0:T(8,128)(2,1)S(1)}, bf16[4,128,128]{2,1,0:T(8,128)(2,1)}, u32[]{:S(2)}) copy-start(bf16[4,128,128]{2,1,0:T(8,128)(2,1)} %constant.7.clone.refs_16_) | copy-start | bytes 393220
  11.7 11.0 %copy-start.5 = (f32[64,128]{1,0:T(8,128)S(1)}, f32[64,128]{1,0:T(8,128)}, u32[]{:S(2)}) copy-start(f32[64,128]{1,0:T(8,128)} %refs_13_.3) | copy-start | bytes 98308
  11.7 11.0 %copy-start.6 = (f32[4,16,16]{2,1,0:T(8,128)S(1)}, f32[4,16,16]{2,1,0:T(8,128)}, u32[]{:S(2)}) copy-start(f32[4,16,16]{2,1,0:T(8,128)} %refs_15_.1) | copy-start | bytes 12292
  13.3 5.1 %collective-permute-start.4 = (f32[17,16,128]{2,1,0:T(8,128)S(1)}, f32[17,16,128]{2,1,0:T(8,128)S(1)}, u32[]{:S(2)}, u32[]{:S(2)}) collective-permute-start(f32[17,16,128]{2,1,0:T(8,128)S(1)} %get-tuple-element.45), channel_id=1, source_target_pairs={{0,1},{1,0},{2,3},{3,2},{4,5},{5,4},{6,7},{7,6},{8,9},{9,8},{10,11... | collective-permute-start | bytes 417800 | tf_op jit(solution)/shard_map/ppermute | solution.py:448
  14.9 7.8 %collective-permute-start.5 = (f32[17,16,128]{2,1,0:T(8,128)S(1)}, f32[17,16,128]{2,1,0:T(8,128)S(1)}, u32[]{:S(2)}, u32[]{:S(2)}) collective-permute-start(f32[17,16,128]{2,1,0:T(8,128)S(1)} %get-tuple-element.46), channel_id=1, source_target_pairs={{1,2},{2,1},{5,6},{6,5},{9,10},{10,9},{13,14},{14,13},{17,18},{18,... | collective-permute-start | bytes 417800 | tf_op jit(solution)/shard_map/ppermute | solution.py:448

commit v4 on v3

--- a/solution.py
+++ b/solution.py
@@ -102,7 +102,7 @@
 def prepare(geo, *refs):
     count = 2 * LEVELS + 2
     outside, (field, *rest) = refs[:count], refs[count:]
-    coarse, (send_a, send_b, send_c, send_d, half, *inside) = rest[:LEVELS], rest[LEVELS:]
+    coarse, (send_a, send_b, send_c, half, *inside) = rest[:LEVELS], rest[LEVELS:]
     sems = inside.pop()
     copies = [pltpu.make_async_copy(a, b, sems.at[i]) for i, (a, b) in enumerate(zip(outside, inside))]
     for copy in copies:
@@ -169,11 +169,8 @@
         send_a[last, pl.ds(j, 1), pl.ds(0, m)] = jnp.where(even, upper, lower)
         send_b[last, pl.ds(j, 1), pl.ds(0, m)] = jnp.where(even, lower, upper)
     r = R >> LEVELS
-    forward = (e // 2) % 2 == 0
     for i in range(2):
-        lower, upper = coarse[LEVELS - 1][i], coarse[LEVELS - 1][r + i]
-        send_c[i] = jnp.where(forward, upper, lower)
-        send_d[i] = jnp.where(forward, lower, upper)
+        send_c[i] = jnp.where(even, coarse[LEVELS - 1][r + i], coarse[LEVELS - 1][i])
 
 
 def east_rows(source, factors, out, count, block, factor_at=0, source_at=0, out_at=0):
@@ -193,28 +190,34 @@
     lax.fori_loop(0, count // block, step, 0)
 
 
+def interior(geo, field, widths0, factors, inner):
+    for k, a in enumerate(taps(widths0[...].astype(F32))):
+        factors[k] = a
+    east_rows(field, factors, inner, geo["R"] - 2 * H, 4, H)
+
+
 def middle(geo, *refs):
     Z, R, M, bases = geo["Z"], geo["R"], geo["M"], geo["bases"]
     it = iter(refs)
     take = lambda count: [next(it) for _ in range(count)]
     (field,) = take(1)
     coarse = take(LEVELS)
-    got_a, got_b, got_c, got_d, widths0 = take(5)
+    got_a, got_b, got_c, got_d, factors, inner = take(6)
     widths, gains = take(LEVELS), take(LEVELS)
-    eastward, factors = take(2)
+    (eastward,) = take(1)
     joined = take(LEVELS)
     send_x, send_y = take(2)
     wide, gain = take(LEVELS), take(LEVELS)
-    (full,) = take(1)
+    below, above = take(2)
     e, n = lax.axis_index("east"), lax.axis_index("north")
     even = e % 2 == 0
-    forward = (e // 2) % 2 == 0
-    for k, a in enumerate(taps(widths0[...].astype(F32))):
-        factors[k] = a
-    full[pl.ds(H, R)] = field[...]
-    full[0:H] = jnp.where(even, got_b[0:H], got_a[0:H])
-    full[H + R : R + 2 * H] = jnp.where(even, got_a[0:H], got_b[0:H])
-    east_rows(full, factors, eastward, R, 4)
+    below[0:H] = jnp.where(even, got_b[0:H], got_a[0:H])
+    below[H : 3 * H] = field[0 : 2 * H]
+    above[0 : 2 * H] = field[R - 2 * H : R]
+    above[2 * H : 3 * H] = jnp.where(even, got_a[0:H], got_b[0:H])
+    east_rows(below, factors, eastward, H, 4)
+    east_rows(above, factors, eastward, H, 4, R - H, 0, R - H)
+    eastward[H : R - H] = inner[...]
     for l in range(1, LEVELS + 1):
         r, out, own = R >> l, joined[l - 1], coarse[l - 1]
         out[H : H + r + 2] = own[...]
@@ -229,9 +232,9 @@
             out[r + H + i] = out[r + H + i] + upper
     r, out = R >> LEVELS, joined[LEVELS - 1]
     for i in range(2):
-        c, d = got_c[i], got_d[i]
-        out[i] = out[i] + jnp.where(forward, d, c)
-        out[r + 2 * H + i] = out[r + 2 * H + i] + jnp.where(forward, c, d)
+        far = got_c[i]
+        out[i] = out[i] + jnp.where(even, far, got_d[H + r + i])
+        out[r + 2 * H + i] = out[r + 2 * H + i] + jnp.where(even, got_d[H + i], far)
     last = H + SLOT
     rows_a, rows_b = got_a[last], got_b[last]
     lower, upper = jnp.where(even, rows_b, rows_a), jnp.where(even, rows_a, rows_b)
@@ -268,22 +271,41 @@
             low_side = jnp.where(here, roll(row, at), low_side)
             high_side = jnp.where(here, roll(row, at - M + H), high_side)
         send(geo["coarse_tiles"] + t, low_side, high_side)
-    base = geo["coarse_tiles"] + R // per
-    for t in range(wide[0].shape[0] // Z):
-        low_side, high_side = zero, zero
-        for j, ref in enumerate((*wide, *gain)):
-            rows, m = ref.shape[0], M >> (j % LEVELS + 1)
-            have = min(max(rows - t * Z, 0), Z)
-            if not have:
-                continue
-            part = ref[pl.ds(t * Z, have), :]
+    low_side, high_side, q = zero, zero, 0
+    for l in range(LEVELS):
+        rows, m, at = wide[l].shape[0], M >> (l + 1), geo["frames"][l + 1]
+        for c in range(0, rows, Z):
+            have = min(rows - c, Z)
+            width, weight = wide[l][pl.ds(c, have), :], gain[l][pl.ds(c, have), :]
             if have < Z:
-                part = jnp.concatenate([part, jnp.zeros((Z - have, LANES), F32)], axis=0)
-            here = (lane >= 16 * j) & (lane < 16 * j + H + 1)
-            at = geo["frames"][j % LEVELS + 1]
-            low_side = jnp.where(here, roll(part, 16 * j - at), low_side)
-            high_side = jnp.where(here, roll(part, 16 * j - at - m + H + 1), high_side)
-        send(base + t, low_side, high_side)
+                fill = jnp.zeros((Z - have, LANES), F32)
+                width, weight = jnp.concatenate([width, fill], axis=0), jnp.concatenate([weight, fill], axis=0)
+            begin = SLOT * q
+            here, last_lane = (lane >= begin) & (lane < begin + H + 1), lane == begin + H + 1
+            low_side = jnp.where(here, roll(width, begin - at), low_side)
+            low_side = jnp.where(last_lane, roll(weight, begin + H + 1 - at), low_side)
+            high_side = jnp.where(here, roll(width, begin - at - m + H + 1), high_side)
+            high_side = jnp.where(last_lane, roll(weight, begin + H + 2 - at - m), high_side)
+            q += 1
+    send(geo["coarse_tiles"] + R // per, low_side, high_side)
+
+
+def own_north(geo, eastward, factors, shifts, out):
+    R = geo["R"]
+    for x0 in range(0, R, R // 2):
+        north_rows(eastward, out, range(x0, x0 + R // 2), lambda k, x: factors[k, pl.ds(x, 1), :], shifts)
+
+
+def north_rows(source, target, rows, factor, shifts):
+    Z = source.shape[1]
+    data = source[pl.ds(rows[0], len(rows))].reshape(len(rows) * Z, LANES)
+    pair = jnp.concatenate(split(data), axis=1)
+    for k in range(1, H + 1, 2):
+        moved = mm(pair, shifts[:, (k - 1) * LANES : (k + 1) * LANES])
+        for i, x in enumerate(rows):
+            here = moved[i * Z : (i + 1) * Z]
+            before = factor(0, x) * source[x] if k == 1 else target[x]
+            target[x] = before + factor(k, x) * here[:, :LANES] + factor(k + 1, x) * here[:, LANES:]
 
 
 def kron(vertical, transposed):
@@ -309,12 +331,12 @@
     Z, R, M, bases, frames = geo["Z"], geo["R"], geo["M"], geo["bases"], geo["frames"]
     it = iter(refs)
     take = lambda count: [next(it) for _ in range(count)]
-    eastward, factors = take(2)
+    (north0,) = take(1)
     joined = take(LEVELS)
     wide, gain = take(LEVELS), take(LEVELS)
     got_x, got_y, gain0, widths0, vertical, table, shifts = take(7)
     (out,) = take(1)
-    got_low, got_high, ext, passed, north, result, spread, wf, gf, cf, north0, edge = take(12)
+    got_low, got_high, ext, passed, north, result, spread, wf, gf, cf, edge = take(11)
     e, n = lax.axis_index("east"), lax.axis_index("north")
     has_low, has_high = e > 0, e < geo["E"] - 1
     north_even = n % 2 == 0
@@ -332,13 +354,18 @@
     width_at = starts(2 * H)
     for l in range(LEVELS):
         r, m, at = R >> (l + 1), M >> (l + 1), frames[l + 1]
-        for source, target, j in ((wide[l], wf, l), (gain[l], gf, LEVELS + l)):
-            for c in range(0, r + 2 * H, 8):
-                t, row = base + c // Z, c % Z
-                low_side = roll(got_low[t, row : row + 8, :], at - H - 1 - 16 * j)
-                high_side = roll(got_high[t, row : row + 8, :], at + m - 16 * j)
-                joint = jnp.where(lane8 < at, low_side, jnp.where(lane8 < at + m, source[pl.ds(c, 8), :], high_side))
-                target[pl.ds(width_at[l] + c, 8), :] = jnp.where((lane8 >= at - H - 1) & (lane8 < at + m + H + 1), joint, 0.0)
+        for c in range(0, r + 2 * H, 8):
+            row = c % Z
+            begin = SLOT * (sum(-(-(R >> i) // Z) + 1 for i in range(1, l + 1)) + c // Z)
+            lower, upper = got_low[base, row : row + 8, :], got_high[base, row : row + 8, :]
+            width = jnp.where(
+                lane8 < at,
+                roll(lower, at - H - 1 - begin),
+                jnp.where(lane8 < at + m, wide[l][pl.ds(c, 8), :], roll(upper, at + m - begin)),
+            )
+            wf[pl.ds(width_at[l] + c, 8), :] = jnp.where((lane8 >= at - H - 1) & (lane8 < at + m + H + 1), width, 0.0)
+            weight = jnp.where(lane8 == at - 1, roll(lower, at - H - 2 - begin), gain[l][pl.ds(c, 8), :])
+            gf[pl.ds(width_at[l] + c, 8), :] = jnp.where(lane8 == at + m, roll(upper, at + m - H - 1 - begin), weight)
         for i in range(r + 2 * H + 2):
             t, s = divmod(ext_at[l] + i, PER_TILE)
             own = roll(joined[l][i], at - 1 - bases[l])
@@ -355,16 +382,6 @@
         r = R >> (l + 1)
         east_rows(ext, cf, passed, r + 2, 2, width_at[l] + H - 1, ext_at[l], out_at[l])
 
-    def north_rows(source, target, rows, factor):
-        data = source[pl.ds(rows[0], len(rows))].reshape(len(rows) * Z, LANES)
-        pair = jnp.concatenate(split(data), axis=1)
-        for k in range(1, H + 1, 2):
-            moved = mm(pair, shifts[:, (k - 1) * LANES : (k + 1) * LANES])
-            for i, x in enumerate(rows):
-                here = moved[i * Z : (i + 1) * Z]
-                before = factor(0, x) * source[x] if k == 1 else target[x]
-                target[x] = before + factor(k, x) * here[:, :LANES] + factor(k + 1, x) * here[:, LANES:]
-
     total = out_at[-1]
 
     def coarse_factor(k, x):
@@ -372,8 +389,8 @@
         return cf[k, pl.ds(width_at[l] + H - 1 + x - out_at[l], 1), :]
 
     half = -(-total // 2)
-    north_rows(passed, north, range(0, half), coarse_factor)
-    north_rows(passed, north, range(half, total), coarse_factor)
+    north_rows(passed, north, range(0, half), coarse_factor, shifts)
+    north_rows(passed, north, range(half, total), coarse_factor, shifts)
     for l in range(LEVELS - 1, -1, -1):
         r, m, at = R >> (l + 1), M >> (l + 1), frames[l + 1]
         groups = (r + 2 + 7) // 8
@@ -423,15 +440,10 @@
         edge[t] = summed
     matrix = kron(vertical[0], True)
     widen = table[LEVELS][:, 0 : 6 * Z]
-    factor0 = lambda k, x: factors[k, pl.ds(x, 1), :]
-    for x0 in range(0, R, R // 2):
-        north_rows(eastward, north0, range(x0, x0 + R // 2), factor0)
     at_edge = (lane < H) | (lane >= M - H)
     for b in range(R // 8):
-        for i in range(8):
-            x = 8 * b + i
-            north0[x] = north0[x] + jnp.where(at_edge, roll(edge[b], M - H - 2 * H * i), 0.0)
-        mixed = mix(matrix, north0[8 * b : 8 * b + 8].reshape(8 * Z, LANES))
+        rows = [north0[8 * b + i] + jnp.where(at_edge, roll(edge[b], M - H - 2 * H * i), 0.0) for i in range(8)]
+        mixed = mix(matrix, jnp.concatenate(rows, axis=0))
         high, low = split(spread[4 * b : 4 * b + 6].reshape(6 * Z, LANES))
         added = mm(widen, high) + mm(widen, low)
         weight = gain0[pl.ds(8 * b, 8), :]
@@ -439,13 +451,14 @@
             out[z, pl.ds(8 * b, 8), :] = weight * mixed[z * 8 : z * 8 + 8] + added[z * 8 : z * 8 + 8]
 
 
-def swap(x, axis, first, by=1):
+def swap(x, axis, first):
+    route = [(i, i + 1) for i in range(first, lax.axis_size(axis) - 1, 2)]
+    return lax.ppermute(x, axis, route + [(j, i) for i, j in route])
+
+
+def far(x, axis):
     count = lax.axis_size(axis)
-    route = []
-    for i in range(count - by):
-        if (i // by) % 2 == first:
-            route += [(i, i + by), (i + by, i)]
-    return lax.ppermute(x, axis, route)
+    return lax.ppermute(x, axis, [(i, i + 2) for i in range(0, count - 2, 2)] + [(i, i - 2) for i in range(3, count, 2)])
 
 
 def body(inc, w0, w1, w2, w3, g0, g1, g2, g3, vertical):
@@ -464,7 +477,7 @@
     outs = pl.pallas_call(
         functools.partial(prepare, geo),
         out_shape=[shape(R, Z, M)] + [shape((R >> l) + 2, Z, M) for l in levels]
-        + [shape(east_tiles, Z, M)] * 2 + [shape(2, Z, M)] * 2,
+        + [shape(east_tiles, Z, M)] * 2 + [shape(2, Z, M)],
         in_specs=[pl.BlockSpec(memory_space=pltpu.HBM)] * len(given),
         scratch_shapes=[pltpu.VMEM((R, Z, M), F32)] + [pltpu.VMEM(x.shape, x.dtype) for x in given]
         + [pltpu.SemaphoreType.DMA((len(given),))],
@@ -473,23 +486,32 @@
     field, coarse, sends = outs[0], outs[1 : 1 + LEVELS], outs[1 + LEVELS :]
     got_b = swap(sends[1], "east", 1)
     got_a = swap(sends[0], "east", 0)
-    got_c = swap(sends[2], "east", 0, 2)
-    got_d = swap(sends[3], "east", 1, 2)
+    got_c = far(sends[2], "east")
+    forward, got_c = lax.optimization_barrier((got_b, got_c))
+    got_d = swap(forward, "east", 0)
+    factors, inner = pl.pallas_call(
+        functools.partial(interior, geo),
+        out_shape=[shape(H + 1, R, M), shape(R - 2 * H, Z, M)],
+        compiler_params=params,
+    )(field, w0)
     wide_shapes = [shape((R >> l) + 2 * H, M) for l in levels]
-    north_tiles = geo["coarse_tiles"] + R * H // LANES + wide_shapes[0].shape[0] // Z
+    north_tiles = geo["coarse_tiles"] + R * H // LANES + 1
     outs = pl.pallas_call(
         functools.partial(middle, geo),
-        out_shape=[shape(R, Z, M), shape(H + 1, R, M)]
-        + [shape((R >> l) + 2 * H + 2, Z, M) for l in levels]
+        out_shape=[shape(R, Z, M)] + [shape((R >> l) + 2 * H + 2, Z, M) for l in levels]
         + [shape(north_tiles, Z, M)] * 2 + wide_shapes * 2,
-        scratch_shapes=[pltpu.VMEM((R + 2 * H, Z, M), F32)],
+        scratch_shapes=[pltpu.VMEM((3 * H, Z, M), F32)] * 2,
         compiler_params=params,
-    )(field, *coarse, got_a, got_b, got_c, got_d, w0, w1, w2, w3, g1, g2, g3)
-    eastward, factors = outs[0], outs[1]
-    joined, (send_x, send_y) = outs[2 : 2 + LEVELS], outs[2 + LEVELS : 4 + LEVELS]
-    wide, gain = outs[4 + LEVELS : 4 + 2 * LEVELS], outs[4 + 2 * LEVELS :]
+    )(field, *coarse, got_a, got_b, got_c, got_d, factors, inner, w1, w2, w3, g1, g2, g3)
+    eastward = outs[0]
+    joined, (send_x, send_y) = outs[1 : 1 + LEVELS], outs[1 + LEVELS : 3 + LEVELS]
+    wide, gain = outs[3 + LEVELS : 3 + 2 * LEVELS], outs[3 + 2 * LEVELS :]
     got_x = swap(send_x, "north", 0)
     got_y = swap(send_y, "north", 1)
+    shifts = jnp.asarray(shifts)
+    north0 = pl.pallas_call(
+        functools.partial(own_north, geo), out_shape=shape(R, Z, M), compiler_params=params
+    )(eastward, factors, shifts)
     rows1 = (R >> 1) + 2
     out_rows = sum((R >> l) + 2 for l in levels)
     width_rows = out_rows + LEVELS * (2 * H - 2)
@@ -501,11 +523,11 @@
             for dims in (
                 (north_tiles, Z, M), (north_tiles, Z, M), (total_rows, Z, M), (out_rows, Z, M), (out_rows, Z, M),
                 (rows1, Z, M), (rows1, Z, M), (width_rows, M), (width_rows, M), (H + 1, width_rows, M),
-                (R, Z, M), (R // H, Z, M),
+                (R // H, Z, M),
             )
         ],
         compiler_params=params,
-    )(eastward, factors, *joined, *wide, *gain, got_x, got_y, g0, w0, vertical, jnp.asarray(up), jnp.asarray(shifts))
+    )(north0, *joined, *wide, *gain, got_x, got_y, g0, w0, vertical, jnp.asarray(up), shifts)
 
 
 def solution(mesh):

time: 28.4 us -> 26.7 us (0.940)
  waiting for transfers between devices: 9.16 us -> 6.95 us
    ppermute x6, waiting for transfers between devices: 9.16 us -> 6.95 us  [the longest x5 5.15 us: swap(): return lax.ppermute(x, axis, route + [(j, i) for i, j in route])]
    pallas_call x1 -> x3, Pallas kernels: 1.59 us -> 2.33 us  [the longest x1 1.06 us: body(): pl.pallas_call(functools.partial(middle, geo), out_shape=[shape(R, Z, M)]...]
    pallas_call x1, Pallas kernels: 5.46 us -> 4.95 us  [body(): pl.pallas_call(functools.partial(finish, geo), out_shape=shape(Z, R, M),...]
  transfers between devices with their start and end apart: 6 -> 6, of which waited for: 4 -> 4; matrix products, arithmetic and copies ran while one was open for 0% -> 0% of each run, Pallas kernels for 0% -> 5%
where the time goes in v4:
time: 26.7 us; the launch traced here: 26.5 us
  starting transfers between devices  10.2 us (38%)
  Pallas kernels  8.86 us (33%)
  waiting for transfers between devices  6.95 us (26%)
  local copies, waits for them, and re-layouts  0.3 us (1%)
    ppermute x5, starting transfers between devices, swap(): return lax.ppermute(x, axis, route + [(j, i) for i, j in route])  6.72 us
    ppermute x5, waiting for transfers between devices, swap(): return lax.ppermute(x, axis, route + [(j, i) for i, j in route])  5.15 us
    pallas_call x1, Pallas kernels, body(): pl.pallas_call(functools.partial(finish, geo), out_shape=shape(Z, R, M),...  4.95 us
    ppermute x1, starting transfers between devices, far(): lax.ppermute(x, axis, [(i, i + 2) for i in range(0, count - 2, 2)] + [(i,...  3.49 us
    ppermute x1, waiting for transfers between devices, far(): lax.ppermute(x, axis, [(i, i + 2) for i in range(0, count - 2, 2)] + [(i,...  1.8 us
    pallas_call x1, Pallas kernels, body(): pl.pallas_call(functools.partial(prepare, geo), out_shape=[shape(R, Z, M)...  1.59 us
    pallas_call x1, Pallas kernels, body(): pl.pallas_call(functools.partial(middle, geo), out_shape=[shape(R, Z, M)]...  1.06 us
    pallas_call x1, Pallas kernels, body(): pl.pallas_call(functools.partial(own_north, geo), out_shape=shape(R, Z, M...  0.73 us
  transfers between devices with their start and end apart: 6, of which 4 were waited for; matrix products, arithmetic and copies ran while one was open for 0% of the time, Pallas kernels for 5%

profile of v4, /device:TPU:20, one launch (start us, length us, event | category | flops | bytes accessed | tf_op | source)
XLA Modules:
  0.0 26.5 jit_solution(7590611329326846945)
XLA Ops:
  0.0 0.0 copy-start.1
  0.0 1.6 %shard_map.127 = (f32[64,16,128]{2,1,0:T(8,128)S(1)}, f32[34,16,128]{2,1,0:T(8,128)S(1)}, f32[18,16,128]{2,1,0:T(8,128)S(1)}, f32[10,16,128]{2,1,0:T(8,128)S(1)}...) custom-call(f32[16,64,128]{2,1,0:T(8,128)} %refs_0_.1, ...), custom_call_target="tpu_custom_call" | custom-call | tf_op jit(solution)/shard_map/pallas_call | solution.py:477
  1.6 1.9 %collective-permute-start.1 = (f32[19,16,128]{2,1,0:T(8,128)S(1)}, f32[19,16,128]{2,1,0:T(8,128)S(1)}, u32[]{:S(2)}, u32[]{:S(2)}) collective-permute-start(f32[19,16,128]{2,1,0:T(8,128)S(1)} %get-tuple-element.33), channel_id=1, source_target_pairs={{4,8},{12,16},{20,24},{8,4},{16,12},{24,20},{5,9},{13,17},{21,25},... | collective-permute-start | bytes 466952 | tf_op jit(solution)/shard_map/ppermute | solution.py:456
  3.5 3.5 %collective-permute-start.2 = (f32[2,16,128]{2,1,0:T(8,128)S(1)}, f32[2,16,128]{2,1,0:T(8,128)S(1)}, u32[]{:S(2)}, u32[]{:S(2)}) collective-permute-start(f32[2,16,128]{2,1,0:T(8,128)S(1)} %get-tuple-element.34), channel_id=1, source_target_pairs={{0,8},{8,16},{16,24},{12,4},{20,12},{28,20},{1,9},{9,17},{17,25},{... | collective-permute-start | bytes 49160 | tf_op jit(solution)/shard_map/ppermute | solution.py:461
  7.0 0.3 %collective-permute-start = (f32[19,16,128]{2,1,0:T(8,128)S(1)}, f32[19,16,128]{2,1,0:T(8,128)S(1)}, u32[]{:S(2)}, u32[]{:S(2)}) collective-permute-start(f32[19,16,128]{2,1,0:T(8,128)S(1)} %get-tuple-element.32), channel_id=1, source_target_pairs={{0,4},{8,12},{16,20},{24,28},{4,0},{12,8},{20,16},{28,24},{1,5},{9... | collective-permute-start | bytes 466952 | tf_op jit(solution)/shard_map/ppermute | solution.py:456
  7.4 1.8 %collective-permute-done.2.refs_6_ = f32[2,16,128]{2,1,0:T(8,128)S(1)} collective-permute-done((f32[2,16,128]{2,1,0:T(8,128)S(1)}, f32[2,16,128]{2,1,0:T(8,128)S(1)}, u32[]{:S(2)}, u32[]{:S(2)}) %collective-permute-start.2) | collective-permute-done | bytes 16416 | tf_op jit(solution)/shard_map/ppermute | solution.py:461
  9.2 0.0 collective-permute-done.1.refs_5_
  9.2 0.5 %collective-permute-start.3 = (f32[19,16,128]{2,1,0:T(8,128)S(1)}, f32[19,16,128]{2,1,0:T(8,128)S(1)}, u32[]{:S(2)}, u32[]{:S(2)}) collective-permute-start(f32[19,16,128]{2,1,0:T(8,128)S(1)} %collective-permute-done.1.refs_5_), channel_id=1, source_target_pairs={{0,4},{8,12},{16,20},{24,28},{4,0},{12,8},{20,16},{28,24},{1,5},{9... | collective-permute-start | bytes 466952 | tf_op jit(solution)/shard_map/ppermute | solution.py:456
  9.7 0.0 copy-done.1
  9.7 0.0 copy-start.3
  9.7 0.0 copy-start.4
  9.7 0.0 copy-start.8
  9.7 0.0 copy-start.9
  9.7 0.0 copy-start.10
  9.7 0.5 %shard_map.128 = (f32[9,64,128]{2,1,0:T(8,128)S(1)}, f32[48,16,128]{2,1,0:T(8,128)S(1)}) custom-call(f32[64,16,128]{2,1,0:T(8,128)S(1)} %get-tuple-element.28.field.refs_0_, s32[64,128]{1,0:T(8,128)S(1)} %copy-done.1), custom_call_target="tpu_custom_call" | custom-call | tf_op jit(solution)/shard_map/pallas_call | solution.py:492
  10.3 0.0 copy-start.7
  10.3 0.0 collective-permute-done.refs_4_
  10.3 0.4 %collective-permute-done.3.refs_7_ = f32[19,16,128]{2,1,0:T(8,128)S(1)} collective-permute-done((f32[19,16,128]{2,1,0:T(8,128)S(1)}, f32[19,16,128]{2,1,0:T(8,128)S(1)}, u32[]{:S(2)}, u32[]{:S(2)}) %collective-permute-start.3) | collective-permute-done | bytes 155680 | tf_op jit(solution)/shard_map/ppermute | solution.py:456
  10.7 0.0 copy-done.3
  10.7 0.0 copy-done.4
  10.7 0.0 copy-done.8
  10.7 0.0 copy-done.9
  10.7 0.0 copy-done.10
  10.7 0.2 copy-done.7
  11.0 0.0 copy-start
  11.0 1.1 %shard_map.129 = (f32[64,16,128]{2,1,0:T(8,128)S(1)}, f32[50,16,128]{2,1,0:T(8,128)S(1)}, f32[34,16,128]{2,1,0:T(8,128)S(1)}, f32[26,16,128]{2,1,0:T(8,128)S(1)}...) custom-call(f32[64,16,128]{2,1,0:T(8,128)S(1)} %get-tuple-element.28, ...), custom_call_target="tpu_custom_call" | custom-call | tf_op jit(solution)/shard_map/pallas_call | solution.py:499
  12.0 1.6 %collective-permute-start.4 = (f32[15,16,128]{2,1,0:T(8,128)S(1)}, f32[15,16,128]{2,1,0:T(8,128)S(1)}, u32[]{:S(2)}, u32[]{:S(2)}) collective-permute-start(f32[15,16,128]{2,1,0:T(8,128)S(1)} %get-tuple-element.49), channel_id=1, source_target_pairs={{0,1},{2,3},{1,0},{3,2},{4,5},{6,7},{5,4},{7,6},{8,9},{10,11},{9,8... | collective-permute-start | bytes 368648 | tf_op jit(solution)/shard_map/ppermute | solution.py:456
  13.6 2.4 %collective-permute-start.5 = (f32[15,16,128]{2,1,0:T(8,128)S(1)}, f32[15,16,128]{2,1,0:T(8,128)S(1)}, u32[]{:S(2)}, u32[]{:S(2)}) collective-permute-start(f32[15,16,128]{2,1,0:T(8,128)S(1)} %get-tuple-element.50), channel_id=1, source_target_pairs={{1,2},{2,1},{5,6},{6,5},{9,10},{10,9},{13,14},{14,13},{17,18},{18,... | collective-permute-start | bytes 368648 | tf_op jit(solution)/shard_map/ppermute | solution.py:456
  16.0 0.0 copy-done
  16.0 0.0 copy-start.2
  16.0 0.0 copy-start.5
  16.0 0.0 copy-start.6
  16.0 0.7 %shard_map.130.refs_0_ = f32[64,16,128]{2,1,0:T(8,128)S(1)} custom-call(f32[64,16,128]{2,1,0:T(8,128)S(1)} %get-tuple-element.39.eastward, f32[9,64,128]{2,1,0:T(8,128)S(1)} %get-tuple-element.37.refs_8_.factors, bf16[256,1024]{1,0:T(8,128)(2,1)S(1)} %copy-done), custom_call_target="tpu_custom_call" | custom-call | tf_op jit(solution)/shard_map/pallas_call | solution.py:512
  16.8 0.7 %collective-permute-done.4.refs_10_ = f32[15,16,128]{2,1,0:T(8,128)S(1)} collective-permute-done((f32[15,16,128]{2,1,0:T(8,128)S(1)}, f32[15,16,128]{2,1,0:T(8,128)S(1)}, u32[]{:S(2)}, u32[]{:S(2)}) %collective-permute-start.4) | collective-permute-done | bytes 122912 | tf_op jit(solution)/shard_map/ppermute | solution.py:456
  17.5 4.0 %collective-permute-done.5.refs_11_ = f32[15,16,128]{2,1,0:T(8,128)S(1)} collective-permute-done((f32[15,16,128]{2,1,0:T(8,128)S(1)}, f32[15,16,128]{2,1,0:T(8,128)S(1)}, u32[]{:S(2)}, u32[]{:S(2)}) %collective-permute-start.5) | collective-permute-done | bytes 122912 | tf_op jit(solution)/shard_map/ppermute | solution.py:456
  21.5 0.0 copy-done.2
  21.5 0.0 copy-done.5
  21.5 0.0 copy-done.6
  21.5 5.0 %shard_map.131 = f32[16,64,128]{2,1,0:T(8,128)} custom-call(f32[64,16,128]{2,1,0:T(8,128)S(1)} %shard_map.130.refs_0_, f32[50,16,128]{2,1,0:T(8,128)S(1)} %get-tuple-element.40.refs_1_, f32[34,16,128]{2,1,0:T(8,128)S(1)} %get-tuple-element.41.refs_2_, f32[26,16,128]{2,1,0:T(8,128)S(1)} %get-tuple-element.42.refs_3_, ...), custom_call_target="tpu_custom_call" | custom-call | tf_op jit(solution)/shard_map/pallas_call | solution.py:518
Async XLA Ops:
  0.0 9.7 %copy-start.1 = (s32[64,128]{1,0:T(8,128)S(1)}, s32[64,128]{1,0:T(8,128)}, u32[]{:S(2)}) copy-start(s32[64,128]{1,0:T(8,128)} %refs_13_.3) | copy-start | bytes 98308
  1.6 7.6 %collective-permute-start.1 = (f32[19,16,128]{2,1,0:T(8,128)S(1)}, f32[19,16,128]{2,1,0:T(8,128)S(1)}, u32[]{:S(2)}, u32[]{:S(2)}) collective-permute-start(f32[19,16,128]{2,1,0:T(8,128)S(1)} %get-tuple-element.33), channel_id=1, source_target_pairs={{4,8},{12,16},{20,24},{8,4},{16,12},{24,20},{5,9},{13,17},{21,25},... | collective-permute-start | bytes 466952 | tf_op jit(solution)/shard_map/ppermute | solution.py:456
  3.5 5.6 %collective-permute-start.2 = (f32[2,16,128]{2,1,0:T(8,128)S(1)}, f32[2,16,128]{2,1,0:T(8,128)S(1)}, u32[]{:S(2)}, u32[]{:S(2)}) collective-permute-start(f32[2,16,128]{2,1,0:T(8,128)S(1)} %get-tuple-element.34), channel_id=1, source_target_pairs={{0,8},{8,16},{16,24},{12,4},{20,12},{28,20},{1,9},{9,17},{17,25},{... | collective-permute-start | bytes 49160 | tf_op jit(solution)/shard_map/ppermute | solution.py:461
  7.0 3.3 %collective-permute-start = (f32[19,16,128]{2,1,0:T(8,128)S(1)}, f32[19,16,128]{2,1,0:T(8,128)S(1)}, u32[]{:S(2)}, u32[]{:S(2)}) collective-permute-start(f32[19,16,128]{2,1,0:T(8,128)S(1)} %get-tuple-element.32), channel_id=1, source_target_pairs={{0,4},{8,12},{16,20},{24,28},{4,0},{12,8},{20,16},{28,24},{1,5},{9... | collective-permute-start | bytes 466952 | tf_op jit(solution)/shard_map/ppermute | solution.py:456
  9.2 1.6 %collective-permute-start.3 = (f32[19,16,128]{2,1,0:T(8,128)S(1)}, f32[19,16,128]{2,1,0:T(8,128)S(1)}, u32[]{:S(2)}, u32[]{:S(2)}) collective-permute-start(f32[19,16,128]{2,1,0:T(8,128)S(1)} %collective-permute-done.1.refs_5_), channel_id=1, source_target_pairs={{0,4},{8,12},{16,20},{24,28},{4,0},{12,8},{20,16},{28,24},{1,5},{9... | collective-permute-start | bytes 466952 | tf_op jit(solution)/shard_map/ppermute | solution.py:456
  9.7 1.0 %copy-start.3 = (s32[32,64]{1,0:T(8,128)S(1)}, s32[32,64]{1,0:T(8,128)}, u32[]{:S(2)}) copy-start(s32[32,64]{1,0:T(8,128)} %refs_10_.1) | copy-start | bytes 24580
  9.7 1.0 %copy-start.4 = (f32[32,64]{1,0:T(8,128)S(1)}, f32[32,64]{1,0:T(8,128)}, u32[]{:S(2)}) copy-start(f32[32,64]{1,0:T(8,128)} %refs_13_.2) | copy-start | bytes 24580
  9.7 1.0 %copy-start.8 = (f32[16,32]{1,0:T(8,128)S(1)}, f32[16,32]{1,0:T(8,128)}, u32[]{:S(2)}) copy-start(f32[16,32]{1,0:T(8,128)} %refs_14_.2) | copy-start | bytes 6148
  9.7 1.0 %copy-start.9 = (s32[8,16]{1,0:T(8,128)S(1)}, s32[8,16]{1,0:T(8,128)}, u32[]{:S(2)}) copy-start(s32[8,16]{1,0:T(8,128)} %refs_12_.2) | copy-start | bytes 1540
  9.7 1.0 %copy-start.10 = (f32[8,16]{1,0:T(8,128)S(1)}, f32[8,16]{1,0:T(8,128)}, u32[]{:S(2)}) copy-start(f32[8,16]{1,0:T(8,128)} %refs_15_.2) | copy-start | bytes 1540
  10.3 0.7 %copy-start.7 = (s32[16,32]{1,0:T(8,128)S(1)}, s32[16,32]{1,0:T(8,128)}, u32[]{:S(2)}) copy-start(s32[16,32]{1,0:T(8,128)} %refs_11_.1) | copy-start | bytes 6148
  11.0 5.0 %copy-start = (bf16[256,1024]{1,0:T(8,128)(2,1)S(1)}, bf16[256,1024]{1,0:T(8,128)(2,1)}, u32[]{:S(2)}) copy-start(bf16[256,1024]{1,0:T(8,128)(2,1)} %constant.7.clone.shifts.refs_16_) | copy-start | bytes 1572868
  12.0 5.5 %collective-permute-start.4 = (f32[15,16,128]{2,1,0:T(8,128)S(1)}, f32[15,16,128]{2,1,0:T(8,128)S(1)}, u32[]{:S(2)}, u32[]{:S(2)}) collective-permute-start(f32[15,16,128]{2,1,0:T(8,128)S(1)} %get-tuple-element.49), channel_id=1, source_target_pairs={{0,1},{2,3},{1,0},{3,2},{4,5},{6,7},{5,4},{7,6},{8,9},{10,11},{9,8... | collective-permute-start | bytes 368648 | tf_op jit(solution)/shard_map/ppermute | solution.py:456
  13.6 7.9 %collective-permute-start.5 = (f32[15,16,128]{2,1,0:T(8,128)S(1)}, f32[15,16,128]{2,1,0:T(8,128)S(1)}, u32[]{:S(2)}, u32[]{:S(2)}) collective-permute-start(f32[15,16,128]{2,1,0:T(8,128)S(1)} %get-tuple-element.50), channel_id=1, source_target_pairs={{1,2},{2,1},{5,6},{6,5},{9,10},{10,9},{13,14},{14,13},{17,18},{18,... | collective-permute-start | bytes 368648 | tf_op jit(solution)/shard_map/ppermute | solution.py:456
  16.0 5.5 %copy-start.2 = (bf16[4,128,128]{2,1,0:T(8,128)(2,1)S(1)}, bf16[4,128,128]{2,1,0:T(8,128)(2,1)}, u32[]{:S(2)}) copy-start(bf16[4,128,128]{2,1,0:T(8,128)(2,1)} %constant.8.clone.refs_15_) | copy-start | bytes 393220
  16.0 5.5 %copy-start.5 = (f32[64,128]{1,0:T(8,128)S(1)}, f32[64,128]{1,0:T(8,128)}, u32[]{:S(2)}) copy-start(f32[64,128]{1,0:T(8,128)} %refs_12_.3) | copy-start | bytes 98308
  16.0 5.5 %copy-start.6 = (f32[4,16,16]{2,1,0:T(8,128)S(1)}, f32[4,16,16]{2,1,0:T(8,128)}, u32[]{:S(2)}) copy-start(f32[4,16,16]{2,1,0:T(8,128)} %refs_14_.3) | copy-start | bytes 12292

commit v5 on v4

--- a/solution.py
+++ b/solution.py
@@ -100,15 +100,14 @@
 
 
 def prepare(geo, *refs):
-    count = 2 * LEVELS + 2
+    count = 2
     outside, (field, *rest) = refs[:count], refs[count:]
-    coarse, (send_a, send_b, send_c, half, *inside) = rest[:LEVELS], rest[LEVELS:]
+    coarse, (send_far, half, *inside) = rest[:LEVELS], rest[LEVELS:]
     sems = inside.pop()
     copies = [pltpu.make_async_copy(a, b, sems.at[i]) for i, (a, b) in enumerate(zip(outside, inside))]
     for copy in copies:
         copy.start()
-    inc, table, *small = inside
-    widths, gains = small[:LEVELS], small[LEVELS:]
+    inc, table = inside
     Z, R, M, bases = geo["Z"], geo["R"], geo["M"], geo["bases"]
     e, n = lax.axis_index("east"), lax.axis_index("north")
     has_low, has_high = e > 0, e < geo["E"] - 1
@@ -144,6 +143,15 @@
                 total = jnp.where(has_high, total, 0.0)
             out[j + 1] = total
         source, low, top = out, -1, r + 1
+    r = R >> LEVELS
+    for i in range(2):
+        send_far[i] = jnp.where(even, coarse[LEVELS - 1][r + i], coarse[LEVELS - 1][i])
+
+
+def gather(geo, field, *refs):
+    coarse, got_far, widths, gains, send_a, send_b = refs[:LEVELS], refs[LEVELS], refs[LEVELS + 1 : 2 * LEVELS + 1], refs[2 * LEVELS + 1 : -2], refs[-2], refs[-1]
+    Z, R, M, bases = geo["Z"], geo["R"], geo["M"], geo["bases"]
+    even = lax.axis_index("east") % 2 == 0
     start = R - H
     send_a[0:H] = field[pl.ds(jnp.where(even, start, 0), H)]
     send_b[0:H] = field[pl.ds(jnp.where(even, 0, start), H)]
@@ -168,9 +176,7 @@
         upper = ref[pl.ds(r - 1, 1), :].astype(F32)
         send_a[last, pl.ds(j, 1), pl.ds(0, m)] = jnp.where(even, upper, lower)
         send_b[last, pl.ds(j, 1), pl.ds(0, m)] = jnp.where(even, lower, upper)
-    r = R >> LEVELS
-    for i in range(2):
-        send_c[i] = jnp.where(even, coarse[LEVELS - 1][r + i], coarse[LEVELS - 1][i])
+    send_b[last + 1 : last + 3] = got_far[...]
 
 
 def east_rows(source, factors, out, count, block, factor_at=0, source_at=0, out_at=0):
@@ -202,7 +208,7 @@
     take = lambda count: [next(it) for _ in range(count)]
     (field,) = take(1)
     coarse = take(LEVELS)
-    got_a, got_b, got_c, got_d, factors, inner = take(6)
+    got_a, got_b, got_d, factors, inner = take(5)
     widths, gains = take(LEVELS), take(LEVELS)
     (eastward,) = take(1)
     joined = take(LEVELS)
@@ -232,7 +238,7 @@
             out[r + H + i] = out[r + H + i] + upper
     r, out = R >> LEVELS, joined[LEVELS - 1]
     for i in range(2):
-        far = got_c[i]
+        far = got_b[H + SLOT + 1 + i]
         out[i] = out[i] + jnp.where(even, far, got_d[H + r + i])
         out[r + 2 * H + i] = out[r + 2 * H + i] + jnp.where(even, got_d[H + i], far)
     last = H + SLOT
@@ -266,7 +272,7 @@
     for t in range(R // per):
         low_side, high_side = zero, zero
         for s in range(per):
-            row, at = eastward[t * per + s], 2 * H * (s % H) + H * (s // H)
+            row, at = eastward[t * per + s], 2 * H * (H - 1 - s % H) + H * (s // H)
             here = (lane >= at) & (lane < at + H)
             low_side = jnp.where(here, roll(row, at), low_side)
             high_side = jnp.where(here, roll(row, at - M + H), high_side)
@@ -290,10 +296,25 @@
     send(geo["coarse_tiles"] + R // per, low_side, high_side)
 
 
-def own_north(geo, eastward, factors, shifts, out):
-    R = geo["R"]
+def own_north(geo, eastward, factors, shifts, widths0, vertical, mixed, matrices, edge_taps, north):
+    R, Z = geo["R"], geo["Z"]
     for x0 in range(0, R, R // 2):
-        north_rows(eastward, out, range(x0, x0 + R // 2), lambda k, x: factors[k, pl.ds(x, 1), :], shifts)
+        north_rows(eastward, north, range(x0, x0 + R // 2), lambda k, x: factors[k, pl.ds(x, 1), :], shifts)
+    matrix = kron(vertical[0], True)
+    for b in range(R // 8):
+        mixed[b] = mix(matrix, north[8 * b : 8 * b + 8].reshape(8 * Z, LANES))
+    for l in range(LEVELS + 1):
+        for i, part in enumerate(kron(vertical[l] * 4.0**l, False)):
+            matrices[l, i] = part
+    lane8 = lanes_of(8)
+    slot = lane8 % (2 * H)
+    width = jnp.zeros((H, LANES), F32)
+    for s in range(H):
+        rows = widths0[pl.ds(s, R // H, stride=H), :].astype(F32)
+        at = H - 1 - s
+        width = jnp.where(lane8 // (2 * H) == at, roll(rows, 2 * H * at + H), width)
+    for k, a in enumerate(taps(width)):
+        edge_taps[k] = jnp.where((slot >= H - k) & (slot < H + k), a, 0.0)
 
 
 def north_rows(source, target, rows, factor, shifts):
@@ -331,10 +352,10 @@
     Z, R, M, bases, frames = geo["Z"], geo["R"], geo["M"], geo["bases"], geo["frames"]
     it = iter(refs)
     take = lambda count: [next(it) for _ in range(count)]
-    (north0,) = take(1)
+    mixed0, matrices, edge_taps = take(3)
     joined = take(LEVELS)
     wide, gain = take(LEVELS), take(LEVELS)
-    got_x, got_y, gain0, widths0, vertical, table, shifts = take(7)
+    got_x, got_y, gain0, table, shifts = take(5)
     (out,) = take(1)
     got_low, got_high, ext, passed, north, result, spread, wf, gf, cf, edge = take(11)
     e, n = lax.axis_index("east"), lax.axis_index("north")
@@ -394,7 +415,7 @@
     for l in range(LEVELS - 1, -1, -1):
         r, m, at = R >> (l + 1), M >> (l + 1), frames[l + 1]
         groups = (r + 2 + 7) // 8
-        matrix = kron(vertical[l + 1] * 4.0 ** (l + 1), False)
+        matrix = [matrices[l + 1, 0], matrices[l + 1, 1]]
         for g in range(groups):
             have = min(8, r + 2 - 8 * g)
             data = north[out_at[l] + 8 * g : out_at[l] + 8 * g + have].reshape(have * Z, LANES)
@@ -419,12 +440,6 @@
         flat = result.reshape(result.shape[0] * Z, LANES)
         spread_flat = spread.reshape(spread.shape[0] * Z, LANES)
         spread_flat[pl.ds(0, (r + 2) * Z), :] = dot_exact(flat[pl.ds(0, (r + 2) * Z), :], table[l])
-    slot = lane8 % (2 * H)
-    width = jnp.zeros((H, LANES), F32)
-    for s in range(H):
-        rows = widths0[pl.ds(s, R // H, stride=H), :].astype(F32)
-        width = jnp.where(lane8 // (2 * H) == s, roll(rows, 2 * H * s + H), width)
-    edge_taps = [jnp.where((slot >= H - k) & (slot < H + k), a, 0.0) for k, a in enumerate(taps(width))]
     low_half = lane % (2 * H) < H
     for t in range(R // H):
         tile = geo["coarse_tiles"] + t // 2
@@ -436,29 +451,26 @@
         halo = jnp.where(low_half, low_side, high_side)
         summed = jnp.zeros((Z, LANES), F32)
         for k in range(1, H + 1):
-            summed = summed + edge_taps[k][t : t + 1] * jnp.where(low_half, roll(halo, -k), roll(halo, k))
+            summed = summed + edge_taps[k, pl.ds(t, 1), :] * jnp.where(low_half, roll(halo, -k), roll(halo, k))
         edge[t] = summed
-    matrix = kron(vertical[0], True)
+    edge_flat = edge.reshape(R // H * Z, LANES)
+    edge_flat[...] = mix([matrices[0, 0], matrices[0, 1]], edge_flat[...])
     widen = table[LEVELS][:, 0 : 6 * Z]
-    at_edge = (lane < H) | (lane >= M - H)
+    at_edge = (lane8 < H) | (lane8 >= M - H)
     for b in range(R // 8):
-        rows = [north0[8 * b + i] + jnp.where(at_edge, roll(edge[b], M - H - 2 * H * i), 0.0) for i in range(8)]
-        mixed = mix(matrix, jnp.concatenate(rows, axis=0))
         high, low = split(spread[4 * b : 4 * b + 6].reshape(6 * Z, LANES))
         added = mm(widen, high) + mm(widen, low)
         weight = gain0[pl.ds(8 * b, 8), :]
         for z in range(Z):
-            out[z, pl.ds(8 * b, 8), :] = weight * mixed[z * 8 : z * 8 + 8] + added[z * 8 : z * 8 + 8]
+            row = edge_flat[pl.ds(b * Z + z, 8, stride=0), :]
+            moved = pltpu.roll(row, H, 1, stride=2 * H, stride_axis=0)
+            here = mixed0[b, z * 8 : z * 8 + 8, :] + jnp.where(at_edge, moved, 0.0)
+            out[z, pl.ds(8 * b, 8), :] = weight * here + added[z * 8 : z * 8 + 8]
 
 
 def swap(x, axis, first):
     route = [(i, i + 1) for i in range(first, lax.axis_size(axis) - 1, 2)]
     return lax.ppermute(x, axis, route + [(j, i) for i, j in route])
-
-
-def far(x, axis):
-    count = lax.axis_size(axis)
-    return lax.ppermute(x, axis, [(i, i + 2) for i in range(0, count - 2, 2)] + [(i, i - 2) for i in range(3, count, 2)])
 
 
 def body(inc, w0, w1, w2, w3, g0, g1, g2, g3, vertical):
@@ -473,27 +485,32 @@
     levels = range(1, LEVELS + 1)
     params = pltpu.CompilerParams(vmem_limit_bytes=48 * 1024 * 1024)
     east_tiles = H + SLOT + 1
-    given = (inc, jnp.asarray(down), w1, w2, w3, g1, g2, g3)
+    given = (inc, jnp.asarray(down))
     outs = pl.pallas_call(
         functools.partial(prepare, geo),
         out_shape=[shape(R, Z, M)] + [shape((R >> l) + 2, Z, M) for l in levels]
-        + [shape(east_tiles, Z, M)] * 2 + [shape(2, Z, M)],
+        + [shape(2, Z, M)],
         in_specs=[pl.BlockSpec(memory_space=pltpu.HBM)] * len(given),
         scratch_shapes=[pltpu.VMEM((R, Z, M), F32)] + [pltpu.VMEM(x.shape, x.dtype) for x in given]
         + [pltpu.SemaphoreType.DMA((len(given),))],
         compiler_params=params,
     )(*[pltpu.with_memory_space_constraint(x, pltpu.HBM) for x in given])
-    field, coarse, sends = outs[0], outs[1 : 1 + LEVELS], outs[1 + LEVELS :]
-    got_b = swap(sends[1], "east", 1)
-    got_a = swap(sends[0], "east", 0)
-    got_c = far(sends[2], "east")
-    forward, got_c = lax.optimization_barrier((got_b, got_c))
-    got_d = swap(forward, "east", 0)
+    field, coarse, send_far = outs[0], outs[1 : 1 + LEVELS], outs[1 + LEVELS]
+    got_far = swap(send_far, "east", 0)
+    send_a, send_b = pl.pallas_call(
+        functools.partial(gather, geo),
+        out_shape=[shape(east_tiles, Z, M), shape(east_tiles + 2, Z, M)],
+        compiler_params=params,
+    )(field, *coarse, got_far, w1, w2, w3, g1, g2, g3)
+    got_b = swap(send_b, "east", 1)
+    got_a = swap(send_a, "east", 0)
     factors, inner = pl.pallas_call(
         functools.partial(interior, geo),
         out_shape=[shape(H + 1, R, M), shape(R - 2 * H, Z, M)],
         compiler_params=params,
     )(field, w0)
+    forward, inner, got_a = lax.optimization_barrier((got_b, inner, got_a))
+    got_d = swap(forward, "east", 0)
     wide_shapes = [shape((R >> l) + 2 * H, M) for l in levels]
     north_tiles = geo["coarse_tiles"] + R * H // LANES + 1
     outs = pl.pallas_call(
@@ -502,16 +519,22 @@
         + [shape(north_tiles, Z, M)] * 2 + wide_shapes * 2,
         scratch_shapes=[pltpu.VMEM((3 * H, Z, M), F32)] * 2,
         compiler_params=params,
-    )(field, *coarse, got_a, got_b, got_c, got_d, factors, inner, w1, w2, w3, g1, g2, g3)
+    )(field, *coarse, got_a, got_b, got_d, factors, inner, w1, w2, w3, g1, g2, g3)
     eastward = outs[0]
     joined, (send_x, send_y) = outs[1 : 1 + LEVELS], outs[1 + LEVELS : 3 + LEVELS]
     wide, gain = outs[3 + LEVELS : 3 + 2 * LEVELS], outs[3 + 2 * LEVELS :]
     got_x = swap(send_x, "north", 0)
     got_y = swap(send_y, "north", 1)
     shifts = jnp.asarray(shifts)
-    north0 = pl.pallas_call(
-        functools.partial(own_north, geo), out_shape=shape(R, Z, M), compiler_params=params
-    )(eastward, factors, shifts)
+    assert R // H == 8 and 8 * Z == LANES
+    window = pl.pallas_call(
+        functools.partial(own_north, geo),
+        out_shape=[
+            shape(R // 8, LANES, LANES), jax.ShapeDtypeStruct((LEVELS + 1, 2, LANES, LANES), BF16), shape(H + 1, 8, LANES)
+        ],
+        scratch_shapes=[pltpu.VMEM((R, Z, M), F32)],
+        compiler_params=params,
+    )(eastward, factors, shifts, w0, vertical)
     rows1 = (R >> 1) + 2
     out_rows = sum((R >> l) + 2 for l in levels)
     width_rows = out_rows + LEVELS * (2 * H - 2)
@@ -527,7 +550,7 @@
             )
         ],
         compiler_params=params,
-    )(north0, *joined, *wide, *gain, got_x, got_y, g0, w0, vertical, jnp.asarray(up), shifts)
+    )(*window, *joined, *wide, *gain, got_x, got_y, g0, jnp.asarray(up), shifts)
 
 
 def solution(mesh):

time: 26.7 us -> 25.8 us (0.966)
  starting transfers between devices: 10.2 us -> 7.82 us
  waiting for transfers between devices: 6.95 us -> 8.9 us
    ppermute x5 -> x6, waiting for transfers between devices: 5.15 us -> 8.9 us  [swap(): return lax.ppermute(x, axis, route + [(j, i) for i, j in route])]
    ppermute x1 -> x0, starting transfers between devices: 3.49 us -> none  [far(): lax.ppermute(x, axis, [(i, i + 2) for i in range(0, count - 2, 2)] + [(i,...]
    ppermute x1 -> x0, waiting for transfers between devices: 1.8 us -> none  [far(): lax.ppermute(x, axis, [(i, i + 2) for i in range(0, count - 2, 2)] + [(i,...]
    ppermute x5 -> x6, starting transfers between devices: 6.72 us -> 7.82 us  [swap(): return lax.ppermute(x, axis, route + [(j, i) for i, j in route])]
    pallas_call x1, Pallas kernels: 4.95 us -> 3.98 us  [body(): pl.pallas_call(functools.partial(finish, geo), out_shape=shape(Z, R, M),...]
    pallas_call x1 -> x2, Pallas kernels: 0.73 us -> 1.53 us  [the longest x1 1.48 us: body(): pl.pallas_call(functools.partial(own_north, geo), out_shape=[shape(R // 8...]
  transfers between devices with their start and end apart: 6 -> 6, of which waited for: 4 -> 5; matrix products, arithmetic and copies ran while one was open for 0% -> 0% of each run, Pallas kernels for 5% -> 8%
where the time goes in v5:
time: 25.8 us; the launch traced here: 25.6 us
  waiting for transfers between devices  8.9 us (34%)
  Pallas kernels  8.64 us (33%)
  starting transfers between devices  7.82 us (30%)
    ppermute x6, waiting for transfers between devices, swap(): return lax.ppermute(x, axis, route + [(j, i) for i, j in route])  8.9 us
    ppermute x6, starting transfers between devices, swap(): return lax.ppermute(x, axis, route + [(j, i) for i, j in route])  7.82 us
    pallas_call x1, Pallas kernels, body(): pl.pallas_call(functools.partial(finish, geo), out_shape=shape(Z, R, M),...  3.98 us
    pallas_call x1, Pallas kernels, body(): pl.pallas_call(functools.partial(prepare, geo), out_shape=[shape(R, Z, M)...  1.54 us
    pallas_call x1, Pallas kernels, body(): pl.pallas_call(functools.partial(own_north, geo), out_shape=[shape(R // 8...  1.48 us
    pallas_call x1, Pallas kernels, body(): pl.pallas_call(functools.partial(middle, geo), out_shape=[shape(R, Z, M)]...  1.06 us
    pallas_call x1, Pallas kernels, body(): pl.pallas_call(functools.partial(interior, geo), out_shape=[shape(H + 1,...  0.54 us
  transfers between devices with their start and end apart: 6, of which 5 were waited for; matrix products, arithmetic and copies ran while one was open for 0% of the time, Pallas kernels for 8%

profile of v5, /device:TPU:20, one launch (start us, length us, event | category | flops | bytes accessed | tf_op | source)
XLA Modules:
  0.0 25.6 jit_solution(15565583048738361742)
XLA Ops:
  0.0 0.0 copy-start.3
  0.0 0.0 copy-start.4
  0.0 0.0 copy-start.7
  0.0 0.0 copy-start.9
  0.0 0.0 copy-start.10
  0.0 1.5 %shard_map.127 = (f32[64,16,128]{2,1,0:T(8,128)S(1)}, f32[34,16,128]{2,1,0:T(8,128)S(1)}, f32[18,16,128]{2,1,0:T(8,128)S(1)}, f32[10,16,128]{2,1,0:T(8,128)S(1)}, f32[2,16,128]{2,1,0:T(8,128)S(1)}) custom-call(f32[16,64,128]{2,1,0:T(8,128)} %refs_0_.1, bf16[4,128,128]{2,1,0:T(8,128)(2,1)} %constant.6.clone.refs_1_), custom_call_target="tpu_custom_call" | custom-call | tf_op jit(solution)/shard_map/pallas_call | solution.py:489
  1.6 0.0 copy-start.6
  1.6 0.1 collective-permute-start
  1.7 1.2 %collective-permute-done.refs_3_ = f32[2,16,128]{2,1,0:T(8,128)S(1)} collective-permute-done((f32[2,16,128]{2,1,0:T(8,128)S(1)}, f32[2,16,128]{2,1,0:T(8,128)S(1)}, u32[]{:S(2)}, u32[]{:S(2)}) %collective-permute-start) | collective-permute-done | bytes 16416 | tf_op jit(solution)/shard_map/ppermute | solution.py:473
  2.8 0.0 copy-done.3
  2.8 0.0 copy-done.4
  2.8 0.0 copy-done.7
  2.9 0.0 copy-done.9
  2.9 0.0 copy-done.10
  2.9 0.0 copy-done.6
  2.9 0.0 copy-start.2
  2.9 2.1 %collective-permute-start.1 = (f32[21,16,128]{2,1,0:T(8,128)S(1)}, f32[21,16,128]{2,1,0:T(8,128)S(1)}, u32[]{:S(2)}, u32[]{:S(2)}) collective-permute-start(f32[21,16,128]{2,1,0:T(8,128)S(1)} %get-tuple-element.37), channel_id=1, source_target_pairs={{4,8},{12,16},{20,24},{8,4},{16,12},{24,20},{5,9},{13,17},{21,25},... | collective-permute-start | bytes 516104 | tf_op jit(solution)/shard_map/ppermute | solution.py:473
  5.1 1.5 %collective-permute-start.2 = (f32[19,16,128]{2,1,0:T(8,128)S(1)}, f32[19,16,128]{2,1,0:T(8,128)S(1)}, u32[]{:S(2)}, u32[]{:S(2)}) collective-permute-start(f32[19,16,128]{2,1,0:T(8,128)S(1)} %get-tuple-element.39), channel_id=1, source_target_pairs={{0,4},{8,12},{16,20},{24,28},{4,0},{12,8},{20,16},{28,24},{1,5},{9... | collective-permute-start | bytes 466952 | tf_op jit(solution)/shard_map/ppermute | solution.py:473
  6.6 0.0 copy-done.2
  6.6 0.5 %shard_map.129 = (f32[9,64,128]{2,1,0:T(8,128)S(1)}, f32[48,16,128]{2,1,0:T(8,128)S(1)}) custom-call(f32[64,16,128]{2,1,0:T(8,128)S(1)} %get-tuple-element.32.field.refs_0_, s32[64,128]{1,0:T(8,128)S(1)} %copy-done.2), custom_call_target="tpu_custom_call" | custom-call | tf_op jit(solution)/shard_map/pallas_call | solution.py:507
  7.2 0.5 %collective-permute-done.2.refs_4_ = f32[19,16,128]{2,1,0:T(8,128)S(1)} collective-permute-done((f32[19,16,128]{2,1,0:T(8,128)S(1)}, f32[19,16,128]{2,1,0:T(8,128)S(1)}, u32[]{:S(2)}, u32[]{:S(2)}) %collective-permute-start.2) | collective-permute-done | bytes 155680 | tf_op jit(solution)/shard_map/ppermute | solution.py:473
  7.6 2.0 %collective-permute-done.1.refs_5_ = f32[21,16,128]{2,1,0:T(8,128)S(1)} collective-permute-done((f32[21,16,128]{2,1,0:T(8,128)S(1)}, f32[21,16,128]{2,1,0:T(8,128)S(1)}, u32[]{:S(2)}, u32[]{:S(2)}) %collective-permute-start.1) | collective-permute-done | bytes 172064 | tf_op jit(solution)/shard_map/ppermute | solution.py:473
  9.7 0.2 collective-permute-start.3
  9.8 1.2 %collective-permute-done.3.refs_6_ = f32[21,16,128]{2,1,0:T(8,128)S(1)} collective-permute-done((f32[21,16,128]{2,1,0:T(8,128)S(1)}, f32[21,16,128]{2,1,0:T(8,128)S(1)}, u32[]{:S(2)}, u32[]{:S(2)}) %collective-permute-start.3) | collective-permute-done | bytes 172064 | tf_op jit(solution)/shard_map/ppermute | solution.py:473
  11.1 0.0 copy-start
  11.1 0.0 copy-start.8
  11.1 1.1 %shard_map.130 = (f32[64,16,128]{2,1,0:T(8,128)S(1)}, f32[50,16,128]{2,1,0:T(8,128)S(1)}, f32[34,16,128]{2,1,0:T(8,128)S(1)}, f32[26,16,128]{2,1,0:T(8,128)S(1)}...) custom-call(f32[64,16,128]{2,1,0:T(8,128)S(1)} %get-tuple-element.32, ...), custom_call_target="tpu_custom_call" | custom-call | tf_op jit(solution)/shard_map/pallas_call | solution.py:516
  12.1 1.6 %collective-permute-start.4 = (f32[15,16,128]{2,1,0:T(8,128)S(1)}, f32[15,16,128]{2,1,0:T(8,128)S(1)}, u32[]{:S(2)}, u32[]{:S(2)}) collective-permute-start(f32[15,16,128]{2,1,0:T(8,128)S(1)} %get-tuple-element.57), channel_id=1, source_target_pairs={{0,1},{2,3},{1,0},{3,2},{4,5},{6,7},{5,4},{7,6},{8,9},{10,11},{9,8... | collective-permute-start | bytes 368648 | tf_op jit(solution)/shard_map/ppermute | solution.py:473
  13.7 2.4 %collective-permute-start.5 = (f32[15,16,128]{2,1,0:T(8,128)S(1)}, f32[15,16,128]{2,1,0:T(8,128)S(1)}, u32[]{:S(2)}, u32[]{:S(2)}) collective-permute-start(f32[15,16,128]{2,1,0:T(8,128)S(1)} %get-tuple-element.58), channel_id=1, source_target_pairs={{1,2},{2,1},{5,6},{6,5},{9,10},{10,9},{13,14},{14,13},{17,18},{18,... | collective-permute-start | bytes 368648 | tf_op jit(solution)/shard_map/ppermute | solution.py:473
  16.1 0.0 copy-done
  16.1 0.0 copy-done.8
  16.1 0.0 copy-start.1
  16.1 0.0 copy-start.5
  16.1 1.5 %shard_map.131 = (f32[8,128,128]{2,1,0:T(8,128)S(1)}, bf16[4,2,128,128]{3,2,1,0:T(8,128)(2,1)S(1)}, f32[9,8,128]{2,1,0:T(8,128)S(1)}) custom-call(f32[64,16,128]{2,1,0:T(8,128)S(1)} %get-tuple-element.44.eastward, f32[9,64,128]{2,1,0:T(8,128)S(1)} %get-tuple-element.42.refs_7_.factors, bf16[256,1024]{1,0:T(8,128)(2,1)S(1)} %copy-done, ...), custom_call_target="tpu_custom_call" | custom-call | tf_op jit(solution)/shard_map/pallas_call | solution.py:530
  17.6 0.0 collective-permute-done.4.refs_12_
  17.6 4.0 %collective-permute-done.5.refs_13_ = f32[15,16,128]{2,1,0:T(8,128)S(1)} collective-permute-done((f32[15,16,128]{2,1,0:T(8,128)S(1)}, f32[15,16,128]{2,1,0:T(8,128)S(1)}, u32[]{:S(2)}, u32[]{:S(2)}) %collective-permute-start.5) | collective-permute-done | bytes 122912 | tf_op jit(solution)/shard_map/ppermute | solution.py:473
  21.6 0.0 copy-done.1
  21.6 0.0 copy-done.5
  21.6 4.0 %shard_map.132 = f32[16,64,128]{2,1,0:T(8,128)} custom-call(f32[8,128,128]{2,1,0:T(8,128)S(1)} %get-tuple-element.45.refs_0_, bf16[4,2,128,128]{3,2,1,0:T(8,128)(2,1)S(1)} %get-tuple-element.46.refs_1_, f32[9,8,128]{2,1,0:T(8,128)S(1)} %get-tuple-element.47.refs_2_, f32[50,16,128]{2,1,0:T(8,128)S(1)} %get-tuple-element.48.refs_3_, ...), custom_call_target="tpu_custom_call" | custom-call | tf_op jit(solution)/shard_map/pallas_call | solution.py:541
  (1 shorter events, 0.0 us)
Async XLA Ops:
  0.0 2.8 %copy-start.3 = (s32[32,64]{1,0:T(8,128)S(1)}, s32[32,64]{1,0:T(8,128)}, u32[]{:S(2)}) copy-start(s32[32,64]{1,0:T(8,128)} %refs_9_.3) | copy-start | bytes 24580
  0.0 2.8 %copy-start.4 = (f32[32,64]{1,0:T(8,128)S(1)}, f32[32,64]{1,0:T(8,128)}, u32[]{:S(2)}) copy-start(f32[32,64]{1,0:T(8,128)} %refs_12_.1) | copy-start | bytes 24580
  0.0 2.8 %copy-start.7 = (f32[16,32]{1,0:T(8,128)S(1)}, f32[16,32]{1,0:T(8,128)}, u32[]{:S(2)}) copy-start(f32[16,32]{1,0:T(8,128)} %refs_13_.1) | copy-start | bytes 6148
  0.0 2.8 %copy-start.9 = (s32[8,16]{1,0:T(8,128)S(1)}, s32[8,16]{1,0:T(8,128)}, u32[]{:S(2)}) copy-start(s32[8,16]{1,0:T(8,128)} %refs_11_.1) | copy-start | bytes 1540
  0.0 2.8 %copy-start.10 = (f32[8,16]{1,0:T(8,128)S(1)}, f32[8,16]{1,0:T(8,128)}, u32[]{:S(2)}) copy-start(f32[8,16]{1,0:T(8,128)} %refs_14_.2) | copy-start | bytes 1540
  1.6 1.3 %copy-start.6 = (s32[16,32]{1,0:T(8,128)S(1)}, s32[16,32]{1,0:T(8,128)}, u32[]{:S(2)}) copy-start(s32[16,32]{1,0:T(8,128)} %refs_10_.1) | copy-start | bytes 6148
  1.6 1.2 %collective-permute-start = (f32[2,16,128]{2,1,0:T(8,128)S(1)}, f32[2,16,128]{2,1,0:T(8,128)S(1)}, u32[]{:S(2)}, u32[]{:S(2)}) collective-permute-start(f32[2,16,128]{2,1,0:T(8,128)S(1)} %get-tuple-element.36), channel_id=1, source_target_pairs={{0,4},{8,12},{16,20},{24,28},{4,0},{12,8},{20,16},{28,24},{1,5},{9... | collective-permute-start | bytes 49160 | tf_op jit(solution)/shard_map/ppermute | solution.py:473
  2.9 3.7 %copy-start.2 = (s32[64,128]{1,0:T(8,128)S(1)}, s32[64,128]{1,0:T(8,128)}, u32[]{:S(2)}) copy-start(s32[64,128]{1,0:T(8,128)} %widths0.3) | copy-start | bytes 98308
  2.9 6.7 %collective-permute-start.1 = (f32[21,16,128]{2,1,0:T(8,128)S(1)}, f32[21,16,128]{2,1,0:T(8,128)S(1)}, u32[]{:S(2)}, u32[]{:S(2)}) collective-permute-start(f32[21,16,128]{2,1,0:T(8,128)S(1)} %get-tuple-element.37), channel_id=1, source_target_pairs={{4,8},{12,16},{20,24},{8,4},{16,12},{24,20},{5,9},{13,17},{21,25},... | collective-permute-start | bytes 516104 | tf_op jit(solution)/shard_map/ppermute | solution.py:473
  5.1 2.6 %collective-permute-start.2 = (f32[19,16,128]{2,1,0:T(8,128)S(1)}, f32[19,16,128]{2,1,0:T(8,128)S(1)}, u32[]{:S(2)}, u32[]{:S(2)}) collective-permute-start(f32[19,16,128]{2,1,0:T(8,128)S(1)} %get-tuple-element.39), channel_id=1, source_target_pairs={{0,4},{8,12},{16,20},{24,28},{4,0},{12,8},{20,16},{28,24},{1,5},{9... | collective-permute-start | bytes 466952 | tf_op jit(solution)/shard_map/ppermute | solution.py:473
  9.7 1.4 %collective-permute-start.3 = (f32[21,16,128]{2,1,0:T(8,128)S(1)}, f32[21,16,128]{2,1,0:T(8,128)S(1)}, u32[]{:S(2)}, u32[]{:S(2)}) collective-permute-start(f32[21,16,128]{2,1,0:T(8,128)S(1)} %collective-permute-done.1.refs_5_), channel_id=1, source_target_pairs={{0,4},{8,12},{16,20},{24,28},{4,0},{12,8},{20,16},{28,24},{1,5},{9... | collective-permute-start | bytes 516104 | tf_op jit(solution)/shard_map/ppermute | solution.py:473
  11.1 5.0 %copy-start = (bf16[256,1024]{1,0:T(8,128)(2,1)S(1)}, bf16[256,1024]{1,0:T(8,128)(2,1)}, u32[]{:S(2)}) copy-start(bf16[256,1024]{1,0:T(8,128)(2,1)} %constant.7.clone.shifts.refs_16_) | copy-start | bytes 1572868
  11.1 5.0 %copy-start.8 = (f32[4,16,16]{2,1,0:T(8,128)S(1)}, f32[4,16,16]{2,1,0:T(8,128)}, u32[]{:S(2)}) copy-start(f32[4,16,16]{2,1,0:T(8,128)} %vertical.1) | copy-start | bytes 12292
  12.1 5.5 %collective-permute-start.4 = (f32[15,16,128]{2,1,0:T(8,128)S(1)}, f32[15,16,128]{2,1,0:T(8,128)S(1)}, u32[]{:S(2)}, u32[]{:S(2)}) collective-permute-start(f32[15,16,128]{2,1,0:T(8,128)S(1)} %get-tuple-element.57), channel_id=1, source_target_pairs={{0,1},{2,3},{1,0},{3,2},{4,5},{6,7},{5,4},{7,6},{8,9},{10,11},{9,8... | collective-permute-start | bytes 368648 | tf_op jit(solution)/shard_map/ppermute | solution.py:473
  13.7 7.9 %collective-permute-start.5 = (f32[15,16,128]{2,1,0:T(8,128)S(1)}, f32[15,16,128]{2,1,0:T(8,128)S(1)}, u32[]{:S(2)}, u32[]{:S(2)}) collective-permute-start(f32[15,16,128]{2,1,0:T(8,128)S(1)} %get-tuple-element.58), channel_id=1, source_target_pairs={{1,2},{2,1},{5,6},{6,5},{9,10},{10,9},{13,14},{14,13},{17,18},{18,... | collective-permute-start | bytes 368648 | tf_op jit(solution)/shard_map/ppermute | solution.py:473
  16.1 5.5 %copy-start.1 = (bf16[4,128,128]{2,1,0:T(8,128)(2,1)S(1)}, bf16[4,128,128]{2,1,0:T(8,128)(2,1)}, u32[]{:S(2)}) copy-start(bf16[4,128,128]{2,1,0:T(8,128)(2,1)} %constant.8.clone.refs_15_) | copy-start | bytes 393220
  16.1 5.5 %copy-start.5 = (f32[64,128]{1,0:T(8,128)S(1)}, f32[64,128]{1,0:T(8,128)}, u32[]{:S(2)}) copy-start(f32[64,128]{1,0:T(8,128)} %refs_14_.3) | copy-start | bytes 98308

commit v6 on v5

--- a/solution.py
+++ b/solution.py
@@ -65,6 +65,20 @@
     return bases, frames, down.astype(jnp.bfloat16), up.astype(jnp.bfloat16), shifts.astype(jnp.bfloat16)
 
 
+def place(geo, index):
+    full = geo["coarse_tiles"] * PER_TILE
+    if index < full:
+        return divmod(index, PER_TILE)
+    return geo["coarse_tiles"] + geo["R"] * H // LANES, geo["width_slots"] + index - full
+
+
+def packed(geo, row, l, s):
+    lane, m = lanes_of(row.shape[0]), geo["M"] >> (l + 1)
+    here = (lane >= SLOT * s) & (lane < SLOT * (s + 1))
+    at = SLOT * s - geo["bases"][l]
+    return here, roll(row, at), roll(row, at - m + H)
+
+
 def split(x):
     high = x.astype(BF16)
     return high, (x - high.astype(F32)).astype(BF16)
@@ -181,19 +195,22 @@
 
 def east_rows(source, factors, out, count, block, factor_at=0, source_at=0, out_at=0):
     def step(b, carry):
-        x0 = b * block
-        rows = [source[x0 + i + source_at] for i in range(block + 2 * H)]
-        for i in range(block):
-            def factor(k):
-                return factors[k, pl.ds(x0 + i + factor_at, 1), :]
-
-            total = factor(0) * rows[i + H]
-            for k in range(1, H + 1):
-                total = total + factor(k) * (rows[i + H + k] + rows[i + H - k])
-            out[x0 + i + out_at] = total
+        east_block(source, factors, out, b * block, block, factor_at, source_at, out_at)
         return carry
 
     lax.fori_loop(0, count // block, step, 0)
+
+
+def east_block(source, factors, out, x0, block, factor_at, source_at, out_at):
+    rows = [source[x0 + i + source_at] for i in range(block + 2 * H)]
+    for i in range(block):
+        def factor(k):
+            return factors[k, pl.ds(x0 + i + factor_at, 1), :]
+
+        total = factor(0) * rows[i + H]
+        for k in range(1, H + 1):
+            total = total + factor(k) * (rows[i + H + k] + rows[i + H - k])
+        out[x0 + i + out_at] = total
 
 
 def interior(geo, field, widths0, factors, inner):
@@ -208,7 +225,7 @@
     take = lambda count: [next(it) for _ in range(count)]
     (field,) = take(1)
     coarse = take(LEVELS)
-    got_a, got_b, got_d, factors, inner = take(5)
+    got_a, got_b, factors, inner = take(4)
     widths, gains = take(LEVELS), take(LEVELS)
     (eastward,) = take(1)
     joined = take(LEVELS)
@@ -239,8 +256,8 @@
     r, out = R >> LEVELS, joined[LEVELS - 1]
     for i in range(2):
         far = got_b[H + SLOT + 1 + i]
-        out[i] = out[i] + jnp.where(even, far, got_d[H + r + i])
-        out[r + 2 * H + i] = out[r + 2 * H + i] + jnp.where(even, got_d[H + i], far)
+        out[i] = out[i] + jnp.where(even, far, 0.0)
+        out[r + 2 * H + i] = out[r + 2 * H + i] + jnp.where(even, 0.0, far)
     last = H + SLOT
     rows_a, rows_b = got_a[last], got_b[last]
     lower, upper = jnp.where(even, rows_b, rows_a), jnp.where(even, rows_a, rows_b)
@@ -263,10 +280,8 @@
     for t in range(geo["coarse_tiles"]):
         low_side, high_side = zero, zero
         for s, (l, i) in enumerate(todo[t * PER_TILE : (t + 1) * PER_TILE]):
-            row, m = joined[l][i], M >> (l + 1)
-            here = (lane >= SLOT * s) & (lane < SLOT * (s + 1))
-            low_side = jnp.where(here, roll(row, SLOT * s - bases[l]), low_side)
-            high_side = jnp.where(here, roll(row, SLOT * s - bases[l] - m + H), high_side)
+            here, lower, upper = packed(geo, joined[l][i], l, s)
+            low_side, high_side = jnp.where(here, lower, low_side), jnp.where(here, upper, high_side)
         send(t, low_side, high_side)
     per = LANES // H
     for t in range(R // per):
@@ -293,7 +308,30 @@
             high_side = jnp.where(here, roll(width, begin - at - m + H + 1), high_side)
             high_side = jnp.where(last_lane, roll(weight, begin + H + 2 - at - m), high_side)
             q += 1
+    for l, i in todo[geo["coarse_tiles"] * PER_TILE :]:
+        here, lower, upper = packed(geo, joined[l][i], l, q)
+        low_side, high_side = jnp.where(here, lower, low_side), jnp.where(here, upper, high_side)
+        q += 1
     send(geo["coarse_tiles"] + R // per, low_side, high_side)
+
+
+def forwarded(geo, got_d):
+    even, r = lax.axis_index("east") % 2 == 0, geo["R"] >> LEVELS
+    for i in range(2):
+        yield i, jnp.where(even, 0.0, got_d[H + r + i])
+        yield r + 2 * H + i, jnp.where(even, got_d[H + i], 0.0)
+
+
+def patch(geo, before_x, before_y, got_d, send_x, send_y):
+    north_even = lax.axis_index("north") % 2 == 0
+    send_x[...] = before_x[...]
+    send_y[...] = before_y[...]
+    first = sum((geo["R"] >> l) + 2 * H + 2 for l in range(1, LEVELS))
+    for i, row in forwarded(geo, got_d):
+        t, s = place(geo, first + i)
+        here, lower, upper = packed(geo, row, LEVELS - 1, s)
+        send_x[t] = send_x[t] + jnp.where(here, jnp.where(north_even, upper, lower), 0.0)
+        send_y[t] = send_y[t] + jnp.where(here, jnp.where(north_even, lower, upper), 0.0)
 
 
 def own_north(geo, eastward, factors, shifts, widths0, vertical, mixed, matrices, edge_taps, north):
@@ -355,7 +393,7 @@
     mixed0, matrices, edge_taps = take(3)
     joined = take(LEVELS)
     wide, gain = take(LEVELS), take(LEVELS)
-    got_x, got_y, gain0, table, shifts = take(5)
+    got_x, got_y, got_d, gain0, table, shifts = take(6)
     (out,) = take(1)
     got_low, got_high, ext, passed, north, result, spread, wf, gf, cf, edge = take(11)
     e, n = lax.axis_index("east"), lax.axis_index("north")
@@ -369,44 +407,64 @@
     base = geo["coarse_tiles"] + R // per
     levels = range(1, LEVELS + 1)
     rows_of = [R >> l for l in levels]
-    starts = lambda more: [sum(rows_of[:l]) + l * more for l in range(LEVELS + 1)]
-    ext_at = starts(2 * H + 2)
-    out_at = starts(2)
-    width_at = starts(2 * H)
-    for l in range(LEVELS):
-        r, m, at = R >> (l + 1), M >> (l + 1), frames[l + 1]
+    wire_at = [sum(r + 2 * H + 2 for r in rows_of[:l]) for l in range(LEVELS)]
+    groups = [[0], list(range(1, LEVELS))]
+    group_of = [0] + [1] * (LEVELS - 1)
+    used = [frames[l] + d for l in range(2, LEVELS + 1) for d in range(-H - 1, (M >> l) + H + 1)]
+    assert len(set(used)) == len(used)
+    begins = lambda more: [0 if g == 0 else rows_of[0] + more for g in group_of]
+    ext_at, out_at, width_at = begins(2 * H + 2), begins(2), begins(2 * H)
+    extra = dict(forwarded(geo, got_d))
+
+    def widths_chunk(l, c):
+        r, m, at = rows_of[l], M >> (l + 1), frames[l + 1]
+        row = c % Z
+        begin = SLOT * (sum(-(-(q + 2 * H) // Z) for q in rows_of[:l]) + c // Z)
+        lower, upper = got_low[base, row : row + 8, :], got_high[base, row : row + 8, :]
+        width = jnp.where(
+            lane8 < at,
+            roll(lower, at - H - 1 - begin),
+            jnp.where(lane8 < at + m, wide[l][pl.ds(c, 8), :], roll(upper, at + m - begin)),
+        )
+        width = jnp.where((lane8 >= at - H - 1) & (lane8 < at + m + H + 1), width, 0.0)
+        weight = jnp.where(lane8 == at - 1, roll(lower, at - H - 2 - begin), gain[l][pl.ds(c, 8), :])
+        return width, jnp.where(lane8 == at + m, roll(upper, at + m - H - 1 - begin), weight)
+
+    def source_row(l, i):
+        m, at = M >> (l + 1), frames[l + 1]
+        t, s = place(geo, wire_at[l] + i)
+        own = joined[l][i]
+        if l == LEVELS - 1 and i in extra:
+            own = own + extra[i]
+        own = roll(own, at - 1 - bases[l])
+        low_side = roll(got_low[t], at - H - 1 - SLOT * s)
+        high_side = roll(got_high[t], at + m - 1 - SLOT * s)
+        return (
+            jnp.where((lane >= at - 1) & (lane < at + m + 1), own, 0.0)
+            + jnp.where((lane >= at - H - 1) & (lane < at + 1), low_side, 0.0)
+            + jnp.where((lane >= at + m - 1) & (lane < at + m + H + 1), high_side, 0.0)
+        )
+
+    for g in groups:
+        r = rows_of[g[0]]
         for c in range(0, r + 2 * H, 8):
-            row = c % Z
-            begin = SLOT * (sum(-(-(R >> i) // Z) + 1 for i in range(1, l + 1)) + c // Z)
-            lower, upper = got_low[base, row : row + 8, :], got_high[base, row : row + 8, :]
-            width = jnp.where(
-                lane8 < at,
-                roll(lower, at - H - 1 - begin),
-                jnp.where(lane8 < at + m, wide[l][pl.ds(c, 8), :], roll(upper, at + m - begin)),
-            )
-            wf[pl.ds(width_at[l] + c, 8), :] = jnp.where((lane8 >= at - H - 1) & (lane8 < at + m + H + 1), width, 0.0)
-            weight = jnp.where(lane8 == at - 1, roll(lower, at - H - 2 - begin), gain[l][pl.ds(c, 8), :])
-            gf[pl.ds(width_at[l] + c, 8), :] = jnp.where(lane8 == at + m, roll(upper, at + m - H - 1 - begin), weight)
-        for i in range(r + 2 * H + 2):
-            t, s = divmod(ext_at[l] + i, PER_TILE)
-            own = roll(joined[l][i], at - 1 - bases[l])
-            low_side = roll(got_low[t], at - H - 1 - SLOT * s)
-            high_side = roll(got_high[t], at + m - 1 - SLOT * s)
-            ext[ext_at[l] + i] = (
-                jnp.where((lane >= at - 1) & (lane < at + m + 1), own, 0.0)
-                + jnp.where((lane >= at - H - 1) & (lane < at + 1), low_side, 0.0)
-                + jnp.where((lane >= at + m - 1) & (lane < at + m + H + 1), high_side, 0.0)
-            )
+            parts = [widths_chunk(l, c) for l in g if c < rows_of[l] + 2 * H]
+            wf[pl.ds(width_at[g[0]] + c, 8), :] = functools.reduce(jnp.add, [p[0] for p in parts])
+            gf[pl.ds(width_at[g[0]] + c, 8), :] = functools.reduce(jnp.add, [p[1] for p in parts])
     for k, a in enumerate(taps(wf[...])):
         cf[k] = a
-    for l in range(LEVELS):
-        r = R >> (l + 1)
-        east_rows(ext, cf, passed, r + 2, 2, width_at[l] + H - 1, ext_at[l], out_at[l])
-
-    total = out_at[-1]
+    for g in groups:
+        r = rows_of[g[0]]
+        for i in range(r + 2 * H + 2):
+            parts = [source_row(l, i) for l in g if i < rows_of[l] + 2 * H + 2]
+            ext[ext_at[g[0]] + i] = functools.reduce(jnp.add, parts)
+        for x in range(0, r + 2, 4):
+            east_block(ext, cf, passed, x, min(4, r + 2 - x), width_at[g[0]] + H - 1, ext_at[g[0]], out_at[g[0]])
+
+    total = rows_of[0] + rows_of[1] + 4
 
     def coarse_factor(k, x):
-        l = max(i for i in range(LEVELS) if out_at[i] <= x)
+        l = 0 if x < out_at[1] else 1
         return cf[k, pl.ds(width_at[l] + H - 1 + x - out_at[l], 1), :]
 
     half = -(-total // 2)
@@ -414,9 +472,9 @@
     north_rows(passed, north, range(half, total), coarse_factor, shifts)
     for l in range(LEVELS - 1, -1, -1):
         r, m, at = R >> (l + 1), M >> (l + 1), frames[l + 1]
-        groups = (r + 2 + 7) // 8
+        blocks = (r + 2 + 7) // 8
         matrix = [matrices[l + 1, 0], matrices[l + 1, 1]]
-        for g in range(groups):
+        for g in range(blocks):
             have = min(8, r + 2 - 8 * g)
             data = north[out_at[l] + 8 * g : out_at[l] + 8 * g + have].reshape(have * Z, LANES)
             if have < 8:
@@ -477,9 +535,10 @@
     Z, R, M = inc.shape
     bases, frames, down, up, shifts = tables(R, M)
     total_rows = sum((R >> l) + 2 * H + 2 for l in range(1, LEVELS + 1))
+    width_slots = sum(-(-((R >> l) + 2 * H) // Z) for l in range(1, LEVELS + 1))
     geo = dict(
         Z=Z, R=R, M=M, bases=bases, frames=frames, E=lax.axis_size("east"), N=lax.axis_size("north"),
-        coarse_tiles=-(-total_rows // PER_TILE),
+        coarse_tiles=-(-(total_rows - PER_TILE + width_slots) // PER_TILE), width_slots=width_slots,
     )
     shape = lambda *dims: jax.ShapeDtypeStruct(dims, F32)
     levels = range(1, LEVELS + 1)
@@ -519,10 +578,13 @@
         + [shape(north_tiles, Z, M)] * 2 + wide_shapes * 2,
         scratch_shapes=[pltpu.VMEM((3 * H, Z, M), F32)] * 2,
         compiler_params=params,
-    )(field, *coarse, got_a, got_b, got_d, factors, inner, w1, w2, w3, g1, g2, g3)
+    )(field, *coarse, got_a, got_b, factors, inner, w1, w2, w3, g1, g2, g3)
     eastward = outs[0]
     joined, (send_x, send_y) = outs[1 : 1 + LEVELS], outs[1 + LEVELS : 3 + LEVELS]
     wide, gain = outs[3 + LEVELS : 3 + 2 * LEVELS], outs[3 + 2 * LEVELS :]
+    send_x, send_y = pl.pallas_call(
+        functools.partial(patch, geo), out_shape=[shape(north_tiles, Z, M)] * 2, compiler_params=params
+    )(send_x, send_y, got_d)
     got_x = swap(send_x, "north", 0)
     got_y = swap(send_y, "north", 1)
     shifts = jnp.asarray(shifts)
@@ -536,21 +598,21 @@
         compiler_params=params,
     )(eastward, factors, shifts, w0, vertical)
     rows1 = (R >> 1) + 2
-    out_rows = sum((R >> l) + 2 for l in levels)
-    width_rows = out_rows + LEVELS * (2 * H - 2)
+    out_rows = (R >> 1) + (R >> 2) + 4
+    ext_rows, width_rows = out_rows + 4 * H, out_rows + 4 * H - 4
     return pl.pallas_call(
         functools.partial(finish, geo),
         out_shape=shape(Z, R, M),
         scratch_shapes=[
             pltpu.VMEM(dims, F32)
             for dims in (
-                (north_tiles, Z, M), (north_tiles, Z, M), (total_rows, Z, M), (out_rows, Z, M), (out_rows, Z, M),
+                (north_tiles, Z, M), (north_tiles, Z, M), (ext_rows, Z, M), (out_rows, Z, M), (out_rows, Z, M),
                 (rows1, Z, M), (rows1, Z, M), (width_rows, M), (width_rows, M), (H + 1, width_rows, M),
                 (R // H, Z, M),
             )
         ],
         compiler_params=params,
-    )(*window, *joined, *wide, *gain, got_x, got_y, g0, jnp.asarray(up), shifts)
+    )(*window, *joined, *wide, *gain, got_x, got_y, got_d, g0, jnp.asarray(up), shifts)
 
 
 def solution(mesh):

time: 25.8 us -> 23.9 us (0.926)
  waiting for transfers between devices: 8.9 us -> 7.71 us
  Pallas kernels: 8.64 us -> 7.93 us
    ppermute x6, waiting for transfers between devices: 8.9 us -> 7.71 us  [swap(): return lax.ppermute(x, axis, route + [(j, i) for i, j in route])]
    pallas_call x1, Pallas kernels: 3.98 us -> 3.23 us  [body(): pl.pallas_call(functools.partial(finish, geo), out_shape=shape(Z, R, M),...]
  transfers between devices with their start and end apart: 6 -> 6, of which waited for: 5 -> 5; matrix products, arithmetic and copies ran while one was open for 0% -> 0% of each run, Pallas kernels for 8% -> 13%
where the time goes in v6:
time: 23.9 us; the launch traced here: 23.7 us
  Pallas kernels  7.93 us (33%)
  starting transfers between devices  7.83 us (33%)
  waiting for transfers between devices  7.71 us (32%)
    ppermute x6, starting transfers between devices, swap(): return lax.ppermute(x, axis, route + [(j, i) for i, j in route])  7.83 us
    ppermute x6, waiting for transfers between devices, swap(): return lax.ppermute(x, axis, route + [(j, i) for i, j in route])  7.71 us
    pallas_call x1, Pallas kernels, body(): pl.pallas_call(functools.partial(finish, geo), out_shape=shape(Z, R, M),...  3.23 us
    pallas_call x1, Pallas kernels, body(): pl.pallas_call(functools.partial(prepare, geo), out_shape=[shape(R, Z, M)...  1.53 us
    pallas_call x1, Pallas kernels, body(): pl.pallas_call(functools.partial(own_north, geo), out_shape=[shape(R // 8...  1.45 us
    pallas_call x1, Pallas kernels, body(): pl.pallas_call(functools.partial(middle, geo), out_shape=[shape(R, Z, M)]...  1.04 us
    pallas_call x1, Pallas kernels, body(): pl.pallas_call(functools.partial(interior, geo), out_shape=[shape(H + 1,...  0.53 us
  transfers between devices with their start and end apart: 6, of which 5 were waited for; matrix products, arithmetic and copies ran while one was open for 0% of the time, Pallas kernels for 13%

profile of v6, /device:TPU:20, one launch (start us, length us, event | category | flops | bytes accessed | tf_op | source)
XLA Modules:
  0.0 23.7 jit_solution(13846966875333341178)
XLA Ops:
  0.0 0.0 copy-start.3
  0.0 0.0 copy-start.4
  0.0 0.0 copy-start.7
  0.0 0.0 copy-start.9
  0.0 0.0 copy-start.10
  0.0 1.5 %shard_map.127 = (f32[64,16,128]{2,1,0:T(8,128)S(1)}, f32[34,16,128]{2,1,0:T(8,128)S(1)}, f32[18,16,128]{2,1,0:T(8,128)S(1)}, f32[10,16,128]{2,1,0:T(8,128)S(1)}, f32[2,16,128]{2,1,0:T(8,128)S(1)}) custom-call(f32[16,64,128]{2,1,0:T(8,128)} %refs_0_.1, bf16[4,128,128]{2,1,0:T(8,128)(2,1)} %constant.6.clone.refs_1_), custom_call_target="tpu_custom_call" | custom-call | tf_op jit(solution)/shard_map/pallas_call | solution.py:548
  1.6 0.0 copy-start.6
  1.6 0.1 collective-permute-start
  1.7 1.2 %collective-permute-done.refs_3_ = f32[2,16,128]{2,1,0:T(8,128)S(1)} collective-permute-done((f32[2,16,128]{2,1,0:T(8,128)S(1)}, f32[2,16,128]{2,1,0:T(8,128)S(1)}, u32[]{:S(2)}, u32[]{:S(2)}) %collective-permute-start) | collective-permute-done | bytes 16416 | tf_op jit(solution)/shard_map/ppermute | solution.py:531
  2.8 0.0 copy-done.3
  2.8 0.0 copy-done.4
  2.8 0.0 copy-done.7
  2.8 0.0 copy-done.9
  2.8 0.0 copy-done.10
  2.9 0.0 copy-done.6
  2.9 0.0 copy-start.1
  2.9 2.1 %collective-permute-start.1 = (f32[21,16,128]{2,1,0:T(8,128)S(1)}, f32[21,16,128]{2,1,0:T(8,128)S(1)}, u32[]{:S(2)}, u32[]{:S(2)}) collective-permute-start(f32[21,16,128]{2,1,0:T(8,128)S(1)} %get-tuple-element.39), channel_id=1, source_target_pairs={{4,8},{12,16},{20,24},{8,4},{16,12},{24,20},{5,9},{13,17},{21,25},... | collective-permute-start | bytes 516104 | tf_op jit(solution)/shard_map/ppermute | solution.py:531
  5.1 1.5 %collective-permute-start.2 = (f32[19,16,128]{2,1,0:T(8,128)S(1)}, f32[19,16,128]{2,1,0:T(8,128)S(1)}, u32[]{:S(2)}, u32[]{:S(2)}) collective-permute-start(f32[19,16,128]{2,1,0:T(8,128)S(1)} %get-tuple-element.41), channel_id=1, source_target_pairs={{0,4},{8,12},{16,20},{24,28},{4,0},{12,8},{20,16},{28,24},{1,5},{9... | collective-permute-start | bytes 466952 | tf_op jit(solution)/shard_map/ppermute | solution.py:531
  6.6 0.0 copy-done.1
  6.6 0.5 %shard_map.129 = (f32[9,64,128]{2,1,0:T(8,128)S(1)}, f32[48,16,128]{2,1,0:T(8,128)S(1)}) custom-call(f32[64,16,128]{2,1,0:T(8,128)S(1)} %get-tuple-element.34.field.refs_0_, s32[64,128]{1,0:T(8,128)S(1)} %copy-done.1), custom_call_target="tpu_custom_call" | custom-call | tf_op jit(solution)/shard_map/pallas_call | solution.py:566
  7.2 0.5 %collective-permute-done.2.refs_4_ = f32[19,16,128]{2,1,0:T(8,128)S(1)} collective-permute-done((f32[19,16,128]{2,1,0:T(8,128)S(1)}, f32[19,16,128]{2,1,0:T(8,128)S(1)}, u32[]{:S(2)}, u32[]{:S(2)}) %collective-permute-start.2) | collective-permute-done | bytes 155680 | tf_op jit(solution)/shard_map/ppermute | solution.py:531
  7.6 2.0 %collective-permute-done.1.refs_5_ = f32[21,16,128]{2,1,0:T(8,128)S(1)} collective-permute-done((f32[21,16,128]{2,1,0:T(8,128)S(1)}, f32[21,16,128]{2,1,0:T(8,128)S(1)}, u32[]{:S(2)}, u32[]{:S(2)}) %collective-permute-start.1) | collective-permute-done | bytes 172064 | tf_op jit(solution)/shard_map/ppermute | solution.py:531
  9.7 0.2 collective-permute-start.3
  9.8 0.0 copy-start
  9.8 1.0 %shard_map.130 = (f32[64,16,128]{2,1,0:T(8,128)S(1)}, f32[50,16,128]{2,1,0:T(8,128)S(1)}, f32[34,16,128]{2,1,0:T(8,128)S(1)}, f32[26,16,128]{2,1,0:T(8,128)S(1)}...) custom-call(f32[64,16,128]{2,1,0:T(8,128)S(1)} %get-tuple-element.34, ...), custom_call_target="tpu_custom_call" | custom-call | tf_op jit(solution)/shard_map/pallas_call | solution.py:575
  10.9 0.2 collective-permute-done.3.got_d.refs_14_
  11.1 0.0 copy-start.8
  11.1 0.1 shard_map.132
  11.2 1.6 %collective-permute-start.4 = (f32[14,16,128]{2,1,0:T(8,128)S(1)}, f32[14,16,128]{2,1,0:T(8,128)S(1)}, u32[]{:S(2)}, u32[]{:S(2)}) collective-permute-start(f32[14,16,128]{2,1,0:T(8,128)S(1)} %get-tuple-element.61), channel_id=1, source_target_pairs={{0,1},{2,3},{1,0},{3,2},{4,5},{6,7},{5,4},{7,6},{8,9},{10,11},{9,8... | collective-permute-start | bytes 344072 | tf_op jit(solution)/shard_map/ppermute | solution.py:531
  12.7 2.4 %collective-permute-start.5 = (f32[14,16,128]{2,1,0:T(8,128)S(1)}, f32[14,16,128]{2,1,0:T(8,128)S(1)}, u32[]{:S(2)}, u32[]{:S(2)}) collective-permute-start(f32[14,16,128]{2,1,0:T(8,128)S(1)} %get-tuple-element.62), channel_id=1, source_target_pairs={{1,2},{2,1},{5,6},{6,5},{9,10},{10,9},{13,14},{14,13},{17,18},{18,... | collective-permute-start | bytes 344072 | tf_op jit(solution)/shard_map/ppermute | solution.py:531
  15.1 0.0 copy-done
  15.1 0.0 copy-done.8
  15.1 0.0 copy-start.2
  15.1 0.0 copy-start.5
  15.2 1.4 %shard_map.131 = (f32[8,128,128]{2,1,0:T(8,128)S(1)}, bf16[4,2,128,128]{3,2,1,0:T(8,128)(2,1)S(1)}, f32[9,8,128]{2,1,0:T(8,128)S(1)}) custom-call(f32[64,16,128]{2,1,0:T(8,128)S(1)} %get-tuple-element.45.eastward, f32[9,64,128]{2,1,0:T(8,128)S(1)} %get-tuple-element.43.refs_6_.factors, bf16[256,1024]{1,0:T(8,128)(2,1)S(1)} %copy-done, ...), custom_call_target="tpu_custom_call" | custom-call | tf_op jit(solution)/shard_map/pallas_call | solution.py:592
  16.6 0.0 collective-permute-done.4.refs_12_
  16.6 3.8 %collective-permute-done.5.refs_13_ = f32[14,16,128]{2,1,0:T(8,128)S(1)} collective-permute-done((f32[14,16,128]{2,1,0:T(8,128)S(1)}, f32[14,16,128]{2,1,0:T(8,128)S(1)}, u32[]{:S(2)}, u32[]{:S(2)}) %collective-permute-start.5) | collective-permute-done | bytes 114720 | tf_op jit(solution)/shard_map/ppermute | solution.py:531
  20.5 0.0 copy-done.2
  20.5 0.0 copy-done.5
  20.5 3.2 %shard_map.133 = f32[16,64,128]{2,1,0:T(8,128)} custom-call(f32[8,128,128]{2,1,0:T(8,128)S(1)} %get-tuple-element.46.refs_0_, bf16[4,2,128,128]{3,2,1,0:T(8,128)(2,1)S(1)} %get-tuple-element.47.refs_1_, f32[9,8,128]{2,1,0:T(8,128)S(1)} %get-tuple-element.48.refs_2_, f32[50,16,128]{2,1,0:T(8,128)S(1)} %get-tuple-element.49.refs_3_, ...), custom_call_target="tpu_custom_call" | custom-call | tf_op jit(solution)/shard_map/pallas_call | solution.py:603
  (1 shorter events, 0.0 us)
Async XLA Ops:
  0.0 2.8 %copy-start.3 = (s32[32,64]{1,0:T(8,128)S(1)}, s32[32,64]{1,0:T(8,128)}, u32[]{:S(2)}) copy-start(s32[32,64]{1,0:T(8,128)} %refs_8_.3) | copy-start | bytes 24580
  0.0 2.8 %copy-start.4 = (f32[32,64]{1,0:T(8,128)S(1)}, f32[32,64]{1,0:T(8,128)}, u32[]{:S(2)}) copy-start(f32[32,64]{1,0:T(8,128)} %refs_11_.1) | copy-start | bytes 24580
  0.0 2.8 %copy-start.7 = (f32[16,32]{1,0:T(8,128)S(1)}, f32[16,32]{1,0:T(8,128)}, u32[]{:S(2)}) copy-start(f32[16,32]{1,0:T(8,128)} %refs_12_.1) | copy-start | bytes 6148
  0.0 2.8 %copy-start.9 = (s32[8,16]{1,0:T(8,128)S(1)}, s32[8,16]{1,0:T(8,128)}, u32[]{:S(2)}) copy-start(s32[8,16]{1,0:T(8,128)} %refs_10_.1) | copy-start | bytes 1540
  0.0 2.8 %copy-start.10 = (f32[8,16]{1,0:T(8,128)S(1)}, f32[8,16]{1,0:T(8,128)}, u32[]{:S(2)}) copy-start(f32[8,16]{1,0:T(8,128)} %refs_13_.1) | copy-start | bytes 1540
  1.6 1.3 %copy-start.6 = (s32[16,32]{1,0:T(8,128)S(1)}, s32[16,32]{1,0:T(8,128)}, u32[]{:S(2)}) copy-start(s32[16,32]{1,0:T(8,128)} %refs_9_.3) | copy-start | bytes 6148
  1.6 1.2 %collective-permute-start = (f32[2,16,128]{2,1,0:T(8,128)S(1)}, f32[2,16,128]{2,1,0:T(8,128)S(1)}, u32[]{:S(2)}, u32[]{:S(2)}) collective-permute-start(f32[2,16,128]{2,1,0:T(8,128)S(1)} %get-tuple-element.38), channel_id=1, source_target_pairs={{0,4},{8,12},{16,20},{24,28},{4,0},{12,8},{20,16},{28,24},{1,5},{9... | collective-permute-start | bytes 49160 | tf_op jit(solution)/shard_map/ppermute | solution.py:531
  2.9 3.7 %copy-start.1 = (s32[64,128]{1,0:T(8,128)S(1)}, s32[64,128]{1,0:T(8,128)}, u32[]{:S(2)}) copy-start(s32[64,128]{1,0:T(8,128)} %widths0.3) | copy-start | bytes 98308
  2.9 6.7 %collective-permute-start.1 = (f32[21,16,128]{2,1,0:T(8,128)S(1)}, f32[21,16,128]{2,1,0:T(8,128)S(1)}, u32[]{:S(2)}, u32[]{:S(2)}) collective-permute-start(f32[21,16,128]{2,1,0:T(8,128)S(1)} %get-tuple-element.39), channel_id=1, source_target_pairs={{4,8},{12,16},{20,24},{8,4},{16,12},{24,20},{5,9},{13,17},{21,25},... | collective-permute-start | bytes 516104 | tf_op jit(solution)/shard_map/ppermute | solution.py:531
  5.1 2.6 %collective-permute-start.2 = (f32[19,16,128]{2,1,0:T(8,128)S(1)}, f32[19,16,128]{2,1,0:T(8,128)S(1)}, u32[]{:S(2)}, u32[]{:S(2)}) collective-permute-start(f32[19,16,128]{2,1,0:T(8,128)S(1)} %get-tuple-element.41), channel_id=1, source_target_pairs={{0,4},{8,12},{16,20},{24,28},{4,0},{12,8},{20,16},{28,24},{1,5},{9... | collective-permute-start | bytes 466952 | tf_op jit(solution)/shard_map/ppermute | solution.py:531
  9.7 1.4 %collective-permute-start.3 = (f32[21,16,128]{2,1,0:T(8,128)S(1)}, f32[21,16,128]{2,1,0:T(8,128)S(1)}, u32[]{:S(2)}, u32[]{:S(2)}) collective-permute-start(f32[21,16,128]{2,1,0:T(8,128)S(1)} %collective-permute-done.1.refs_5_), channel_id=1, source_target_pairs={{0,4},{8,12},{16,20},{24,28},{4,0},{12,8},{20,16},{28,24},{1,5},{9... | collective-permute-start | bytes 516104 | tf_op jit(solution)/shard_map/ppermute | solution.py:531
  9.8 5.3 %copy-start = (bf16[256,1024]{1,0:T(8,128)(2,1)S(1)}, bf16[256,1024]{1,0:T(8,128)(2,1)}, u32[]{:S(2)}) copy-start(bf16[256,1024]{1,0:T(8,128)(2,1)} %constant.7.clone.shifts.refs_17_) | copy-start | bytes 1572868
  11.1 4.1 %copy-start.8 = (f32[4,16,16]{2,1,0:T(8,128)S(1)}, f32[4,16,16]{2,1,0:T(8,128)}, u32[]{:S(2)}) copy-start(f32[4,16,16]{2,1,0:T(8,128)} %vertical.1) | copy-start | bytes 12292
  11.2 5.4 %collective-permute-start.4 = (f32[14,16,128]{2,1,0:T(8,128)S(1)}, f32[14,16,128]{2,1,0:T(8,128)S(1)}, u32[]{:S(2)}, u32[]{:S(2)}) collective-permute-start(f32[14,16,128]{2,1,0:T(8,128)S(1)} %get-tuple-element.61), channel_id=1, source_target_pairs={{0,1},{2,3},{1,0},{3,2},{4,5},{6,7},{5,4},{7,6},{8,9},{10,11},{9,8... | collective-permute-start | bytes 344072 | tf_op jit(solution)/shard_map/ppermute | solution.py:531
  12.7 7.7 %collective-permute-start.5 = (f32[14,16,128]{2,1,0:T(8,128)S(1)}, f32[14,16,128]{2,1,0:T(8,128)S(1)}, u32[]{:S(2)}, u32[]{:S(2)}) collective-permute-start(f32[14,16,128]{2,1,0:T(8,128)S(1)} %get-tuple-element.62), channel_id=1, source_target_pairs={{1,2},{2,1},{5,6},{6,5},{9,10},{10,9},{13,14},{14,13},{17,18},{18,... | collective-permute-start | bytes 344072 | tf_op jit(solution)/shard_map/ppermute | solution.py:531
  15.1 5.3 %copy-start.2 = (bf16[4,128,128]{2,1,0:T(8,128)(2,1)S(1)}, bf16[4,128,128]{2,1,0:T(8,128)(2,1)}, u32[]{:S(2)}) copy-start(bf16[4,128,128]{2,1,0:T(8,128)(2,1)} %constant.8.clone.refs_16_) | copy-start | bytes 393220
  15.1 5.3 %copy-start.5 = (f32[64,128]{1,0:T(8,128)S(1)}, f32[64,128]{1,0:T(8,128)}, u32[]{:S(2)}) copy-start(f32[64,128]{1,0:T(8,128)} %refs_15_.1) | copy-start | bytes 98308

commit v7 on v6

--- a/solution.py
+++ b/solution.py
@@ -386,41 +386,99 @@
     return mm(matrix[0], high) + mm(matrix[0], low) + mm(matrix[1], high)
 
 
+def arrange(geo):
+    rows_of = [geo["R"] >> l for l in range(1, LEVELS + 1)]
+    groups = [[0], list(range(1, LEVELS))]
+    wire_at = [sum(r + 2 * H + 2 for r in rows_of[:l]) for l in range(LEVELS)]
+    begins = lambda more: [0] + [rows_of[0] + more] * (LEVELS - 1)
+    frames, M = geo["frames"], geo["M"]
+    used = [frames[l] + d for l in range(2, LEVELS + 1) for d in range(-H - 1, (M >> l) + H + 1)]
+    assert len(set(used)) == len(used)
+    return rows_of, groups, wire_at, begins
+
+
+def side_rows(geo, got, high):
+    frames, M, wire_at = geo["frames"], geo["M"], arrange(geo)[2]
+    lane = lanes_of(geo["Z"])
+    first, masks = [], []
+    for l in range(LEVELS):
+        m, at = M >> (l + 1), frames[l + 1]
+        begin = jnp.where(high, at + m - 1, at - H - 1)
+        first.append(begin)
+        masks.append((lane >= begin) & (lane < begin + SLOT))
+
+    def row(l, i):
+        t, s = place(geo, wire_at[l] + i)
+        return jnp.where(masks[l], pltpu.roll(got[t], (first[l] + LANES - SLOT * s) % LANES, 1), 0.0)
+
+    return row
+
+
+def side_edge(geo, got, high, edge_taps, t):
+    Z = geo["Z"]
+    lane = lanes_of(Z) % (2 * H)
+    inside = (lane < H) != high
+    shift = jnp.where(high, 0 if t % 2 else H, LANES - H if t % 2 else 0)
+    halo = jnp.where(inside, pltpu.roll(got[geo["coarse_tiles"] + t // 2], shift, 1), 0.0)
+    total = jnp.zeros((Z, LANES), F32)
+    for k in range(1, H + 1):
+        total = total + edge_taps[k, pl.ds(t, 1), :] * pltpu.roll(halo, jnp.where(high, LANES - k, k), 1)
+    return jnp.where(inside, 0.0, total)
+
+
+def near_side(geo, *refs):
+    joined, (got_x, got_d, edge_taps, ext, edge) = refs[:LEVELS], refs[LEVELS:]
+    Z, M, bases, frames = geo["Z"], geo["M"], geo["bases"], geo["frames"]
+    high = lax.axis_index("north") % 2 == 0
+    lane = lanes_of(Z)
+    rows_of, groups, _, begins = arrange(geo)
+    extra = dict(forwarded(geo, got_d))
+    side = side_rows(geo, got_x, high)
+
+    def source_row(l, i):
+        m, at = M >> (l + 1), frames[l + 1]
+        own = joined[l][i]
+        if l == LEVELS - 1 and i in extra:
+            own = own + extra[i]
+        own = roll(own, at - 1 - bases[l])
+        return jnp.where((lane >= at - 1) & (lane < at + m + 1), own, 0.0) + side(l, i)
+
+    for g in groups:
+        for i in range(rows_of[g[0]] + 2 * H + 2):
+            parts = [source_row(l, i) for l in g if i < rows_of[l] + 2 * H + 2]
+            ext[begins(2 * H + 2)[g[0]] + i] = functools.reduce(jnp.add, parts)
+    for t in range(geo["R"] // H):
+        edge[t] = side_edge(geo, got_x, high, edge_taps, t)
+
+
 def finish(geo, *refs):
     Z, R, M, bases, frames = geo["Z"], geo["R"], geo["M"], geo["bases"], geo["frames"]
     it = iter(refs)
     take = lambda count: [next(it) for _ in range(count)]
     mixed0, matrices, edge_taps = take(3)
-    joined = take(LEVELS)
+    near, near_edge = take(2)
     wide, gain = take(LEVELS), take(LEVELS)
-    got_x, got_y, got_d, gain0, table, shifts = take(6)
-    (out,) = take(1)
-    got_low, got_high, ext, passed, north, result, spread, wf, gf, cf, edge = take(11)
+    got_x, got_y, gain0, table, shifts = take(5)
+    (result_hbm,) = take(1)
+    ext, passed, north, result, spread, wf, gf, cf, edge, out, sems = take(11)
     e, n = lax.axis_index("east"), lax.axis_index("north")
     has_low, has_high = e > 0, e < geo["E"] - 1
     north_even = n % 2 == 0
-    got_low[...] = jnp.where(north_even, got_y[...], got_x[...])
-    got_high[...] = jnp.where(north_even, got_x[...], got_y[...])
     lane = lanes_of(Z)
     lane8 = lanes_of(8)
     per = LANES // H
     base = geo["coarse_tiles"] + R // per
-    levels = range(1, LEVELS + 1)
-    rows_of = [R >> l for l in levels]
-    wire_at = [sum(r + 2 * H + 2 for r in rows_of[:l]) for l in range(LEVELS)]
-    groups = [[0], list(range(1, LEVELS))]
-    group_of = [0] + [1] * (LEVELS - 1)
-    used = [frames[l] + d for l in range(2, LEVELS + 1) for d in range(-H - 1, (M >> l) + H + 1)]
-    assert len(set(used)) == len(used)
-    begins = lambda more: [0 if g == 0 else rows_of[0] + more for g in group_of]
+    rows_of, groups, _, begins = arrange(geo)
     ext_at, out_at, width_at = begins(2 * H + 2), begins(2), begins(2 * H)
-    extra = dict(forwarded(geo, got_d))
+    tile_x, tile_y = got_x[base], got_y[base]
+    tile_low, tile_high = jnp.where(north_even, tile_y, tile_x), jnp.where(north_even, tile_x, tile_y)
+    side = side_rows(geo, got_y, jnp.logical_not(north_even))
 
     def widths_chunk(l, c):
         r, m, at = rows_of[l], M >> (l + 1), frames[l + 1]
         row = c % Z
         begin = SLOT * (sum(-(-(q + 2 * H) // Z) for q in rows_of[:l]) + c // Z)
-        lower, upper = got_low[base, row : row + 8, :], got_high[base, row : row + 8, :]
+        lower, upper = tile_low[row : row + 8], tile_high[row : row + 8]
         width = jnp.where(
             lane8 < at,
             roll(lower, at - H - 1 - begin),
@@ -429,21 +487,6 @@
         width = jnp.where((lane8 >= at - H - 1) & (lane8 < at + m + H + 1), width, 0.0)
         weight = jnp.where(lane8 == at - 1, roll(lower, at - H - 2 - begin), gain[l][pl.ds(c, 8), :])
         return width, jnp.where(lane8 == at + m, roll(upper, at + m - H - 1 - begin), weight)
-
-    def source_row(l, i):
-        m, at = M >> (l + 1), frames[l + 1]
-        t, s = place(geo, wire_at[l] + i)
-        own = joined[l][i]
-        if l == LEVELS - 1 and i in extra:
-            own = own + extra[i]
-        own = roll(own, at - 1 - bases[l])
-        low_side = roll(got_low[t], at - H - 1 - SLOT * s)
-        high_side = roll(got_high[t], at + m - 1 - SLOT * s)
-        return (
-            jnp.where((lane >= at - 1) & (lane < at + m + 1), own, 0.0)
-            + jnp.where((lane >= at - H - 1) & (lane < at + 1), low_side, 0.0)
-            + jnp.where((lane >= at + m - 1) & (lane < at + m + H + 1), high_side, 0.0)
-        )
 
     for g in groups:
         r = rows_of[g[0]]
@@ -456,8 +499,8 @@
     for g in groups:
         r = rows_of[g[0]]
         for i in range(r + 2 * H + 2):
-            parts = [source_row(l, i) for l in g if i < rows_of[l] + 2 * H + 2]
-            ext[ext_at[g[0]] + i] = functools.reduce(jnp.add, parts)
+            parts = [side(l, i) for l in g if i < rows_of[l] + 2 * H + 2]
+            ext[ext_at[g[0]] + i] = functools.reduce(jnp.add, parts, near[ext_at[g[0]] + i])
         for x in range(0, r + 2, 4):
             east_block(ext, cf, passed, x, min(4, r + 2 - x), width_at[g[0]] + H - 1, ext_at[g[0]], out_at[g[0]])
 
@@ -498,23 +541,13 @@
         flat = result.reshape(result.shape[0] * Z, LANES)
         spread_flat = spread.reshape(spread.shape[0] * Z, LANES)
         spread_flat[pl.ds(0, (r + 2) * Z), :] = dot_exact(flat[pl.ds(0, (r + 2) * Z), :], table[l])
-    low_half = lane % (2 * H) < H
     for t in range(R // H):
-        tile = geo["coarse_tiles"] + t // 2
-        low_side, high_side = got_low[tile], got_high[tile]
-        if t % 2:
-            low_side = roll(low_side, -H)
-        else:
-            high_side = roll(high_side, H)
-        halo = jnp.where(low_half, low_side, high_side)
-        summed = jnp.zeros((Z, LANES), F32)
-        for k in range(1, H + 1):
-            summed = summed + edge_taps[k, pl.ds(t, 1), :] * jnp.where(low_half, roll(halo, -k), roll(halo, k))
-        edge[t] = summed
+        edge[t] = near_edge[t] + side_edge(geo, got_y, jnp.logical_not(north_even), edge_taps, t)
     edge_flat = edge.reshape(R // H * Z, LANES)
     edge_flat[...] = mix([matrices[0, 0], matrices[0, 1]], edge_flat[...])
     widen = table[LEVELS][:, 0 : 6 * Z]
     at_edge = (lane8 < H) | (lane8 >= M - H)
+    copies = []
     for b in range(R // 8):
         high, low = split(spread[4 * b : 4 * b + 6].reshape(6 * Z, LANES))
         added = mm(widen, high) + mm(widen, low)
@@ -524,6 +557,12 @@
             moved = pltpu.roll(row, H, 1, stride=2 * H, stride_axis=0)
             here = mixed0[b, z * 8 : z * 8 + 8, :] + jnp.where(at_edge, moved, 0.0)
             out[z, pl.ds(8 * b, 8), :] = weight * here + added[z * 8 : z * 8 + 8]
+        if b % 2:
+            part = pl.ds(8 * (b - 1), 16)
+            copies.append(pltpu.make_async_copy(out.at[:, part, :], result_hbm.at[:, part, :], sems.at[b // 2]))
+            copies[-1].start()
+    for copy in copies:
+        copy.wait()
 
 
 def swap(x, axis, first):
@@ -600,19 +639,23 @@
     rows1 = (R >> 1) + 2
     out_rows = (R >> 1) + (R >> 2) + 4
     ext_rows, width_rows = out_rows + 4 * H, out_rows + 4 * H - 4
+    near = pl.pallas_call(
+        functools.partial(near_side, geo), out_shape=[shape(ext_rows, Z, M), shape(R // H, Z, M)], compiler_params=params
+    )(*joined, got_x, got_d, window[2])
     return pl.pallas_call(
         functools.partial(finish, geo),
         out_shape=shape(Z, R, M),
+        out_specs=pl.BlockSpec(memory_space=pltpu.HBM),
         scratch_shapes=[
             pltpu.VMEM(dims, F32)
             for dims in (
-                (north_tiles, Z, M), (north_tiles, Z, M), (ext_rows, Z, M), (out_rows, Z, M), (out_rows, Z, M),
+                (ext_rows, Z, M), (out_rows, Z, M), (out_rows, Z, M),
                 (rows1, Z, M), (rows1, Z, M), (width_rows, M), (width_rows, M), (H + 1, width_rows, M),
-                (R // H, Z, M),
+                (R // H, Z, M), (Z, R, M),
             )
-        ],
+        ] + [pltpu.SemaphoreType.DMA((R // 16,))],
         compiler_params=params,
-    )(*window, *joined, *wide, *gain, got_x, got_y, got_d, g0, jnp.asarray(up), shifts)
+    )(*window, *near, *wide, *gain, got_x, got_y, g0, jnp.asarray(up), shifts)
 
 
 def solution(mesh):

time: 23.9 us -> 23.7 us (level)
  waiting for transfers between devices: 7.71 us -> 6.83 us
  Pallas kernels: 7.93 us -> 8.57 us
    ppermute x6, waiting for transfers between devices: 7.71 us -> 6.83 us  [swap(): return lax.ppermute(x, axis, route + [(j, i) for i, j in route])]
    pallas_call x0 -> x1, Pallas kernels: none -> 0.85 us  [body(): pl.pallas_call(functools.partial(near_side, geo), out_shape=[shape(ext_ro...]
  transfers between devices with their start and end apart: 6 -> 6, of which waited for: 5 -> 5; matrix products, arithmetic and copies ran while one was open for 0% -> 0% of each run, Pallas kernels for 13% -> 17%
where the time goes in v7:
time: 23.7 us; the launch traced here: 23.5 us
  Pallas kernels  8.57 us (36%)
  starting transfers between devices  7.83 us (33%)
  waiting for transfers between devices  6.83 us (29%)
    ppermute x6, starting transfers between devices, swap(): return lax.ppermute(x, axis, route + [(j, i) for i, j in route])  7.83 us
    ppermute x6, waiting for transfers between devices, swap(): return lax.ppermute(x, axis, route + [(j, i) for i, j in route])  6.83 us
    pallas_call x1, Pallas kernels, body(): pl.pallas_call(functools.partial(finish, geo), out_shape=shape(Z, R, M),...  3 us
    pallas_call x1, Pallas kernels, body(): pl.pallas_call(functools.partial(prepare, geo), out_shape=[shape(R, Z, M)...  1.53 us
    pallas_call x1, Pallas kernels, body(): pl.pallas_call(functools.partial(own_north, geo), out_shape=[shape(R // 8...  1.46 us
    pallas_call x1, Pallas kernels, body(): pl.pallas_call(functools.partial(middle, geo), out_shape=[shape(R, Z, M)]...  1.05 us
    pallas_call x1, Pallas kernels, body(): pl.pallas_call(functools.partial(near_side, geo), out_shape=[shape(ext_ro...  0.85 us
    pallas_call x1, Pallas kernels, body(): pl.pallas_call(functools.partial(interior, geo), out_shape=[shape(H + 1,...  0.53 us
  transfers between devices with their start and end apart: 6, of which 5 were waited for; matrix products, arithmetic and copies ran while one was open for 0% of the time, Pallas kernels for 17%

profile of v7, /device:TPU:20, one launch (start us, length us, event | category | flops | bytes accessed | tf_op | source)
XLA Modules:
  0.0 23.5 jit_solution(4845506177730163091)
XLA Ops:
  0.0 0.0 copy-start.3
  0.0 0.0 copy-start.4
  0.0 0.0 copy-start.7
  0.0 0.0 copy-start.9
  0.0 0.0 copy-start.10
  0.0 1.5 %shard_map.127 = (f32[64,16,128]{2,1,0:T(8,128)S(1)}, f32[34,16,128]{2,1,0:T(8,128)S(1)}, f32[18,16,128]{2,1,0:T(8,128)S(1)}, f32[10,16,128]{2,1,0:T(8,128)S(1)}, f32[2,16,128]{2,1,0:T(8,128)S(1)}) custom-call(f32[16,64,128]{2,1,0:T(8,128)} %refs_0_.1, bf16[4,128,128]{2,1,0:T(8,128)(2,1)} %constant.6.clone.refs_1_), custom_call_target="tpu_custom_call" | custom-call | tf_op jit(solution)/shard_map/pallas_call | solution.py:587
  1.6 0.0 copy-start.6
  1.6 0.1 collective-permute-start
  1.7 1.2 %collective-permute-done.refs_3_ = f32[2,16,128]{2,1,0:T(8,128)S(1)} collective-permute-done((f32[2,16,128]{2,1,0:T(8,128)S(1)}, f32[2,16,128]{2,1,0:T(8,128)S(1)}, u32[]{:S(2)}, u32[]{:S(2)}) %collective-permute-start) | collective-permute-done | bytes 16416 | tf_op jit(solution)/shard_map/ppermute | solution.py:570
  2.8 0.0 copy-done.3
  2.8 0.0 copy-done.4
  2.8 0.0 copy-done.7
  2.8 0.0 copy-done.9
  2.8 0.0 copy-done.10
  2.9 0.0 copy-done.6
  2.9 0.0 copy-start.2
  2.9 2.1 %collective-permute-start.1 = (f32[21,16,128]{2,1,0:T(8,128)S(1)}, f32[21,16,128]{2,1,0:T(8,128)S(1)}, u32[]{:S(2)}, u32[]{:S(2)}) collective-permute-start(f32[21,16,128]{2,1,0:T(8,128)S(1)} %get-tuple-element.41), channel_id=1, source_target_pairs={{4,8},{12,16},{20,24},{8,4},{16,12},{24,20},{5,9},{13,17},{21,25},... | collective-permute-start | bytes 516104 | tf_op jit(solution)/shard_map/ppermute | solution.py:570
  5.1 1.5 %collective-permute-start.2 = (f32[19,16,128]{2,1,0:T(8,128)S(1)}, f32[19,16,128]{2,1,0:T(8,128)S(1)}, u32[]{:S(2)}, u32[]{:S(2)}) collective-permute-start(f32[19,16,128]{2,1,0:T(8,128)S(1)} %get-tuple-element.43), channel_id=1, source_target_pairs={{0,4},{8,12},{16,20},{24,28},{4,0},{12,8},{20,16},{28,24},{1,5},{9... | collective-permute-start | bytes 466952 | tf_op jit(solution)/shard_map/ppermute | solution.py:570
  6.6 0.0 copy-done.2
  6.6 0.5 %shard_map.129 = (f32[9,64,128]{2,1,0:T(8,128)S(1)}, f32[48,16,128]{2,1,0:T(8,128)S(1)}) custom-call(f32[64,16,128]{2,1,0:T(8,128)S(1)} %get-tuple-element.36.field.refs_0_, s32[64,128]{1,0:T(8,128)S(1)} %copy-done.2), custom_call_target="tpu_custom_call" | custom-call | tf_op jit(solution)/shard_map/pallas_call | solution.py:605
  7.2 0.5 %collective-permute-done.2.refs_4_ = f32[19,16,128]{2,1,0:T(8,128)S(1)} collective-permute-done((f32[19,16,128]{2,1,0:T(8,128)S(1)}, f32[19,16,128]{2,1,0:T(8,128)S(1)}, u32[]{:S(2)}, u32[]{:S(2)}) %collective-permute-start.2) | collective-permute-done | bytes 155680 | tf_op jit(solution)/shard_map/ppermute | solution.py:570
  7.6 2.0 %collective-permute-done.1.refs_5_ = f32[21,16,128]{2,1,0:T(8,128)S(1)} collective-permute-done((f32[21,16,128]{2,1,0:T(8,128)S(1)}, f32[21,16,128]{2,1,0:T(8,128)S(1)}, u32[]{:S(2)}, u32[]{:S(2)}) %collective-permute-start.1) | collective-permute-done | bytes 172064 | tf_op jit(solution)/shard_map/ppermute | solution.py:570
  9.7 0.2 collective-permute-start.3
  9.8 0.0 copy-start
  9.8 1.0 %shard_map.130 = (f32[64,16,128]{2,1,0:T(8,128)S(1)}, f32[50,16,128]{2,1,0:T(8,128)S(1)}, f32[34,16,128]{2,1,0:T(8,128)S(1)}, f32[26,16,128]{2,1,0:T(8,128)S(1)}...) custom-call(f32[64,16,128]{2,1,0:T(8,128)S(1)} %get-tuple-element.36, ...), custom_call_target="tpu_custom_call" | custom-call | tf_op jit(solution)/shard_map/pallas_call | solution.py:614
  10.9 0.2 collective-permute-done.3.got_d.refs_4_
  11.1 0.0 copy-start.8
  11.1 0.1 shard_map.132
  11.2 1.6 %collective-permute-start.4 = (f32[14,16,128]{2,1,0:T(8,128)S(1)}, f32[14,16,128]{2,1,0:T(8,128)S(1)}, u32[]{:S(2)}, u32[]{:S(2)}) collective-permute-start(f32[14,16,128]{2,1,0:T(8,128)S(1)} %get-tuple-element.57), channel_id=1, source_target_pairs={{0,1},{2,3},{1,0},{3,2},{4,5},{6,7},{5,4},{7,6},{8,9},{10,11},{9,8... | collective-permute-start | bytes 344072 | tf_op jit(solution)/shard_map/ppermute | solution.py:570
  12.7 2.4 %collective-permute-start.5 = (f32[14,16,128]{2,1,0:T(8,128)S(1)}, f32[14,16,128]{2,1,0:T(8,128)S(1)}, u32[]{:S(2)}, u32[]{:S(2)}) collective-permute-start(f32[14,16,128]{2,1,0:T(8,128)S(1)} %get-tuple-element.66), channel_id=1, source_target_pairs={{1,2},{2,1},{5,6},{6,5},{9,10},{10,9},{13,14},{14,13},{17,18},{18,... | collective-permute-start | bytes 344072 | tf_op jit(solution)/shard_map/ppermute | solution.py:570
  15.1 0.0 copy-done
  15.1 0.0 copy-done.8
  15.1 1.5 %shard_map.131 = (f32[8,128,128]{2,1,0:T(8,128)S(1)}, bf16[4,2,128,128]{3,2,1,0:T(8,128)(2,1)S(1)}, f32[9,8,128]{2,1,0:T(8,128)S(1)}) custom-call(f32[64,16,128]{2,1,0:T(8,128)S(1)} %get-tuple-element.47.eastward, f32[9,64,128]{2,1,0:T(8,128)S(1)} %get-tuple-element.45.refs_6_.factors, bf16[256,1024]{1,0:T(8,128)(2,1)S(1)} %copy-done, ...), custom_call_target="tpu_custom_call" | custom-call | tf_op jit(solution)/shard_map/pallas_call | solution.py:631
  16.6 0.0 collective-permute-done.4.refs_3_.refs_11_
  16.6 0.0 copy-start.1
  16.6 0.0 copy-start.5
  16.6 0.9 %shard_map.133 = (f32[84,16,128]{2,1,0:T(8,128)S(1)}, f32[8,16,128]{2,1,0:T(8,128)S(1)}) custom-call(f32[50,16,128]{2,1,0:T(8,128)S(1)} %get-tuple-element.51.refs_0_, f32[34,16,128]{2,1,0:T(8,128)S(1)} %get-tuple-element.52.refs_1_, f32[26,16,128]{2,1,0:T(8,128)S(1)} %get-tuple-element.53.refs_2_, ...), custom_call_target="tpu_custom_call" | custom-call | tf_op jit(solution)/shard_map/pallas_call | solution.py:642
  17.5 3.0 %collective-permute-done.5.refs_12_ = f32[14,16,128]{2,1,0:T(8,128)S(1)} collective-permute-done((f32[14,16,128]{2,1,0:T(8,128)S(1)}, f32[14,16,128]{2,1,0:T(8,128)S(1)}, u32[]{:S(2)}, u32[]{:S(2)}) %collective-permute-start.5) | collective-permute-done | bytes 114720 | tf_op jit(solution)/shard_map/ppermute | solution.py:570
  20.5 0.0 copy-done.1
  20.5 0.0 copy-done.5
  20.5 3.0 %shard_map.134 = f32[16,64,128]{2,1,0:T(8,128)} custom-call(f32[8,128,128]{2,1,0:T(8,128)S(1)} %get-tuple-element.48.refs_0_, bf16[4,2,128,128]{3,2,1,0:T(8,128)(2,1)S(1)} %get-tuple-element.49.refs_1_, f32[9,8,128]{2,1,0:T(8,128)S(1)} %get-tuple-element.50.refs_5_.refs_2_, f32[84,16,128]{2,1,0:T(8,128)S(1)} %get-tuple-element.58.refs_3_, ...), custom_call_target="tpu_custom_call" | custom-call | tf_op jit(solution)/shard_map/pallas_call | solution.py:645
  (1 shorter events, 0.0 us)
Async XLA Ops:
  0.0 2.8 %copy-start.3 = (s32[32,64]{1,0:T(8,128)S(1)}, s32[32,64]{1,0:T(8,128)}, u32[]{:S(2)}) copy-start(s32[32,64]{1,0:T(8,128)} %refs_8_.3) | copy-start | bytes 24580
  0.0 2.8 %copy-start.4 = (f32[32,64]{1,0:T(8,128)S(1)}, f32[32,64]{1,0:T(8,128)}, u32[]{:S(2)}) copy-start(f32[32,64]{1,0:T(8,128)} %refs_11_.1) | copy-start | bytes 24580
  0.0 2.8 %copy-start.7 = (f32[16,32]{1,0:T(8,128)S(1)}, f32[16,32]{1,0:T(8,128)}, u32[]{:S(2)}) copy-start(f32[16,32]{1,0:T(8,128)} %refs_12_.1) | copy-start | bytes 6148
  0.0 2.8 %copy-start.9 = (s32[8,16]{1,0:T(8,128)S(1)}, s32[8,16]{1,0:T(8,128)}, u32[]{:S(2)}) copy-start(s32[8,16]{1,0:T(8,128)} %refs_10_.1) | copy-start | bytes 1540
  0.0 2.8 %copy-start.10 = (f32[8,16]{1,0:T(8,128)S(1)}, f32[8,16]{1,0:T(8,128)}, u32[]{:S(2)}) copy-start(f32[8,16]{1,0:T(8,128)} %refs_13_.2) | copy-start | bytes 1540
  1.6 1.3 %copy-start.6 = (s32[16,32]{1,0:T(8,128)S(1)}, s32[16,32]{1,0:T(8,128)}, u32[]{:S(2)}) copy-start(s32[16,32]{1,0:T(8,128)} %refs_9_.3) | copy-start | bytes 6148
  1.6 1.2 %collective-permute-start = (f32[2,16,128]{2,1,0:T(8,128)S(1)}, f32[2,16,128]{2,1,0:T(8,128)S(1)}, u32[]{:S(2)}, u32[]{:S(2)}) collective-permute-start(f32[2,16,128]{2,1,0:T(8,128)S(1)} %get-tuple-element.40), channel_id=1, source_target_pairs={{0,4},{8,12},{16,20},{24,28},{4,0},{12,8},{20,16},{28,24},{1,5},{9... | collective-permute-start | bytes 49160 | tf_op jit(solution)/shard_map/ppermute | solution.py:570
  2.9 3.7 %copy-start.2 = (s32[64,128]{1,0:T(8,128)S(1)}, s32[64,128]{1,0:T(8,128)}, u32[]{:S(2)}) copy-start(s32[64,128]{1,0:T(8,128)} %widths0.3) | copy-start | bytes 98308
  2.9 6.7 %collective-permute-start.1 = (f32[21,16,128]{2,1,0:T(8,128)S(1)}, f32[21,16,128]{2,1,0:T(8,128)S(1)}, u32[]{:S(2)}, u32[]{:S(2)}) collective-permute-start(f32[21,16,128]{2,1,0:T(8,128)S(1)} %get-tuple-element.41), channel_id=1, source_target_pairs={{4,8},{12,16},{20,24},{8,4},{16,12},{24,20},{5,9},{13,17},{21,25},... | collective-permute-start | bytes 516104 | tf_op jit(solution)/shard_map/ppermute | solution.py:570
  5.1 2.6 %collective-permute-start.2 = (f32[19,16,128]{2,1,0:T(8,128)S(1)}, f32[19,16,128]{2,1,0:T(8,128)S(1)}, u32[]{:S(2)}, u32[]{:S(2)}) collective-permute-start(f32[19,16,128]{2,1,0:T(8,128)S(1)} %get-tuple-element.43), channel_id=1, source_target_pairs={{0,4},{8,12},{16,20},{24,28},{4,0},{12,8},{20,16},{28,24},{1,5},{9... | collective-permute-start | bytes 466952 | tf_op jit(solution)/shard_map/ppermute | solution.py:570
  9.7 1.4 %collective-permute-start.3 = (f32[21,16,128]{2,1,0:T(8,128)S(1)}, f32[21,16,128]{2,1,0:T(8,128)S(1)}, u32[]{:S(2)}, u32[]{:S(2)}) collective-permute-start(f32[21,16,128]{2,1,0:T(8,128)S(1)} %collective-permute-done.1.refs_5_), channel_id=1, source_target_pairs={{0,4},{8,12},{16,20},{24,28},{4,0},{12,8},{20,16},{28,24},{1,5},{9... | collective-permute-start | bytes 516104 | tf_op jit(solution)/shard_map/ppermute | solution.py:570
  9.8 5.3 %copy-start = (bf16[256,1024]{1,0:T(8,128)(2,1)S(1)}, bf16[256,1024]{1,0:T(8,128)(2,1)}, u32[]{:S(2)}) copy-start(bf16[256,1024]{1,0:T(8,128)(2,1)} %constant.7.clone.shifts.refs_15_) | copy-start | bytes 1572868
  11.1 4.1 %copy-start.8 = (f32[4,16,16]{2,1,0:T(8,128)S(1)}, f32[4,16,16]{2,1,0:T(8,128)}, u32[]{:S(2)}) copy-start(f32[4,16,16]{2,1,0:T(8,128)} %vertical.1) | copy-start | bytes 12292
  11.2 5.4 %collective-permute-start.4 = (f32[14,16,128]{2,1,0:T(8,128)S(1)}, f32[14,16,128]{2,1,0:T(8,128)S(1)}, u32[]{:S(2)}, u32[]{:S(2)}) collective-permute-start(f32[14,16,128]{2,1,0:T(8,128)S(1)} %get-tuple-element.57), channel_id=1, source_target_pairs={{0,1},{2,3},{1,0},{3,2},{4,5},{6,7},{5,4},{7,6},{8,9},{10,11},{9,8... | collective-permute-start | bytes 344072 | tf_op jit(solution)/shard_map/ppermute | solution.py:570
  12.7 7.7 %collective-permute-start.5 = (f32[14,16,128]{2,1,0:T(8,128)S(1)}, f32[14,16,128]{2,1,0:T(8,128)S(1)}, u32[]{:S(2)}, u32[]{:S(2)}) collective-permute-start(f32[14,16,128]{2,1,0:T(8,128)S(1)} %get-tuple-element.66), channel_id=1, source_target_pairs={{1,2},{2,1},{5,6},{6,5},{9,10},{10,9},{13,14},{14,13},{17,18},{18,... | collective-permute-start | bytes 344072 | tf_op jit(solution)/shard_map/ppermute | solution.py:570
  16.6 3.8 %copy-start.1 = (bf16[4,128,128]{2,1,0:T(8,128)(2,1)S(1)}, bf16[4,128,128]{2,1,0:T(8,128)(2,1)}, u32[]{:S(2)}) copy-start(bf16[4,128,128]{2,1,0:T(8,128)(2,1)} %constant.8.clone.refs_14_) | copy-start | bytes 393220
  16.6 3.8 %copy-start.5 = (f32[64,128]{1,0:T(8,128)S(1)}, f32[64,128]{1,0:T(8,128)}, u32[]{:S(2)}) copy-start(f32[64,128]{1,0:T(8,128)} %refs_13_.3) | copy-start | bytes 98308

commit v8 on v7

--- a/solution.py
+++ b/solution.py
@@ -543,8 +543,9 @@
         spread_flat[pl.ds(0, (r + 2) * Z), :] = dot_exact(flat[pl.ds(0, (r + 2) * Z), :], table[l])
     for t in range(R // H):
         edge[t] = near_edge[t] + side_edge(geo, got_y, jnp.logical_not(north_even), edge_taps, t)
-    edge_flat = edge.reshape(R // H * Z, LANES)
-    edge_flat[...] = mix([matrices[0, 0], matrices[0, 1]], edge_flat[...])
+    edge_flat = edge.reshape(edge.shape[0] * Z, LANES)
+    used = pl.ds(0, R // H * Z)
+    edge_flat[used, :] = mix([matrices[0, 0], matrices[0, 1]], edge_flat[used, :])
     widen = table[LEVELS][:, 0 : 6 * Z]
     at_edge = (lane8 < H) | (lane8 >= M - H)
     copies = []
@@ -651,7 +652,7 @@
             for dims in (
                 (ext_rows, Z, M), (out_rows, Z, M), (out_rows, Z, M),
                 (rows1, Z, M), (rows1, Z, M), (width_rows, M), (width_rows, M), (H + 1, width_rows, M),
-                (R // H, Z, M), (Z, R, M),
+                (R // H + 1, Z, M), (Z, R, M),
             )
         ] + [pltpu.SemaphoreType.DMA((R // 16,))],
         compiler_params=params,

time: 23.7 us -> 23.7 us (level)
  no operation moved by 1% of the time
where the time goes in v8:
time: 23.7 us; the launch traced here: 23.5 us
  Pallas kernels  8.56 us (36%)
  starting transfers between devices  7.83 us (33%)
  waiting for transfers between devices  6.83 us (29%)
    ppermute x6, starting transfers between devices, swap(): return lax.ppermute(x, axis, route + [(j, i) for i, j in route])  7.83 us
    ppermute x6, waiting for transfers between devices, swap(): return lax.ppermute(x, axis, route + [(j, i) for i, j in route])  6.83 us
    pallas_call x1, Pallas kernels, body(): pl.pallas_call(functools.partial(finish, geo), out_shape=shape(Z, R, M),...  2.99 us
    pallas_call x1, Pallas kernels, body(): pl.pallas_call(functools.partial(prepare, geo), out_shape=[shape(R, Z, M)...  1.53 us
    pallas_call x1, Pallas kernels, body(): pl.pallas_call(functools.partial(own_north, geo), out_shape=[shape(R // 8...  1.46 us
    pallas_call x1, Pallas kernels, body(): pl.pallas_call(functools.partial(middle, geo), out_shape=[shape(R, Z, M)]...  1.05 us
    pallas_call x1, Pallas kernels, body(): pl.pallas_call(functools.partial(near_side, geo), out_shape=[shape(ext_ro...  0.85 us
    pallas_call x1, Pallas kernels, body(): pl.pallas_call(functools.partial(interior, geo), out_shape=[shape(H + 1,...  0.53 us
  transfers between devices with their start and end apart: 6, of which 5 were waited for; matrix products, arithmetic and copies ran while one was open for 0% of the time, Pallas kernels for 17%

profile of v8, /device:TPU:20, one launch (start us, length us, event | category | flops | bytes accessed | tf_op | source)
XLA Modules:
  0.0 23.5 jit_solution(15173307093722656919)
XLA Ops:
  0.0 0.0 copy-start.3
  0.0 0.0 copy-start.4
  0.0 0.0 copy-start.7
  0.0 0.0 copy-start.9
  0.0 0.0 copy-start.10
  0.0 1.5 %shard_map.127 = (f32[64,16,128]{2,1,0:T(8,128)S(1)}, f32[34,16,128]{2,1,0:T(8,128)S(1)}, f32[18,16,128]{2,1,0:T(8,128)S(1)}, f32[10,16,128]{2,1,0:T(8,128)S(1)}, f32[2,16,128]{2,1,0:T(8,128)S(1)}) custom-call(f32[16,64,128]{2,1,0:T(8,128)} %refs_0_.1, bf16[4,128,128]{2,1,0:T(8,128)(2,1)} %constant.6.clone.refs_1_), custom_call_target="tpu_custom_call" | custom-call | tf_op jit(solution)/shard_map/pallas_call | solution.py:588
  1.6 0.0 copy-start.6
  1.6 0.1 collective-permute-start
  1.7 1.2 %collective-permute-done.refs_3_ = f32[2,16,128]{2,1,0:T(8,128)S(1)} collective-permute-done((f32[2,16,128]{2,1,0:T(8,128)S(1)}, f32[2,16,128]{2,1,0:T(8,128)S(1)}, u32[]{:S(2)}, u32[]{:S(2)}) %collective-permute-start) | collective-permute-done | bytes 16416 | tf_op jit(solution)/shard_map/ppermute | solution.py:571
  2.8 0.0 copy-done.3
  2.8 0.0 copy-done.4
  2.8 0.0 copy-done.7
  2.8 0.0 copy-done.9
  2.8 0.0 copy-done.10
  2.9 0.0 copy-done.6
  2.9 0.0 copy-start.2
  2.9 2.1 %collective-permute-start.1 = (f32[21,16,128]{2,1,0:T(8,128)S(1)}, f32[21,16,128]{2,1,0:T(8,128)S(1)}, u32[]{:S(2)}, u32[]{:S(2)}) collective-permute-start(f32[21,16,128]{2,1,0:T(8,128)S(1)} %get-tuple-element.41), channel_id=1, source_target_pairs={{4,8},{12,16},{20,24},{8,4},{16,12},{24,20},{5,9},{13,17},{21,25},... | collective-permute-start | bytes 516104 | tf_op jit(solution)/shard_map/ppermute | solution.py:571
  5.1 1.5 %collective-permute-start.2 = (f32[19,16,128]{2,1,0:T(8,128)S(1)}, f32[19,16,128]{2,1,0:T(8,128)S(1)}, u32[]{:S(2)}, u32[]{:S(2)}) collective-permute-start(f32[19,16,128]{2,1,0:T(8,128)S(1)} %get-tuple-element.43), channel_id=1, source_target_pairs={{0,4},{8,12},{16,20},{24,28},{4,0},{12,8},{20,16},{28,24},{1,5},{9... | collective-permute-start | bytes 466952 | tf_op jit(solution)/shard_map/ppermute | solution.py:571
  6.6 0.0 copy-done.2
  6.6 0.5 %shard_map.129 = (f32[9,64,128]{2,1,0:T(8,128)S(1)}, f32[48,16,128]{2,1,0:T(8,128)S(1)}) custom-call(f32[64,16,128]{2,1,0:T(8,128)S(1)} %get-tuple-element.36.field.refs_0_, s32[64,128]{1,0:T(8,128)S(1)} %copy-done.2), custom_call_target="tpu_custom_call" | custom-call | tf_op jit(solution)/shard_map/pallas_call | solution.py:606
  7.2 0.5 %collective-permute-done.2.refs_4_ = f32[19,16,128]{2,1,0:T(8,128)S(1)} collective-permute-done((f32[19,16,128]{2,1,0:T(8,128)S(1)}, f32[19,16,128]{2,1,0:T(8,128)S(1)}, u32[]{:S(2)}, u32[]{:S(2)}) %collective-permute-start.2) | collective-permute-done | bytes 155680 | tf_op jit(solution)/shard_map/ppermute | solution.py:571
  7.6 2.0 %collective-permute-done.1.refs_5_ = f32[21,16,128]{2,1,0:T(8,128)S(1)} collective-permute-done((f32[21,16,128]{2,1,0:T(8,128)S(1)}, f32[21,16,128]{2,1,0:T(8,128)S(1)}, u32[]{:S(2)}, u32[]{:S(2)}) %collective-permute-start.1) | collective-permute-done | bytes 172064 | tf_op jit(solution)/shard_map/ppermute | solution.py:571
  9.7 0.2 collective-permute-start.3
  9.8 0.0 copy-start
  9.8 1.0 %shard_map.130 = (f32[64,16,128]{2,1,0:T(8,128)S(1)}, f32[50,16,128]{2,1,0:T(8,128)S(1)}, f32[34,16,128]{2,1,0:T(8,128)S(1)}, f32[26,16,128]{2,1,0:T(8,128)S(1)}...) custom-call(f32[64,16,128]{2,1,0:T(8,128)S(1)} %get-tuple-element.36, ...), custom_call_target="tpu_custom_call" | custom-call | tf_op jit(solution)/shard_map/pallas_call | solution.py:615
  10.9 0.2 collective-permute-done.3.got_d.refs_4_
  11.1 0.0 copy-start.8
  11.1 0.1 shard_map.132
  11.2 1.6 %collective-permute-start.4 = (f32[14,16,128]{2,1,0:T(8,128)S(1)}, f32[14,16,128]{2,1,0:T(8,128)S(1)}, u32[]{:S(2)}, u32[]{:S(2)}) collective-permute-start(f32[14,16,128]{2,1,0:T(8,128)S(1)} %get-tuple-element.57), channel_id=1, source_target_pairs={{0,1},{2,3},{1,0},{3,2},{4,5},{6,7},{5,4},{7,6},{8,9},{10,11},{9,8... | collective-permute-start | bytes 344072 | tf_op jit(solution)/shard_map/ppermute | solution.py:571
  12.7 2.4 %collective-permute-start.5 = (f32[14,16,128]{2,1,0:T(8,128)S(1)}, f32[14,16,128]{2,1,0:T(8,128)S(1)}, u32[]{:S(2)}, u32[]{:S(2)}) collective-permute-start(f32[14,16,128]{2,1,0:T(8,128)S(1)} %get-tuple-element.66), channel_id=1, source_target_pairs={{1,2},{2,1},{5,6},{6,5},{9,10},{10,9},{13,14},{14,13},{17,18},{18,... | collective-permute-start | bytes 344072 | tf_op jit(solution)/shard_map/ppermute | solution.py:571
  15.1 0.0 copy-done
  15.1 0.0 copy-done.8
  15.1 1.5 %shard_map.131 = (f32[8,128,128]{2,1,0:T(8,128)S(1)}, bf16[4,2,128,128]{3,2,1,0:T(8,128)(2,1)S(1)}, f32[9,8,128]{2,1,0:T(8,128)S(1)}) custom-call(f32[64,16,128]{2,1,0:T(8,128)S(1)} %get-tuple-element.47.eastward, f32[9,64,128]{2,1,0:T(8,128)S(1)} %get-tuple-element.45.refs_6_.factors, bf16[256,1024]{1,0:T(8,128)(2,1)S(1)} %copy-done, ...), custom_call_target="tpu_custom_call" | custom-call | tf_op jit(solution)/shard_map/pallas_call | solution.py:632
  16.6 0.0 collective-permute-done.4.refs_3_.refs_11_
  16.6 0.0 copy-start.1
  16.6 0.0 copy-start.5
  16.6 0.9 %shard_map.133 = (f32[84,16,128]{2,1,0:T(8,128)S(1)}, f32[8,16,128]{2,1,0:T(8,128)S(1)}) custom-call(f32[50,16,128]{2,1,0:T(8,128)S(1)} %get-tuple-element.51.refs_0_, f32[34,16,128]{2,1,0:T(8,128)S(1)} %get-tuple-element.52.refs_1_, f32[26,16,128]{2,1,0:T(8,128)S(1)} %get-tuple-element.53.refs_2_, ...), custom_call_target="tpu_custom_call" | custom-call | tf_op jit(solution)/shard_map/pallas_call | solution.py:643
  17.5 3.0 %collective-permute-done.5.refs_12_ = f32[14,16,128]{2,1,0:T(8,128)S(1)} collective-permute-done((f32[14,16,128]{2,1,0:T(8,128)S(1)}, f32[14,16,128]{2,1,0:T(8,128)S(1)}, u32[]{:S(2)}, u32[]{:S(2)}) %collective-permute-start.5) | collective-permute-done | bytes 114720 | tf_op jit(solution)/shard_map/ppermute | solution.py:571
  20.5 0.0 copy-done.1
  20.5 0.0 copy-done.5
  20.5 3.0 %shard_map.134 = f32[16,64,128]{2,1,0:T(8,128)} custom-call(f32[8,128,128]{2,1,0:T(8,128)S(1)} %get-tuple-element.48.refs_0_, bf16[4,2,128,128]{3,2,1,0:T(8,128)(2,1)S(1)} %get-tuple-element.49.refs_1_, f32[9,8,128]{2,1,0:T(8,128)S(1)} %get-tuple-element.50.refs_5_.refs_2_, f32[84,16,128]{2,1,0:T(8,128)S(1)} %get-tuple-element.58.refs_3_, ...), custom_call_target="tpu_custom_call" | custom-call | tf_op jit(solution)/shard_map/pallas_call | solution.py:646
  (1 shorter events, 0.0 us)
Async XLA Ops:
  0.0 2.8 %copy-start.3 = (s32[32,64]{1,0:T(8,128)S(1)}, s32[32,64]{1,0:T(8,128)}, u32[]{:S(2)}) copy-start(s32[32,64]{1,0:T(8,128)} %refs_8_.3) | copy-start | bytes 24580
  0.0 2.8 %copy-start.4 = (f32[32,64]{1,0:T(8,128)S(1)}, f32[32,64]{1,0:T(8,128)}, u32[]{:S(2)}) copy-start(f32[32,64]{1,0:T(8,128)} %refs_11_.1) | copy-start | bytes 24580
  0.0 2.8 %copy-start.7 = (f32[16,32]{1,0:T(8,128)S(1)}, f32[16,32]{1,0:T(8,128)}, u32[]{:S(2)}) copy-start(f32[16,32]{1,0:T(8,128)} %refs_12_.1) | copy-start | bytes 6148
  0.0 2.8 %copy-start.9 = (s32[8,16]{1,0:T(8,128)S(1)}, s32[8,16]{1,0:T(8,128)}, u32[]{:S(2)}) copy-start(s32[8,16]{1,0:T(8,128)} %refs_10_.1) | copy-start | bytes 1540
  0.0 2.8 %copy-start.10 = (f32[8,16]{1,0:T(8,128)S(1)}, f32[8,16]{1,0:T(8,128)}, u32[]{:S(2)}) copy-start(f32[8,16]{1,0:T(8,128)} %refs_13_.2) | copy-start | bytes 1540
  1.6 1.3 %copy-start.6 = (s32[16,32]{1,0:T(8,128)S(1)}, s32[16,32]{1,0:T(8,128)}, u32[]{:S(2)}) copy-start(s32[16,32]{1,0:T(8,128)} %refs_9_.3) | copy-start | bytes 6148
  1.6 1.2 %collective-permute-start = (f32[2,16,128]{2,1,0:T(8,128)S(1)}, f32[2,16,128]{2,1,0:T(8,128)S(1)}, u32[]{:S(2)}, u32[]{:S(2)}) collective-permute-start(f32[2,16,128]{2,1,0:T(8,128)S(1)} %get-tuple-element.40), channel_id=1, source_target_pairs={{0,4},{8,12},{16,20},{24,28},{4,0},{12,8},{20,16},{28,24},{1,5},{9... | collective-permute-start | bytes 49160 | tf_op jit(solution)/shard_map/ppermute | solution.py:571
  2.9 3.7 %copy-start.2 = (s32[64,128]{1,0:T(8,128)S(1)}, s32[64,128]{1,0:T(8,128)}, u32[]{:S(2)}) copy-start(s32[64,128]{1,0:T(8,128)} %widths0.3) | copy-start | bytes 98308
  2.9 6.7 %collective-permute-start.1 = (f32[21,16,128]{2,1,0:T(8,128)S(1)}, f32[21,16,128]{2,1,0:T(8,128)S(1)}, u32[]{:S(2)}, u32[]{:S(2)}) collective-permute-start(f32[21,16,128]{2,1,0:T(8,128)S(1)} %get-tuple-element.41), channel_id=1, source_target_pairs={{4,8},{12,16},{20,24},{8,4},{16,12},{24,20},{5,9},{13,17},{21,25},... | collective-permute-start | bytes 516104 | tf_op jit(solution)/shard_map/ppermute | solution.py:571
  5.1 2.6 %collective-permute-start.2 = (f32[19,16,128]{2,1,0:T(8,128)S(1)}, f32[19,16,128]{2,1,0:T(8,128)S(1)}, u32[]{:S(2)}, u32[]{:S(2)}) collective-permute-start(f32[19,16,128]{2,1,0:T(8,128)S(1)} %get-tuple-element.43), channel_id=1, source_target_pairs={{0,4},{8,12},{16,20},{24,28},{4,0},{12,8},{20,16},{28,24},{1,5},{9... | collective-permute-start | bytes 466952 | tf_op jit(solution)/shard_map/ppermute | solution.py:571
  9.7 1.4 %collective-permute-start.3 = (f32[21,16,128]{2,1,0:T(8,128)S(1)}, f32[21,16,128]{2,1,0:T(8,128)S(1)}, u32[]{:S(2)}, u32[]{:S(2)}) collective-permute-start(f32[21,16,128]{2,1,0:T(8,128)S(1)} %collective-permute-done.1.refs_5_), channel_id=1, source_target_pairs={{0,4},{8,12},{16,20},{24,28},{4,0},{12,8},{20,16},{28,24},{1,5},{9... | collective-permute-start | bytes 516104 | tf_op jit(solution)/shard_map/ppermute | solution.py:571
  9.8 5.3 %copy-start = (bf16[256,1024]{1,0:T(8,128)(2,1)S(1)}, bf16[256,1024]{1,0:T(8,128)(2,1)}, u32[]{:S(2)}) copy-start(bf16[256,1024]{1,0:T(8,128)(2,1)} %constant.7.clone.shifts.refs_15_) | copy-start | bytes 1572868
  11.1 4.1 %copy-start.8 = (f32[4,16,16]{2,1,0:T(8,128)S(1)}, f32[4,16,16]{2,1,0:T(8,128)}, u32[]{:S(2)}) copy-start(f32[4,16,16]{2,1,0:T(8,128)} %vertical.1) | copy-start | bytes 12292
  11.2 5.4 %collective-permute-start.4 = (f32[14,16,128]{2,1,0:T(8,128)S(1)}, f32[14,16,128]{2,1,0:T(8,128)S(1)}, u32[]{:S(2)}, u32[]{:S(2)}) collective-permute-start(f32[14,16,128]{2,1,0:T(8,128)S(1)} %get-tuple-element.57), channel_id=1, source_target_pairs={{0,1},{2,3},{1,0},{3,2},{4,5},{6,7},{5,4},{7,6},{8,9},{10,11},{9,8... | collective-permute-start | bytes 344072 | tf_op jit(solution)/shard_map/ppermute | solution.py:571
  12.7 7.7 %collective-permute-start.5 = (f32[14,16,128]{2,1,0:T(8,128)S(1)}, f32[14,16,128]{2,1,0:T(8,128)S(1)}, u32[]{:S(2)}, u32[]{:S(2)}) collective-permute-start(f32[14,16,128]{2,1,0:T(8,128)S(1)} %get-tuple-element.66), channel_id=1, source_target_pairs={{1,2},{2,1},{5,6},{6,5},{9,10},{10,9},{13,14},{14,13},{17,18},{18,... | collective-permute-start | bytes 344072 | tf_op jit(solution)/shard_map/ppermute | solution.py:571
  16.6 3.8 %copy-start.1 = (bf16[4,128,128]{2,1,0:T(8,128)(2,1)S(1)}, bf16[4,128,128]{2,1,0:T(8,128)(2,1)}, u32[]{:S(2)}) copy-start(bf16[4,128,128]{2,1,0:T(8,128)(2,1)} %constant.8.clone.refs_14_) | copy-start | bytes 393220
  16.6 3.8 %copy-start.5 = (f32[64,128]{1,0:T(8,128)S(1)}, f32[64,128]{1,0:T(8,128)}, u32[]{:S(2)}) copy-start(f32[64,128]{1,0:T(8,128)} %refs_13_.3) | copy-start | bytes 98308
